TPU v7x, 512 devices: a whole 4x4x16 slice. The times are simulated.
512 devices in a mesh: rows: 32 (over y, x, core), cov: 16 (over z).
Axes of the slice: x: 4, y: 4, z: 16, core: 2. Of those that a mesh axis runs over, the one named last changes fastest.
Arguments:
- design: bfloat16 [256, 16384, 128], P('cov', 'rows'), may hold values from -6 to 6
- outcome: int32 [16384, 128], P('rows'), may hold values from 0 to 1
- block_fill: int32 [16384], P('rows'), may hold values from 1 to 128
- block_group: int32 [16384], P('rows'), may hold values from 0 to 8191, as said below
- fixed_coef: float32 [256], P('cov'), may hold values from -0.375 to 0.375
- slopes: float32 [256, 8192], P('cov', 'rows'), may hold values from -0.375 to 0.375
- precision: float32 [256, 256], P('cov'), as said below
Outputs:
- fixed_grad: float32 [256], P('cov')
- slope_grad: float32 [256, 8192], P('cov', 'rows')
Inputs may be any that keep to these rules, and one draw needn't show every extreme that they name: block_group names every group and rises along the blocks of each index of rows; group g is owned by index g // 256 of rows; the blocks of rows index d belong to groups owned by d - 1, d or d + 1; every index but the first holds blocks of groups owned by the index below, and every index but the last blocks of groups owned by the index above. `precision`: symmetric.
All inputs are finite; a program needn't handle non-finite values.
Results may differ from a plain program's by a relative error of at most 0.0003.
Values sent between devices are 32-bit elements; how exact they have to be, the bound alone decides.
No kernel may reach another device: no remote copies, remote signals or barrier semaphores. Data moves between devices by JAX's collectives and lax.ppermute only.
A program may use at most 64 MiB of HBM per device.

v0:
```python
import jax
import jax.numpy as jnp
from jax import lax
from jax.sharding import PartitionSpec as P


def from_behind(shard, axis, by):
    peers = lax.axis_size(axis)
    pairs = [(i, i + by) for i in range(peers) if 0 <= i + by < peers]
    return lax.ppermute(shard, axis, pairs)


def body(design, outcome, block_fill, block_group, fixed_coef, slopes, precision):
    group_count = slopes.shape[1]
    from_lower = from_behind(slopes, "rows", 1)
    from_upper = from_behind(slopes, "rows", -1)
    window = jnp.concatenate([from_lower, slopes, from_upper], axis=1)
    offset = (lax.axis_index("rows") - 1) * group_count
    group_index = block_group - offset
    combined = fixed_coef[:, None] + jnp.take(window, group_index, axis=1)
    partial_value = jnp.einsum(
        "pnb,pn->nb",
        design,
        combined,
        precision=lax.Precision.HIGHEST,
        preferred_element_type=jnp.float32,
    )
    logits = lax.psum(partial_value, "cov")
    valid_rows = lax.broadcasted_iota(jnp.int32, logits.shape, 1) < block_fill[:, None]
    residual = jnp.where(
        valid_rows, outcome.astype(jnp.float32) - jax.nn.sigmoid(logits), jnp.float32(0.0)
    )
    block_grads = jnp.einsum(
        "pnb,nb->pn",
        design,
        residual,
        precision=lax.Precision.HIGHEST,
        preferred_element_type=jnp.float32,
    )
    fixed_grad = lax.psum(jnp.sum(block_grads, axis=1), "rows") - fixed_coef
    full_slopes = lax.all_gather(slopes, "cov", axis=0, tiled=True)
    prior_term = jnp.dot(precision, full_slopes, precision=lax.Precision.HIGHEST)
    group_terms = jax.ops.segment_sum(block_grads.T, group_index, num_segments=3 * group_count).T
    given_down = from_behind(group_terms[:, :group_count], "rows", -1)
    given_up = from_behind(group_terms[:, 2 * group_count :], "rows", 1)
    data_part = group_terms[:, group_count : 2 * group_count] + given_down + given_up
    return (fixed_grad, data_part - prior_term)


def solution(mesh):
    return jax.shard_map(
        body,
        mesh=mesh,
        in_specs=(
            P("cov", "rows", None),
            P("rows", None),
            P("rows"),
            P("rows"),
            P("cov"),
            P("cov", "rows"),
            P("cov", None),
        ),
        out_specs=(P("cov"), P("cov", "rows")),
        check_vma=False,
    )
```

profile of v0, /device:TPU:1, one launch (start us, length us, event | category | flops | bytes accessed | tf_op | source)
XLA Modules:
  0.0 277.7 jit_solution(4675480714626069651)
XLA Ops:
  7.2 0.0 copy-start
  7.2 0.0 all-reduce.2.cloned.1.call-start
  7.2 8.9 %collective-permute-start.1 = (f32[16,256]{1,0:T(8,128)}, f32[16,256]{1,0:T(8,128)S(1)}, u32[]{:S(2)}, u32[]{:S(2)}) collective-permute-start(f32[16,256]{1,0:T(8,128)} %param.12), channel_id=1, source_target_pairs={{16,0},{32,16},{48,32},{64,48},{80,64},{96,80},{112,96},{128,112},... | collective-permute-start | bytes 49160 | tf_op jit(solution)/shard_map/ppermute | solution.py:10
  16.2 1.9 collective-permute-start
  18.1 0.7 compare_and_fusion
  18.8 0.0 collective-permute-done.1
  18.8 0.6 collective-permute-done
  19.4 0.7 pad_maximum_fusion
  20.2 0.2 copy.16
  20.3 0.0 copy-start.1
  20.3 0.0 copy-start.4
  20.4 1.0 gather_fusion
  21.4 0.8 select_add_fusion
  22.2 0.0 copy-done
  22.2 3.6 %fusion.2 = f32[512,1,128]{2,1,0:T(1,128)} fusion(f32[16,512,1]{0,2,1:T(1,128)S(1)} %bitcast.21, bf16[16,512,128]{2,1,0:T(8,128)(2,1)S(1)} %copy-done), kind=kOutput, calls=%fused_computation.4 | convolution fusion | flops 12582912 | bytes 2392064 | tf_op jit(solution)/shard_map/pnb,pn->nb/dot_general | solution.py:21
  25.8 0.0 all-reduce.2.cloned.1.call-update
  25.8 128.7 %all-reduce.2.cloned.1.call-done = f32[512,128]{1,0:T(8,128)} async-done(((f32[512,128]{1,0:T(8,128)}), f32[512,128]{1,0:T(8,128)}) %all-reduce.2.cloned.1.call-update) | async-done | bytes 262160 | tf_op jit(solution)/shard_map/psum | solution.py:28
  154.5 0.0 copy-done.1
  154.5 0.0 copy-done.4
  154.5 1.1 subtract_select_fusion
  155.6 0.0 copy-start.2
  155.6 0.0 copy-start.5
  155.6 0.0 copy-start.3
  155.6 3.9 %fusion = f32[512,1,16]{2,1,0:T(1,128)S(1)} fusion(f32[512,128,1]{1,2,0:T(1,128)S(1)} %bitcast.17, bf16[16,512,128]{2,1,0:T(8,128)(2,1)S(1)} %copy-done), kind=kOutput, calls=%fused_computation.2 | convolution fusion | flops 12582912 | bytes 2392064 | tf_op jit(solution)/shard_map/pnb,nb->pn/dot_general | solution.py:33
  159.5 0.1 reduce_sum.9
  159.6 2.9 %scatter_custom_fusion = f32[768,16]{1,0:T(8,128)S(1)} fusion(s32[512]{0:T(512)S(1)} %get-tuple-element.3, f32[512,16]{1,0:T(8,128)S(1)} %bitcast.20, f32[]{:T(128)} %constant.31.clone.1), kind=kCustom, calls=%fused_computation.9 | custom fusion | flops 8192 | bytes 49156 | tf_op jit(solution)/shard_map/scatter-add | solution.py:43
  162.5 0.1 copy.17
  162.6 12.6 %collective-permute-start.3 = (f32[16,256]{1,0:T(8,128)S(1)}, f32[16,256]{1,0:T(8,128)S(1)}, u32[]{:S(2)}, u32[]{:S(2)}) collective-permute-start(f32[16,256]{1,0:T(8,128)S(1)} %get-tuple-element.5), channel_id=1, source_target_pairs={{0,16},{16,32},{32,48},{48,64},{64,80},{80,96},{96,112},{112,128},... | collective-permute-start | bytes 49160 | tf_op jit(solution)/shard_map/ppermute | solution.py:10
  175.2 1.9 collective-permute-start.2
  177.1 0.0 copy-done.2
  177.1 22.5 %all_gather.3 = f32[256,256]{1,0:T(8,128)S(1)} all-gather(f32[16,256]{1,0:T(8,128)S(1)} %copy-done.2), channel_id=1, replica_groups=mesh['rows'=32,'cov'=16] {'cov'}, dimensions={0}, use_global_device_ids=true | all-gather | bytes 278528 | tf_op jit(solution)/shard_map/all_gather | solution.py:41
  199.6 69.9 %psum.15 = f32[16]{0:T(128)S(1)} all-reduce(f32[16]{0:T(128)S(1)} %reduce_sum.9), channel_id=1, replica_groups=mesh['rows'=32,'cov'=16] {'rows'}, use_global_device_ids=true, to_apply=%region_2.3 | all-reduce | flops 16 | bytes 128 | tf_op jit(solution)/shard_map/psum | solution.py:40
  269.5 0.0 copy-done.5
  269.5 0.5 sub.22
  270.0 0.0 collective-permute-done.3
  270.0 0.0 collective-permute-done.2
  270.0 0.0 copy-done.3
  270.0 0.8 fusion.7
  (3 shorter events, 0.0 us)
Async XLA Ops:
  7.2 15.0 %copy-start = (bf16[16,512,128]{2,1,0:T(8,128)(2,1)S(1)}, bf16[16,512,128]{2,1,0:T(8,128)(2,1)}, u32[]{:S(2)}) copy-start(bf16[16,512,128]{2,1,0:T(8,128)(2,1)} %param.7) | copy-start | bytes 6291460
  7.2 147.3 %all-reduce.2.cloned.1.call-start = ((), (), s32[]{:S(2)}) async-start(), calls=%async_computation | async-start | bytes 524288 | tf_op jit(solution)/shard_map/psum | solution.py:28
  7.2 11.6 %collective-permute-start.1 = (f32[16,256]{1,0:T(8,128)}, f32[16,256]{1,0:T(8,128)S(1)}, u32[]{:S(2)}, u32[]{:S(2)}) collective-permute-start(f32[16,256]{1,0:T(8,128)} %param.12), channel_id=1, source_target_pairs={{16,0},{32,16},{48,32},{64,48},{80,64},{96,80},{112,96},{128,112},... | collective-permute-start | bytes 49160 | tf_op jit(solution)/shard_map/ppermute | solution.py:10
  16.2 3.3 %collective-permute-start = (f32[16,256]{1,0:T(8,128)}, f32[16,256]{1,0:T(8,128)S(1)}, u32[]{:S(2)}, u32[]{:S(2)}) collective-permute-start(f32[16,256]{1,0:T(8,128)} %param.12), channel_id=1, source_target_pairs={{0,16},{16,32},{32,48},{48,64},{64,80},{80,96},{96,112},{112,128},... | collective-permute-start | bytes 49160 | tf_op jit(solution)/shard_map/ppermute | solution.py:10
  20.3 134.1 %copy-start.1 = (s32[512,128]{1,0:T(8,128)S(1)}, s32[512,128]{1,0:T(8,128)}, u32[]{:S(2)}) copy-start(s32[512,128]{1,0:T(8,128)} %param.8) | copy-start | bytes 786436
  20.3 134.1 %copy-start.4 = (s32[512]{0:T(512)S(1)}, s32[512]{0:T(512)}, u32[]{:S(2)}) copy-start(s32[512]{0:T(512)} %param.9) | copy-start | bytes 6148
  155.6 21.6 %copy-start.2 = (f32[16,256]{1,0:T(8,128)S(1)}, f32[16,256]{1,0:T(8,128)}, u32[]{:S(2)}) copy-start(f32[16,256]{1,0:T(8,128)} %param.12) | copy-start | bytes 49156
  155.6 113.9 %copy-start.5 = (f32[16]{0:T(128)S(1)}, f32[16]{0:T(128)}, u32[]{:S(2)}) copy-start(f32[16]{0:T(128)} %param.11) | copy-start | bytes 196
  155.6 114.4 %copy-start.3 = (f32[16,256]{1,0:T(8,128)S(1)}, f32[16,256]{1,0:T(8,128)}, u32[]{:S(2)}) copy-start(f32[16,256]{1,0:T(8,128)} %param.13) | copy-start | bytes 49156
  162.6 107.4 %collective-permute-start.3 = (f32[16,256]{1,0:T(8,128)S(1)}, f32[16,256]{1,0:T(8,128)S(1)}, u32[]{:S(2)}, u32[]{:S(2)}) collective-permute-start(f32[16,256]{1,0:T(8,128)S(1)} %get-tuple-element.5), channel_id=1, source_target_pairs={{0,16},{16,32},{32,48},{48,64},{64,80},{80,96},{96,112},{112,128},... | collective-permute-start | bytes 49160 | tf_op jit(solution)/shard_map/ppermute | solution.py:10
  175.2 94.8 %collective-permute-start.2 = (f32[16,256]{1,0:T(8,128)S(1)}, f32[16,256]{1,0:T(8,128)S(1)}, u32[]{:S(2)}, u32[]{:S(2)}) collective-permute-start(f32[16,256]{1,0:T(8,128)S(1)} %get-tuple-element.4), channel_id=1, source_target_pairs={{16,0},{32,16},{48,32},{64,48},{80,64},{96,80},{112,96},{128,112},... | collective-permute-start | bytes 49160 | tf_op jit(solution)/shard_map/ppermute | solution.py:10
Sparse Core Ops, SparseCore 0:
  25.9 128.5 all-reduce.1
where the time goes:
time: 278 us
  waiting for transfers between devices  129 us (46%)
  blocking collectives  92.4 us (33%)
  starting transfers between devices  25.4 us (9%)
  between operations  14.2 us (5%)
  matrix products  8.29 us (3%)
  other arithmetic  6.79 us (2%)
    psum x1, waiting for transfers between devices, body(): logits = lax.psum(partial_value, 'cov')  129 us
    psum x1, blocking collectives, body(): fixed_grad = lax.psum(jnp.sum(block_grads, axis=1), 'rows') - fixed_coef  69.9 us
    ppermute x4, starting transfers between devices, from_behind(): return lax.ppermute(shard, axis, pairs)  25.3 us
    all_gather x1, blocking collectives, body(): full_slopes = lax.all_gather(slopes, 'cov', axis=0, tiled=True)  22.5 us
  transfers between devices with their start and end apart: 5, of which 2 were waited for; matrix products, arithmetic and copies ran while one was open for 0% of the time, Pallas kernels for 0%

commit v1 on v0

v1 whole, which is shorter than its diff:
```python
import jax
import jax.numpy as jnp
from jax import lax
from jax.experimental import pallas as pl
from jax.experimental.pallas import tpu as pltpu
from jax.sharding import PartitionSpec as P

f32 = jnp.float32
bf16 = jnp.bfloat16
VMEM = pl.BlockSpec(memory_space=pltpu.VMEM)
SMEM = pl.BlockSpec(memory_space=pltpu.SMEM)
LANES = 128
ROOM = pltpu.CompilerParams(vmem_limit_bytes=16 << 20)


def from_behind(shard, axis, by):
    peers = lax.axis_size(axis)
    pairs = [(i, i + by) for i in range(peers) if 0 <= i + by < peers]
    return lax.ppermute(shard, axis, pairs)


def exchange(parts, axis):
    return lax.all_to_all(parts, axis, 0, 0, tiled=True)


def three_parts(x):
    a = x.astype(bf16)
    rest = x - a.astype(f32)
    b = rest.astype(bf16)
    c = (rest - b.astype(f32)).astype(bf16)
    return jnp.concatenate([a, b, c], axis=0)


def select_kernel(where_ref, group_ref, fill_ref, outcome_ref, hot_ref, label_ref, valid_ref, scratch_ref):
    window, blocks = hot_ref.shape
    rows = label_ref.shape[0]
    offset = where_ref[0]
    index = group_ref[...] - offset
    for piece in range(0, window, 256):
        ids = lax.broadcasted_iota(jnp.int32, (256, blocks), 0) + piece
        hot_ref[piece : piece + 256, :] = (ids == index).astype(f32).astype(bf16)
    start = pl.multiple_of(where_ref[1] * rows, rows)
    fill = fill_ref[pl.ds(where_ref[1] * rows // LANES, 1), :].astype(f32)
    scratch_ref[...] = jnp.broadcast_to(fill, (LANES, LANES)).T
    column = scratch_ref[pl.ds(pl.multiple_of(lax.rem(start, LANES), rows), rows), :]
    lane = lax.broadcasted_iota(jnp.int32, (rows, LANES), 1).astype(f32)
    valid_ref[...] = (lane < column).astype(f32)
    label_ref[...] = outcome_ref[pl.ds(start, rows), :].astype(f32)


def predict_kernel(lower_ref, own_ref, upper_ref, fixed_ref, hot_ref, design_ref, out_ref, coef_ref):
    size = own_ref.shape[0]
    blocks = out_ref.shape[0]
    parts = [three_parts(r[...]) for r in (lower_ref, own_ref, upper_ref)]
    window = jnp.concatenate(parts, axis=1)
    picked = jnp.dot(window, hot_ref[...], preferred_element_type=f32)
    coefs = picked[:size] + picked[size : 2 * size] + picked[2 * size :]
    padded = jnp.concatenate([coefs, jnp.zeros((LANES - size, blocks), f32)], axis=0)
    coef_ref[...] = padded.T[:, :size] + fixed_ref[...]
    step = 32

    def chunk(i, carry):
        start = pl.multiple_of(i * step, step)
        here = coef_ref[pl.ds(start, step), :]
        total = jnp.zeros((step, LANES), f32)
        for p in range(size):
            total = total + here[:, p : p + 1] * design_ref[p, pl.ds(start, step), :].astype(f32)
        out_ref[pl.ds(start, step), :] = total
        return carry

    lax.fori_loop(0, blocks // step, chunk, 0)


def residual_kernel(parts_ref, label_ref, valid_ref, out_ref):
    logits = jnp.sum(parts_ref[...], axis=0)
    residual = jnp.where(valid_ref[...] > 0.5, label_ref[...] - jax.nn.sigmoid(logits), 0.0)
    out_ref[...] = jnp.broadcast_to(residual[None], out_ref.shape)


def gradient_kernel(design_ref, residual_ref, hot_ref, lower_ref, own_ref, upper_ref, fixed_ref, grad_ref):
    size, blocks, _ = design_ref.shape
    groups = own_ref.shape[1]
    step = 32
    lane = lax.broadcasted_iota(jnp.int32, (step, LANES), 1)

    def chunk(i, carry):
        start = pl.multiple_of(i * step, step)
        residual = residual_ref[pl.ds(start, step), :]
        grads = jnp.zeros((step, LANES), f32)
        for p in range(size):
            product = design_ref[p, pl.ds(start, step), :].astype(f32) * residual
            grads = jnp.where(lane == p, jnp.sum(product, axis=1, keepdims=True), grads)
        grad_ref[pl.ds(start, step), :] = grads
        return carry

    lax.fori_loop(0, blocks // step, chunk, 0)
    grads = grad_ref[...]
    fixed_ref[...] = jnp.broadcast_to(jnp.sum(grads, axis=0, keepdims=True), fixed_ref.shape)
    parts = three_parts(grads.T[:size])
    sums = lax.dot_general(parts, hot_ref[...], (((1,), (1,)), ((), ())), preferred_element_type=f32)
    sums = sums[:size] + sums[size : 2 * size] + sums[2 * size :]
    lower_ref[...] = sums[:, :groups]
    own_ref[...] = sums[:, groups : 2 * groups]
    upper_ref[...] = sums[:, 2 * groups :]


def finish_kernel(fixed_ref, coef_ref, own_ref, down_ref, up_ref, prior_ref, fixed_out, slope_out):
    size = coef_ref.shape[1]
    fixed_out[...] = jnp.sum(fixed_ref[...], axis=0, keepdims=True)[:, :size] - coef_ref[...]
    slope_out[...] = own_ref[...] + down_ref[...] + up_ref[...] - prior_ref[...]


def shape(*dims, dtype=f32):
    return jax.ShapeDtypeStruct(dims, dtype)


def body(design, outcome, block_fill, block_group, fixed_coef, slopes, precision):
    size, group_count = slopes.shape
    blocks = block_group.shape[0]
    covs, rows = lax.axis_size("cov"), lax.axis_size("rows")
    share = blocks // covs

    from_lower = from_behind(slopes, "rows", 1)
    from_upper = from_behind(slopes, "rows", -1)

    gathered = exchange(jnp.broadcast_to(slopes[None], (covs, size, group_count)), "cov")
    prior_term = jnp.dot(
        precision, gathered.reshape(covs * size, group_count), precision=lax.Precision.HIGHEST
    )

    where = jnp.stack([(lax.axis_index("rows") - 1) * group_count, lax.axis_index("cov")])
    hot, label, valid = pl.pallas_call(
        select_kernel,
        out_shape=(
            shape(3 * group_count, blocks, dtype=bf16),
            shape(share, LANES),
            shape(share, LANES),
        ),
        in_specs=[SMEM, VMEM, VMEM, VMEM],
        out_specs=(VMEM, VMEM, VMEM),
        scratch_shapes=[pltpu.VMEM((LANES, LANES), f32)],
        compiler_params=ROOM,
        name="select",
    )(where, block_group.reshape(1, blocks), block_fill.reshape(blocks // LANES, LANES), outcome)

    fixed_row = fixed_coef.reshape(1, size)
    partial = pl.pallas_call(
        predict_kernel,
        out_shape=shape(blocks, LANES),
        in_specs=[VMEM] * 6,
        out_specs=VMEM,
        scratch_shapes=[pltpu.VMEM((blocks, size), f32)],
        compiler_params=ROOM,
        name="predict",
    )(from_lower, slopes, from_upper, fixed_row, hot, design)

    received = exchange(partial.reshape(covs, share, LANES), "cov")
    spread = pl.pallas_call(
        residual_kernel,
        out_shape=shape(covs, share, LANES),
        in_specs=[VMEM] * 3,
        out_specs=VMEM,
        compiler_params=ROOM,
        name="residual",
    )(received, label, valid)
    residual = exchange(spread, "cov").reshape(blocks, LANES)

    to_lower, own, to_upper, fixed_parts = pl.pallas_call(
        gradient_kernel,
        out_shape=(shape(size, group_count),) * 3 + (shape(rows, LANES),),
        in_specs=[VMEM] * 3,
        out_specs=(VMEM,) * 4,
        scratch_shapes=[pltpu.VMEM((blocks, LANES), f32)],
        compiler_params=ROOM,
        name="gradient",
    )(design, residual, hot)

    given_down = from_behind(to_lower, "rows", -1)
    given_up = from_behind(to_upper, "rows", 1)
    fixed_all = exchange(fixed_parts, "rows")
    fixed_grad, slope_grad = pl.pallas_call(
        finish_kernel,
        out_shape=(shape(1, size), shape(size, group_count)),
        in_specs=[VMEM] * 6,
        out_specs=(VMEM, VMEM),
        compiler_params=ROOM,
        name="finish",
    )(fixed_all, fixed_row, own, given_down, given_up, prior_term)
    return (fixed_grad.reshape(size), slope_grad)


def solution(mesh):
    return jax.shard_map(
        body,
        mesh=mesh,
        in_specs=(
            P("cov", "rows", None),
            P("rows", None),
            P("rows"),
            P("rows"),
            P("cov"),
            P("cov", "rows"),
            P("cov", None),
        ),
        out_specs=(P("cov"), P("cov", "rows")),
        check_vma=False,
    )
```

time: 278 us -> 116 us (0.42)
  waiting for transfers between devices: 129 us -> 10.1 us
  blocking collectives: 92.4 us -> 48.1 us
  starting transfers between devices: 25.4 us -> 42.2 us
  between operations: 14.2 us -> 0.78 us
  matrix products: 8.29 us -> 0.2 us
  Pallas kernels: 0 us -> 7.63 us
  other arithmetic: 6.79 us -> 0.08 us
  local copies, waits for them, and re-layouts: 1.37 us -> 6 us
    psum x1 -> x0, waiting for transfers between devices: 129 us -> none  [body(): logits = lax.psum(partial_value, 'cov')]
    psum x1 -> x0, blocking collectives: 69.9 us -> none  [body(): fixed_grad = lax.psum(jnp.sum(block_grads, axis=1), 'rows') - fixed_coef]
    all_to_all x0 -> x2, blocking collectives: none -> 48.1 us  [exchange(): return lax.all_to_all(parts, axis, 0, 0, tiled=True)]
    all_to_all x0 -> x2, starting transfers between devices: none -> 25.3 us  [exchange(): return lax.all_to_all(parts, axis, 0, 0, tiled=True)]
    all_gather x1 -> x0, blocking collectives: 22.5 us -> none  [body(): full_slopes = lax.all_gather(slopes, 'cov', axis=0, tiled=True)]
    all_to_all x0 -> x2, waiting for transfers between devices: none -> 10.1 us  [exchange(): return lax.all_to_all(parts, axis, 0, 0, tiled=True)]
    ppermute x4, starting transfers between devices: 25.3 us -> 16.9 us  [from_behind(): return lax.ppermute(shard, axis, pairs)]
    dot_general x3 -> x1, matrix products: 8.29 us -> 0.2 us  [body(): jnp.dot(precision, gathered.reshape(covs * size, group_count), precision=...]
  transfers between devices with their start and end apart: 5 -> 6, of which waited for: 2 -> 2; matrix products, arithmetic and copies ran while one was open for 0% -> 0% of each run, Pallas kernels for 0% -> 3%
where the time goes in v1:
time: 116 us; the launch traced here: 115 us
  blocking collectives  48.1 us (41%)
  starting transfers between devices  42.2 us (36%)
  waiting for transfers between devices  10.1 us (9%)
  Pallas kernels  7.63 us (7%)
  local copies, waits for them, and re-layouts  6 us (5%)
    all_to_all x2, blocking collectives, exchange(): return lax.all_to_all(parts, axis, 0, 0, tiled=True)  48.1 us
    all_to_all x2, starting transfers between devices, exchange(): return lax.all_to_all(parts, axis, 0, 0, tiled=True)  25.3 us
    ppermute x4, starting transfers between devices, from_behind(): return lax.ppermute(shard, axis, pairs)  16.9 us
    all_to_all x2, waiting for transfers between devices, exchange(): return lax.all_to_all(parts, axis, 0, 0, tiled=True)  10.1 us
    unnamed x18, local copies, waits for them, and re-layouts  5.29 us
    pallas_call x1, Pallas kernels, body(): pl.pallas_call(gradient_kernel, out_shape=(shape(size, group_count),) * 3...  3.23 us
    pallas_call x1, Pallas kernels, body(): pl.pallas_call(predict_kernel, out_shape=shape(blocks, LANES), in_specs=[...  2.96 us
  transfers between devices with their start and end apart: 6, of which 2 were waited for; matrix products, arithmetic and copies ran while one was open for 0% of the time, Pallas kernels for 3%

profile of v1, /device:TPU:1, one launch (start us, length us, event | category | flops | bytes accessed | tf_op | source)
XLA Modules:
  0.0 115.0 jit_solution(10407886272589939446)
XLA Ops:
  0.6 0.0 copy-start
  0.6 4.5 %collective-permute-start = (f32[16,256]{1,0:T(8,128)}, f32[16,256]{1,0:T(8,128)S(1)}, u32[]{:S(2)}, u32[]{:S(2)}) collective-permute-start(f32[16,256]{1,0:T(8,128)} %own_ref.1), channel_id=1, source_target_pairs={{0,16},{16,32},{32,48},{48,64},{64,80},{80,96},{96,112},{112,128},... | collective-permute-start | bytes 49160 | tf_op jit(solution)/shard_map/ppermute | solution.py:19
  5.2 5.6 %collective-permute-start.1 = (f32[16,256]{1,0:T(8,128)}, f32[16,256]{1,0:T(8,128)S(1)}, u32[]{:S(2)}, u32[]{:S(2)}) collective-permute-start(f32[16,256]{1,0:T(8,128)} %own_ref.1), channel_id=1, source_target_pairs={{16,0},{32,16},{48,32},{64,48},{80,64},{96,80},{112,96},{128,112},... | collective-permute-start | bytes 49160 | tf_op jit(solution)/shard_map/ppermute | solution.py:19
  10.7 0.1 pad_add_fusion.where_ref
  10.8 0.0 copy-start.3
  10.8 0.9 copy-done.3
  11.8 0.0 copy-start.5
  11.8 0.7 copy-done.5
  12.5 0.0 copy-start.6
  12.5 0.7 copy-done.6
  13.1 0.8 select.1
  13.9 0.0 collective-permute-done.lower_ref
  13.9 0.0 collective-permute-done.1.upper_ref
  14.0 0.0 copy-start.1
  14.0 1.6 %copy-done.1 = bf16[16,512,128]{2,1,0:T(8,128)(2,1)S(1)} copy-done((bf16[16,512,128]{2,1,0:T(8,128)(2,1)S(1)}, bf16[16,512,128]{2,1,0:T(8,128)(2,1)}, u32[]{:S(2)}) %copy-start.1) | copy-done | bytes 2097176
  15.5 0.0 copy-start.4
  15.5 0.7 copy-done.4
  16.3 0.0 copy-start.7
  16.3 0.7 copy-done.7
  16.9 0.0 copy-start.2
  16.9 3.0 %predict.1 = f32[512,128]{1,0:T(8,128)S(1)} custom-call(f32[16,256]{1,0:T(8,128)S(1)} %collective-permute-done.lower_ref, f32[16,256]{1,0:T(8,128)S(1)} %copy-done.4, f32[16,256]{1,0:T(8,128)S(1)} %collective-permute-done.1.upper_ref, f32[1,16]{1,0:T(1,128)S(1)} %bitcast.20, bf16[768,512]{1,0:T(8,128)(2,1)S(1)} %get-tuple-element.11.hot_ref, ...), custom_call_target="tpu_custom_call" | custom-call | tf_op jit(solution)/shard_map/predict/pallas_call | solution.py:147
  19.9 28.1 %all_to_all.26.parts_ref = f32[16,32,128]{2,1,0:T(8,128)S(1)} all-to-all(f32[16,32,128]{2,1,0:T(8,128)S(1)} %bitcast.16), channel_id=1, replica_groups=mesh['rows'=32,'cov'=16] {'cov'}, dimensions={0} | all-to-all | bytes 524288 | tf_op jit(solution)/shard_map/all_to_all | solution.py:23
  48.0 20.0 %all_to_all.27 = f32[16,32,128]{2,1,0:T(8,128)S(1)} all-to-all(f32[16,32,128]{2,1,0:T(8,128)S(1)} %residual.1), channel_id=1, replica_groups=mesh['rows'=32,'cov'=16] {'cov'}, dimensions={0} | all-to-all | bytes 524288 | tf_op jit(solution)/shard_map/all_to_all | solution.py:23
  68.0 0.0 copy-start.8
  68.0 0.7 broadcast_in_dim.2
  68.7 10.2 %all-to-all-start.3 = ((f32[16,16,256]{2,1,0:T(8,128)}), f32[16,16,256]{2,1,0:T(8,128)S(1)}, u32[]{:S(2)}, u32[]{:S(2)}) async-start(f32[16,16,256]{2,1,0:T(8,128)} %broadcast_in_dim.2), calls=%async_computation.3 | async-start | bytes 524288 | tf_op jit(solution)/shard_map/all_to_all | solution.py:23
  79.0 0.0 copy-done.2
  79.0 3.2 %gradient.1 = (f32[16,256]{1,0:T(8,128)S(1)}, f32[16,256]{1,0:T(8,128)S(1)}, f32[16,256]{1,0:T(8,128)S(1)}, f32[32,128]{1,0:T(8,128)}) custom-call(bf16[16,512,128]{2,1,0:T(8,128)(2,1)S(1)} %copy-done.2, f32[512,128]{1,0:T(8,128)S(1)} %bitcast.15, bf16[768,512]{1,0:T(8,128)(2,1)S(1)} %get-tuple-element.11.hot_ref), custom_call_target="tpu_custom_call" | custom-call | tf_op jit(solution)/shard_map/gradient/pallas_call | solution.py:168
  82.2 2.8 %collective-permute-start.2 = (f32[16,256]{1,0:T(8,128)S(1)}, f32[16,256]{1,0:T(8,128)S(1)}, u32[]{:S(2)}, u32[]{:S(2)}) collective-permute-start(f32[16,256]{1,0:T(8,128)S(1)} %get-tuple-element.16), channel_id=1, source_target_pairs={{16,0},{32,16},{48,32},{64,48},{80,64},{96,80},{112,96},{128,112},... | collective-permute-start | bytes 49160 | tf_op jit(solution)/shard_map/ppermute | solution.py:19
  85.0 4.0 %collective-permute-start.3 = (f32[16,256]{1,0:T(8,128)S(1)}, f32[16,256]{1,0:T(8,128)S(1)}, u32[]{:S(2)}, u32[]{:S(2)}) collective-permute-start(f32[16,256]{1,0:T(8,128)S(1)} %get-tuple-element.17), channel_id=1, source_target_pairs={{0,16},{16,32},{32,48},{48,64},{64,80},{80,96},{96,112},{112,128},... | collective-permute-start | bytes 49160 | tf_op jit(solution)/shard_map/ppermute | solution.py:19
  89.0 3.4 %all-to-all-done.3 = f32[16,16,256]{2,1,0:T(8,128)S(1)} async-done(((f32[16,16,256]{2,1,0:T(8,128)}), f32[16,16,256]{2,1,0:T(8,128)S(1)}, u32[]{:S(2)}, u32[]{:S(2)}) %all-to-all-start.3) | async-done | bytes 262176 | tf_op jit(solution)/shard_map/all_to_all | solution.py:23
  92.4 15.1 %all-to-all-start.2 = ((f32[32,1,128]{2,1,0:T(1,128)}), f32[32,1,128]{2,1,0:T(1,128)S(1)}, u32[]{:S(2)}, u32[]{:S(2)}) async-start(f32[32,1,128]{2,1,0:T(1,128)} %bitcast.8), calls=%async_computation.2 | async-start | bytes 32768 | tf_op jit(solution)/shard_map/all_to_all | solution.py:23
  107.5 0.0 copy-done
  107.5 0.2 fusion.prior_ref
  107.7 6.7 %all-to-all-done.2 = f32[32,1,128]{2,1,0:T(1,128)S(1)} async-done(((f32[32,1,128]{2,1,0:T(1,128)}), f32[32,1,128]{2,1,0:T(1,128)S(1)}, u32[]{:S(2)}, u32[]{:S(2)}) %all-to-all-start.2) | async-done | bytes 16416 | tf_op jit(solution)/shard_map/all_to_all | solution.py:23
  114.4 0.0 collective-permute-done.2.down_ref
  114.4 0.0 collective-permute-done.3.up_ref
  114.4 0.0 copy-done.8
  114.4 0.6 finish.1
  (1 shorter events, 0.0 us)
Async XLA Ops:
  0.6 106.9 %copy-start = (f32[16,256]{1,0:T(8,128)S(1)}, f32[16,256]{1,0:T(8,128)}, u32[]{:S(2)}) copy-start(f32[16,256]{1,0:T(8,128)} %param.13) | copy-start | bytes 49156
  0.6 13.3 %collective-permute-start = (f32[16,256]{1,0:T(8,128)}, f32[16,256]{1,0:T(8,128)S(1)}, u32[]{:S(2)}, u32[]{:S(2)}) collective-permute-start(f32[16,256]{1,0:T(8,128)} %own_ref.1), channel_id=1, source_target_pairs={{0,16},{16,32},{32,48},{48,64},{64,80},{80,96},{96,112},{112,128},... | collective-permute-start | bytes 49160 | tf_op jit(solution)/shard_map/ppermute | solution.py:19
  5.2 8.8 %collective-permute-start.1 = (f32[16,256]{1,0:T(8,128)}, f32[16,256]{1,0:T(8,128)S(1)}, u32[]{:S(2)}, u32[]{:S(2)}) collective-permute-start(f32[16,256]{1,0:T(8,128)} %own_ref.1), channel_id=1, source_target_pairs={{16,0},{32,16},{48,32},{64,48},{80,64},{96,80},{112,96},{128,112},... | collective-permute-start | bytes 49160 | tf_op jit(solution)/shard_map/ppermute | solution.py:19
  10.8 1.0 copy-start.3
  11.8 0.7 copy-start.5
  12.5 0.7 copy-start.6
  14.0 1.6 %copy-start.1 = (bf16[16,512,128]{2,1,0:T(8,128)(2,1)S(1)}, bf16[16,512,128]{2,1,0:T(8,128)(2,1)}, u32[]{:S(2)}) copy-start(bf16[16,512,128]{2,1,0:T(8,128)(2,1)} %design_ref.3) | copy-start | bytes 6291460
  15.5 0.7 copy-start.4
  16.3 0.7 copy-start.7
  16.9 62.1 %copy-start.2 = (bf16[16,512,128]{2,1,0:T(8,128)(2,1)S(1)}, bf16[16,512,128]{2,1,0:T(8,128)(2,1)}, u32[]{:S(2)}) copy-start(bf16[16,512,128]{2,1,0:T(8,128)(2,1)} %design_ref.3) | copy-start | bytes 6291460
  68.0 46.4 %copy-start.8 = (f32[16]{0:T(128)S(1)}, f32[16]{0:T(128)}, u32[]{:S(2)}) copy-start(f32[16]{0:T(128)} %param.11) | copy-start | bytes 196
  68.7 23.7 %all-to-all-start.3 = ((f32[16,16,256]{2,1,0:T(8,128)}), f32[16,16,256]{2,1,0:T(8,128)S(1)}, u32[]{:S(2)}, u32[]{:S(2)}) async-start(f32[16,16,256]{2,1,0:T(8,128)} %broadcast_in_dim.2), calls=%async_computation.3 | async-start | bytes 524288 | tf_op jit(solution)/shard_map/all_to_all | solution.py:23
  82.2 32.2 %collective-permute-start.2 = (f32[16,256]{1,0:T(8,128)S(1)}, f32[16,256]{1,0:T(8,128)S(1)}, u32[]{:S(2)}, u32[]{:S(2)}) collective-permute-start(f32[16,256]{1,0:T(8,128)S(1)} %get-tuple-element.16), channel_id=1, source_target_pairs={{16,0},{32,16},{48,32},{64,48},{80,64},{96,80},{112,96},{128,112},... | collective-permute-start | bytes 49160 | tf_op jit(solution)/shard_map/ppermute | solution.py:19
  85.0 29.4 %collective-permute-start.3 = (f32[16,256]{1,0:T(8,128)S(1)}, f32[16,256]{1,0:T(8,128)S(1)}, u32[]{:S(2)}, u32[]{:S(2)}) collective-permute-start(f32[16,256]{1,0:T(8,128)S(1)} %get-tuple-element.17), channel_id=1, source_target_pairs={{0,16},{16,32},{32,48},{48,64},{64,80},{80,96},{96,112},{112,128},... | collective-permute-start | bytes 49160 | tf_op jit(solution)/shard_map/ppermute | solution.py:19
  92.4 22.0 %all-to-all-start.2 = ((f32[32,1,128]{2,1,0:T(1,128)}), f32[32,1,128]{2,1,0:T(1,128)S(1)}, u32[]{:S(2)}, u32[]{:S(2)}) async-start(f32[32,1,128]{2,1,0:T(1,128)} %bitcast.8), calls=%async_computation.2 | async-start | bytes 32768 | tf_op jit(solution)/shard_map/all_to_all | solution.py:23

commit v2 on v1

v2 whole, which is shorter than its diff:
```python
import jax
import jax.numpy as jnp
from jax import lax
from jax.experimental import pallas as pl
from jax.experimental.pallas import tpu as pltpu
from jax.sharding import PartitionSpec as P

f32 = jnp.float32
bf16 = jnp.bfloat16
VMEM = pl.BlockSpec(memory_space=pltpu.VMEM)
SMEM = pl.BlockSpec(memory_space=pltpu.SMEM)
HBM = pl.BlockSpec(memory_space=pltpu.HBM)
LANES = 128
ROOM = pltpu.CompilerParams(vmem_limit_bytes=16 << 20)


def from_behind(shard, axis, by):
    peers = lax.axis_size(axis)
    pairs = [(i, i + by) for i in range(peers) if 0 <= i + by < peers]
    return lax.ppermute(shard, axis, pairs)


def exchange(parts, axis):
    return lax.all_to_all(parts, axis, 0, 0, tiled=True)


def cost(flops, size):
    return pl.CostEstimate(flops=flops, bytes_accessed=size, transcendentals=0)


def three_parts(x):
    a = x.astype(bf16)
    rest = x - a.astype(f32)
    b = rest.astype(bf16)
    c = (rest - b.astype(f32)).astype(bf16)
    return jnp.concatenate([a, b, c], axis=0)


def add_parts(x):
    size = x.shape[0] // 3
    return x[:size] + x[size : 2 * size] + x[2 * size :]


def select_kernel(
    where_ref, group_hbm, fill_hbm, outcome_hbm, fixed_hbm, slopes_hbm, design_hbm,
    hot_ref, label_ref, valid_ref, fixed_ref, slope_ref, coef_ref, design_ref,
    group_ref, fill_ref, outcome_ref, own_ref, column_ref, sems,
):
    window, blocks = hot_ref.shape
    rows = label_ref.shape[0]
    size, groups = own_ref.shape
    start = pl.multiple_of(where_ref[1] * rows, rows)
    copies = [
        pltpu.make_async_copy(group_hbm, group_ref, sems.at[0]),
        pltpu.make_async_copy(slopes_hbm, own_ref, sems.at[1]),
        pltpu.make_async_copy(fixed_hbm, fixed_ref, sems.at[2]),
        pltpu.make_async_copy(fill_hbm, fill_ref, sems.at[3]),
        pltpu.make_async_copy(outcome_hbm.at[pl.ds(start, rows)], outcome_ref, sems.at[4]),
        pltpu.make_async_copy(design_hbm, design_ref, sems.at[5]),
    ]
    for copy in copies:
        copy.start()
    for copy in copies[:5]:
        copy.wait()
    index = group_ref[...] - where_ref[0]
    for piece in range(0, window, groups):
        ids = lax.broadcasted_iota(jnp.int32, (groups, blocks), 0) + piece
        hot_ref[piece : piece + groups, :] = (ids == index).astype(f32).astype(bf16)
    own = own_ref[...]
    for half in range(groups // LANES):
        slope_ref[half * size : (half + 1) * size, :] = own[:, half * LANES : (half + 1) * LANES]
    coef_ref[...] = add_parts(
        jnp.dot(three_parts(own), hot_ref[groups : 2 * groups, :], preferred_element_type=f32)
    )
    fill = fill_ref[pl.ds(start // LANES, 1), :].astype(f32)
    column_ref[...] = jnp.broadcast_to(fill, (LANES, LANES)).T
    column = column_ref[pl.ds(pl.multiple_of(lax.rem(start, LANES), rows), rows), :]
    lane = lax.broadcasted_iota(jnp.int32, (rows, LANES), 1).astype(f32)
    valid_ref[...] = (lane < column).astype(f32)
    label_ref[...] = outcome_ref[...].astype(f32)
    copies[5].wait()


def predict_kernel(lower_ref, upper_ref, own_coef_ref, fixed_ref, hot_ref, design_ref, out_ref, coef_ref):
    size, groups = lower_ref.shape
    blocks = out_ref.shape[0]
    coefs = own_coef_ref[...]
    coefs += add_parts(
        jnp.dot(three_parts(lower_ref[...]), hot_ref[:groups, :], preferred_element_type=f32)
    )
    coefs += add_parts(
        jnp.dot(three_parts(upper_ref[...]), hot_ref[2 * groups :, :], preferred_element_type=f32)
    )
    padded = jnp.concatenate([coefs, jnp.zeros((LANES - size, blocks), f32)], axis=0)
    coef_ref[...] = padded.T[:, :size] + fixed_ref[...]
    step = 32

    def chunk(i, carry):
        start = pl.multiple_of(i * step, step)
        here = coef_ref[pl.ds(start, step), :]
        total = jnp.zeros((step, LANES), f32)
        for p in range(size):
            total = total + here[:, p : p + 1] * design_ref[p, pl.ds(start, step), :].astype(f32)
        out_ref[pl.ds(start, step), :] = total
        return carry

    lax.fori_loop(0, blocks // step, chunk, 0)


def residual_kernel(parts_ref, label_ref, valid_ref, slope_ref, out_ref):
    rows = label_ref.shape[0]
    logits = jnp.sum(parts_ref[...], axis=0)
    residual = jnp.where(valid_ref[...] > 0.5, label_ref[...] - jax.nn.sigmoid(logits), 0.0)
    peers = out_ref.shape[0]
    out_ref[:, :rows, :] = jnp.broadcast_to(residual[None], (peers,) + residual.shape)
    out_ref[:, rows:, :] = jnp.broadcast_to(slope_ref[...][None], (peers,) + slope_ref.shape)


def gradient_kernel(design_ref, back_ref, fixed_ref, grad_ref):
    size, blocks, _ = design_ref.shape
    step = blocks // back_ref.shape[0]
    lane = lax.broadcasted_iota(jnp.int32, (step, LANES), 1)

    def chunk(i, total):
        start = pl.multiple_of(i * step, step)
        residual = back_ref[i, :step, :]
        grads = jnp.zeros((step, LANES), f32)
        for p in range(size):
            product = design_ref[p, pl.ds(start, step), :].astype(f32) * residual
            grads = jnp.where(lane == p, jnp.sum(product, axis=1, keepdims=True), grads)
        grad_ref[pl.ds(start, step), :] = grads
        return total + grads

    total = lax.fori_loop(0, blocks // step, chunk, jnp.zeros((step, LANES), f32))
    fixed_ref[...] = jnp.broadcast_to(jnp.sum(total, axis=0, keepdims=True), fixed_ref.shape)


def group_kernel(grad_ref, hot_ref, back_ref, precision_ref, lower_ref, own_ref, upper_ref):
    size, groups = own_ref.shape
    rows = back_ref.shape[1] - size * (groups // LANES)
    parts = three_parts(grad_ref[...].T[:size])
    sums = add_parts(
        lax.dot_general(parts, hot_ref[...], (((1,), (1,)), ((), ())), preferred_element_type=f32)
    )
    lower_ref[...] = sums[:, :groups]
    upper_ref[...] = sums[:, 2 * groups :]
    slopes = [
        back_ref[:, rows + half * size : rows + (half + 1) * size, :].reshape(-1, LANES)
        for half in range(groups // LANES)
    ]
    prior = jnp.dot(
        precision_ref[...],
        jnp.concatenate(slopes, axis=1),
        precision=lax.Precision.HIGHEST,
        preferred_element_type=f32,
    )
    own_ref[...] = sums[:, groups : 2 * groups] - prior


def finish_kernel(fixed_all_ref, fixed_ref, own_ref, down_ref, up_ref, fixed_out, slope_out):
    size = fixed_ref.shape[1]
    fixed_out[...] = jnp.sum(fixed_all_ref[...], axis=0, keepdims=True)[:, :size] - fixed_ref[...]
    slope_out[...] = own_ref[...] + down_ref[...] + up_ref[...]


def shape(*dims, dtype=f32):
    return jax.ShapeDtypeStruct(dims, dtype)


def body(design, outcome, block_fill, block_group, fixed_coef, slopes, precision):
    size, group_count = slopes.shape
    blocks = block_group.shape[0]
    covs, rows = lax.axis_size("cov"), lax.axis_size("rows")
    share = blocks // covs
    slope_rows = size * group_count // LANES

    from_lower = from_behind(slopes, "rows", 1)
    from_upper = from_behind(slopes, "rows", -1)

    where = jnp.stack([(lax.axis_index("rows") - 1) * group_count, lax.axis_index("cov")])
    hot, label, valid, fixed_row, own_rows, own_coefs, design_here = pl.pallas_call(
        select_kernel,
        out_shape=(
            shape(3 * group_count, blocks, dtype=bf16),
            shape(share, LANES),
            shape(share, LANES),
            shape(1, size),
            shape(slope_rows, LANES),
            shape(size, blocks),
            shape(*design.shape, dtype=bf16),
        ),
        in_specs=[SMEM] + [HBM] * 6,
        out_specs=(VMEM,) * 7,
        scratch_shapes=[
            pltpu.VMEM((1, blocks), jnp.int32),
            pltpu.VMEM((blocks // LANES, LANES), jnp.int32),
            pltpu.VMEM((share, LANES), jnp.int32),
            pltpu.VMEM((size, group_count), f32),
            pltpu.VMEM((LANES, LANES), f32),
            pltpu.SemaphoreType.DMA((6,)),
        ],
        compiler_params=ROOM,
        cost_estimate=cost(10_000_000, 5_000_000),
        name="select",
    )(
        where,
        *(
            pltpu.with_memory_space_constraint(x, pltpu.HBM)
            for x in (
                block_group.reshape(1, blocks),
                block_fill.reshape(blocks // LANES, LANES),
                outcome,
                fixed_coef.reshape(1, size),
                slopes,
                design,
            )
        ),
    )

    partial = pl.pallas_call(
        predict_kernel,
        out_shape=shape(blocks, LANES),
        in_specs=[VMEM] * 6,
        out_specs=VMEM,
        scratch_shapes=[pltpu.VMEM((blocks, size), f32)],
        compiler_params=ROOM,
        name="predict",
    )(from_lower, from_upper, own_coefs, fixed_row, hot, design_here)

    received = exchange(partial.reshape(covs, share, LANES), "cov")
    spread = pl.pallas_call(
        residual_kernel,
        out_shape=shape(covs, share + slope_rows, LANES),
        in_specs=[VMEM] * 4,
        out_specs=VMEM,
        compiler_params=ROOM,
        name="residual",
    )(received, label, valid, own_rows)
    back = exchange(spread, "cov")

    fixed_parts, grads = pl.pallas_call(
        gradient_kernel,
        out_shape=(shape(rows, LANES), shape(blocks, LANES)),
        in_specs=[VMEM] * 2,
        out_specs=(VMEM,) * 2,
        compiler_params=ROOM,
        name="gradient",
    )(design_here, back)
    fixed_all = exchange(fixed_parts, "rows")

    to_lower, own, to_upper = pl.pallas_call(
        group_kernel,
        out_shape=(shape(size, group_count),) * 3,
        in_specs=[VMEM] * 4,
        out_specs=(VMEM,) * 3,
        compiler_params=ROOM,
        cost_estimate=cost(100_000_000, 5_000_000),
        name="group",
    )(grads, hot, back, precision)
    given_down = from_behind(to_lower, "rows", -1)
    given_up = from_behind(to_upper, "rows", 1)

    fixed_grad, slope_grad = pl.pallas_call(
        finish_kernel,
        out_shape=(shape(1, size), shape(size, group_count)),
        in_specs=[VMEM] * 5,
        out_specs=(VMEM, VMEM),
        compiler_params=ROOM,
        name="finish",
    )(fixed_all, fixed_row, own, given_down, given_up)
    return (fixed_grad.reshape(size), slope_grad)


def solution(mesh):
    return jax.shard_map(
        body,
        mesh=mesh,
        in_specs=(
            P("cov", "rows", None),
            P("rows", None),
            P("rows"),
            P("rows"),
            P("cov"),
            P("cov", "rows"),
            P("cov", None),
        ),
        out_specs=(P("cov"), P("cov", "rows")),
        check_vma=False,
    )
```

time: 116 us -> 104 us (0.90)
  blocking collectives: 48.1 us -> 71.9 us
  starting transfers between devices: 42.2 us -> 22.8 us
  waiting for transfers between devices: 10.1 us -> 0.01 us
  local copies, waits for them, and re-layouts: 6 us -> 0.01 us
    all_to_all x2 -> x0, starting transfers between devices: 25.3 us -> none  [exchange(): return lax.all_to_all(parts, axis, 0, 0, tiled=True)]
    all_to_all x2 -> x3, blocking collectives: 48.1 us -> 71.9 us  [exchange(): return lax.all_to_all(parts, axis, 0, 0, tiled=True)]
    all_to_all x2 -> x0, waiting for transfers between devices: 10.1 us -> none  [exchange(): return lax.all_to_all(parts, axis, 0, 0, tiled=True)]
    ppermute x4, starting transfers between devices: 16.9 us -> 22.8 us  [from_behind(): return lax.ppermute(shard, axis, pairs)]
    unnamed x18 -> x2, local copies, waits for them, and re-layouts: 5.29 us -> 0.01 us
    pallas_call x1, Pallas kernels: 0.78 us -> 2.27 us  [body(): pl.pallas_call(select_kernel, out_shape=(shape(3 * group_count, blocks, d...]
    pallas_call x2 -> x3, Pallas kernels: 3.27 us -> 2.85 us  [the longest x1 2.34 us: body(): pl.pallas_call(gradient_kernel, out_shape=(shape(rows, LANES), shape(bloc...]
  transfers between devices with their start and end apart: 6 -> 4, of which waited for: 2 -> 0; matrix products, arithmetic and copies ran while one was open for 0% -> 0% of each run, Pallas kernels for 3% -> 2%
where the time goes in v2:
time: 104 us
  blocking collectives  71.9 us (69%)
  starting transfers between devices  22.8 us (22%)
  Pallas kernels  8.66 us (8%)
    all_to_all x3, blocking collectives, exchange(): return lax.all_to_all(parts, axis, 0, 0, tiled=True)  71.9 us
    ppermute x4, starting transfers between devices, from_behind(): return lax.ppermute(shard, axis, pairs)  22.8 us
    pallas_call x1, Pallas kernels, body(): pl.pallas_call(predict_kernel, out_shape=shape(blocks, LANES), in_specs=[...  2.92 us
    pallas_call x1, Pallas kernels, body(): pl.pallas_call(gradient_kernel, out_shape=(shape(rows, LANES), shape(bloc...  2.34 us
    pallas_call x1, Pallas kernels, body(): pl.pallas_call(select_kernel, out_shape=(shape(3 * group_count, blocks, d...  2.27 us
  transfers between devices with their start and end apart: 4, of which 0 were waited for; matrix products, arithmetic and copies ran while one was open for 0% of the time, Pallas kernels for 2%

profile of v2, /device:TPU:1, one launch (start us, length us, event | category | flops | bytes accessed | tf_op | source)
XLA Modules:
  0.0 104.1 jit_solution(955470358892795532)
XLA Ops:
  0.6 8.8 %collective-permute-start.1 = (f32[16,256]{1,0:T(8,128)}, f32[16,256]{1,0:T(8,128)S(1)}, u32[]{:S(2)}, u32[]{:S(2)}) collective-permute-start(f32[16,256]{1,0:T(8,128)} %slopes_hbm.1), channel_id=1, source_target_pairs={{16,0},{32,16},{48,32},{64,48},{80,64},{96,80},{112,96},{128,112},... | collective-permute-start | bytes 49160 | tf_op jit(solution)/shard_map/ppermute | solution.py:20
  9.4 1.9 %collective-permute-start = (f32[16,256]{1,0:T(8,128)}, f32[16,256]{1,0:T(8,128)S(1)}, u32[]{:S(2)}, u32[]{:S(2)}) collective-permute-start(f32[16,256]{1,0:T(8,128)} %slopes_hbm.1), channel_id=1, source_target_pairs={{0,16},{16,32},{32,48},{48,64},{64,80},{80,96},{96,112},{112,128},... | collective-permute-start | bytes 49160 | tf_op jit(solution)/shard_map/ppermute | solution.py:20
  11.4 0.1 pad_add_fusion.where_ref
  11.4 2.3 %select.1 = (bf16[768,512]{1,0:T(8,128)(2,1)S(1)}, f32[32,128]{1,0:T(8,128)S(1)}, f32[32,128]{1,0:T(8,128)S(1)}, f32[1,16]{1,0:T(1,128)S(1)}, f32[32,128]{1,0:T(...) custom-call(s32[2]{0:T(128)S(1)} %pad_add_fusion.where_ref, s32[1,512]{1,0:T(1,128)} %bitcast.14, ...), custom_call_target="tpu_custom_call" | custom-call | flops 10000000 | bytes 5000000 | tf_op jit(solution)/shard_map/select/pallas_call | solution.py:181
  13.7 0.0 collective-permute-done.1.upper_ref
  13.7 0.0 collective-permute-done.lower_ref
  13.7 2.9 %predict.1 = f32[512,128]{1,0:T(8,128)S(1)} custom-call(f32[16,256]{1,0:T(8,128)S(1)} %collective-permute-done.lower_ref, f32[16,256]{1,0:T(8,128)S(1)} %collective-permute-done.1.upper_ref, f32[16,512]{1,0:T(8,128)S(1)} %get-tuple-element.17.own_coef_ref, f32[1,16]{1,0:T(1,128)S(1)} %get-tuple-element.18.fixed_ref, ...), custom_call_target="tpu_custom_call" | custom-call | tf_op jit(solution)/shard_map/predict/pallas_call | solution.py:220
  16.7 27.3 %all_to_all.21.parts_ref = f32[16,32,128]{2,1,0:T(8,128)S(1)} all-to-all(f32[16,32,128]{2,1,0:T(8,128)S(1)} %bitcast.11), channel_id=1, replica_groups=mesh['rows'=32,'cov'=16] {'cov'}, dimensions={0} | all-to-all | bytes 524288 | tf_op jit(solution)/shard_map/all_to_all | solution.py:24
  44.0 0.0 copy-start
  44.0 0.1 residual.1
  44.1 30.1 %all_to_all.22.back_ref = f32[16,64,128]{2,1,0:T(8,128)S(1)} all-to-all(f32[16,64,128]{2,1,0:T(8,128)S(1)} %residual.1), channel_id=1, replica_groups=mesh['rows'=32,'cov'=16] {'cov'}, dimensions={0} | all-to-all | bytes 1048576 | tf_op jit(solution)/shard_map/all_to_all | solution.py:24
  74.1 2.3 %gradient.1 = (f32[32,128]{1,0:T(8,128)S(1)}, f32[512,128]{1,0:T(8,128)S(1)}) custom-call(bf16[16,512,128]{2,1,0:T(8,128)(2,1)S(1)} %get-tuple-element.16.design_ref, f32[16,64,128]{2,1,0:T(8,128)S(1)} %all_to_all.22.back_ref), custom_call_target="tpu_custom_call" | custom-call | tf_op jit(solution)/shard_map/gradient/pallas_call | solution.py:241
  76.5 0.0 copy-done
  76.5 0.5 group.1
  77.0 9.1 %collective-permute-start.2 = (f32[16,256]{1,0:T(8,128)S(1)}, f32[16,256]{1,0:T(8,128)S(1)}, u32[]{:S(2)}, u32[]{:S(2)}) collective-permute-start(f32[16,256]{1,0:T(8,128)S(1)} %get-tuple-element.26), channel_id=1, source_target_pairs={{16,0},{32,16},{48,32},{64,48},{80,64},{96,80},{112,96},{128,112},... | collective-permute-start | bytes 49160 | tf_op jit(solution)/shard_map/ppermute | solution.py:20
  86.1 2.9 %collective-permute-start.3 = (f32[16,256]{1,0:T(8,128)S(1)}, f32[16,256]{1,0:T(8,128)S(1)}, u32[]{:S(2)}, u32[]{:S(2)}) collective-permute-start(f32[16,256]{1,0:T(8,128)S(1)} %get-tuple-element.27), channel_id=1, source_target_pairs={{0,16},{16,32},{32,48},{48,64},{64,80},{80,96},{96,112},{112,128},... | collective-permute-start | bytes 49160 | tf_op jit(solution)/shard_map/ppermute | solution.py:20
  89.0 14.5 %all_to_all.23 = f32[32,1,128]{2,1,0:T(1,128)S(1)} all-to-all(f32[32,1,128]{2,1,0:T(1,128)S(1)} %bitcast.13), channel_id=1, replica_groups=mesh['rows'=32,'cov'=16] {'rows'}, dimensions={0} | all-to-all | bytes 32768 | tf_op jit(solution)/shard_map/all_to_all | solution.py:24
  103.5 0.0 collective-permute-done.2.down_ref
  103.5 0.0 collective-permute-done.3.up_ref
  103.5 0.6 finish.1
Async XLA Ops:
  0.6 13.1 %collective-permute-start.1 = (f32[16,256]{1,0:T(8,128)}, f32[16,256]{1,0:T(8,128)S(1)}, u32[]{:S(2)}, u32[]{:S(2)}) collective-permute-start(f32[16,256]{1,0:T(8,128)} %slopes_hbm.1), channel_id=1, source_target_pairs={{16,0},{32,16},{48,32},{64,48},{80,64},{96,80},{112,96},{128,112},... | collective-permute-start | bytes 49160 | tf_op jit(solution)/shard_map/ppermute | solution.py:20
  9.4 4.3 %collective-permute-start = (f32[16,256]{1,0:T(8,128)}, f32[16,256]{1,0:T(8,128)S(1)}, u32[]{:S(2)}, u32[]{:S(2)}) collective-permute-start(f32[16,256]{1,0:T(8,128)} %slopes_hbm.1), channel_id=1, source_target_pairs={{0,16},{16,32},{32,48},{48,64},{64,80},{80,96},{96,112},{112,128},... | collective-permute-start | bytes 49160 | tf_op jit(solution)/shard_map/ppermute | solution.py:20
  44.0 32.5 %copy-start = (f32[16,256]{1,0:T(8,128)S(1)}, f32[16,256]{1,0:T(8,128)}, u32[]{:S(2)}) copy-start(f32[16,256]{1,0:T(8,128)} %precision_ref.1) | copy-start | bytes 49156
  77.0 26.6 %collective-permute-start.2 = (f32[16,256]{1,0:T(8,128)S(1)}, f32[16,256]{1,0:T(8,128)S(1)}, u32[]{:S(2)}, u32[]{:S(2)}) collective-permute-start(f32[16,256]{1,0:T(8,128)S(1)} %get-tuple-element.26), channel_id=1, source_target_pairs={{16,0},{32,16},{48,32},{64,48},{80,64},{96,80},{112,96},{128,112},... | collective-permute-start | bytes 49160 | tf_op jit(solution)/shard_map/ppermute | solution.py:20
  86.1 17.5 %collective-permute-start.3 = (f32[16,256]{1,0:T(8,128)S(1)}, f32[16,256]{1,0:T(8,128)S(1)}, u32[]{:S(2)}, u32[]{:S(2)}) collective-permute-start(f32[16,256]{1,0:T(8,128)S(1)} %get-tuple-element.27), channel_id=1, source_target_pairs={{0,16},{16,32},{32,48},{48,64},{64,80},{80,96},{96,112},{112,128},... | collective-permute-start | bytes 49160 | tf_op jit(solution)/shard_map/ppermute | solution.py:20

commit v3 on v2

--- a/solution.py
+++ b/solution.py
@@ -11,6 +11,7 @@
 SMEM = pl.BlockSpec(memory_space=pltpu.SMEM)
 HBM = pl.BlockSpec(memory_space=pltpu.HBM)
 LANES = 128
+NEAR = 4
 ROOM = pltpu.CompilerParams(vmem_limit_bytes=16 << 20)
 
 
@@ -20,8 +21,8 @@
     return lax.ppermute(shard, axis, pairs)
 
 
-def exchange(parts, axis):
-    return lax.all_to_all(parts, axis, 0, 0, tiled=True)
+def exchange(parts, axis, groups=None):
+    return lax.all_to_all(parts, axis, 0, 0, tiled=True, axis_index_groups=groups)
 
 
 def cost(flops, size):
@@ -44,12 +45,12 @@
 def select_kernel(
     where_ref, group_hbm, fill_hbm, outcome_hbm, fixed_hbm, slopes_hbm, design_hbm,
     hot_ref, label_ref, valid_ref, fixed_ref, slope_ref, coef_ref, design_ref,
-    group_ref, fill_ref, outcome_ref, own_ref, column_ref, sems,
+    group_ref, fill_ref, outcome_ref, own_ref, sems,
 ):
     window, blocks = hot_ref.shape
     rows = label_ref.shape[0]
     size, groups = own_ref.shape
-    start = pl.multiple_of(where_ref[1] * rows, rows)
+    start = pl.multiple_of(lax.rem(where_ref[1], NEAR) * rows, rows)
     copies = [
         pltpu.make_async_copy(group_hbm, group_ref, sems.at[0]),
         pltpu.make_async_copy(slopes_hbm, own_ref, sems.at[1]),
@@ -72,9 +73,8 @@
     coef_ref[...] = add_parts(
         jnp.dot(three_parts(own), hot_ref[groups : 2 * groups, :], preferred_element_type=f32)
     )
-    fill = fill_ref[pl.ds(start // LANES, 1), :].astype(f32)
-    column_ref[...] = jnp.broadcast_to(fill, (LANES, LANES)).T
-    column = column_ref[pl.ds(pl.multiple_of(lax.rem(start, LANES), rows), rows), :]
+    fill = fill_ref[pl.ds(lax.rem(where_ref[1], NEAR), 1), :].astype(f32)
+    column = jnp.broadcast_to(fill, (rows, rows)).T
     lane = lax.broadcasted_iota(jnp.int32, (rows, LANES), 1).astype(f32)
     valid_ref[...] = (lane < column).astype(f32)
     label_ref[...] = outcome_ref[...].astype(f32)
@@ -107,47 +107,64 @@
     lax.fori_loop(0, blocks // step, chunk, 0)
 
 
-def residual_kernel(parts_ref, label_ref, valid_ref, slope_ref, out_ref):
+def spread_rows(out_ref, *pieces):
+    at = 0
+    for piece in pieces:
+        size = piece.shape[0]
+        out_ref[:, at : at + size, :] = jnp.broadcast_to(piece[None], (out_ref.shape[0],) + piece.shape)
+        at += size
+
+
+def gather_kernel(parts_ref, slope_ref, out_ref):
+    spread_rows(out_ref, jnp.sum(parts_ref[...], axis=0), slope_ref[...])
+
+
+def residual_kernel(parts_ref, label_ref, valid_ref, out_ref):
     rows = label_ref.shape[0]
-    logits = jnp.sum(parts_ref[...], axis=0)
+    logits = jnp.sum(parts_ref[:, :rows, :], axis=0)
     residual = jnp.where(valid_ref[...] > 0.5, label_ref[...] - jax.nn.sigmoid(logits), 0.0)
-    peers = out_ref.shape[0]
-    out_ref[:, :rows, :] = jnp.broadcast_to(residual[None], (peers,) + residual.shape)
-    out_ref[:, rows:, :] = jnp.broadcast_to(slope_ref[...][None], (peers,) + slope_ref.shape)
+    spread_rows(out_ref, residual, *(parts_ref[i, rows:, :] for i in range(parts_ref.shape[0])))
 
 
 def gradient_kernel(design_ref, back_ref, fixed_ref, grad_ref):
     size, blocks, _ = design_ref.shape
-    step = blocks // back_ref.shape[0]
+    step = 32
+    share = blocks // NEAR
     lane = lax.broadcasted_iota(jnp.int32, (step, LANES), 1)
-
-    def chunk(i, total):
-        start = pl.multiple_of(i * step, step)
-        residual = back_ref[i, :step, :]
-        grads = jnp.zeros((step, LANES), f32)
-        for p in range(size):
-            product = design_ref[p, pl.ds(start, step), :].astype(f32) * residual
-            grads = jnp.where(lane == p, jnp.sum(product, axis=1, keepdims=True), grads)
-        grad_ref[pl.ds(start, step), :] = grads
-        return total + grads
-
-    total = lax.fori_loop(0, blocks // step, chunk, jnp.zeros((step, LANES), f32))
+    total = jnp.zeros((step, LANES), f32)
+    for peer in range(NEAR):
+
+        def chunk(i, total, peer=peer):
+            inner = pl.multiple_of(i * step, step)
+            start = pl.multiple_of(peer * share + i * step, step)
+            residual = back_ref[peer, pl.ds(inner, step), :]
+            grads = jnp.zeros((step, LANES), f32)
+            for p in range(size):
+                product = design_ref[p, pl.ds(start, step), :].astype(f32) * residual
+                grads = jnp.where(lane == p, jnp.sum(product, axis=1, keepdims=True), grads)
+            grad_ref[pl.ds(start, step), :] = grads
+            return total + grads
+
+        total = lax.fori_loop(0, share // step, chunk, total)
     fixed_ref[...] = jnp.broadcast_to(jnp.sum(total, axis=0, keepdims=True), fixed_ref.shape)
 
 
 def group_kernel(grad_ref, hot_ref, back_ref, precision_ref, lower_ref, own_ref, upper_ref):
     size, groups = own_ref.shape
-    rows = back_ref.shape[1] - size * (groups // LANES)
+    halves = groups // LANES
+    far = precision_ref.shape[1] // (size * NEAR)
+    rows = back_ref.shape[1] - far * size * halves
     parts = three_parts(grad_ref[...].T[:size])
     sums = add_parts(
         lax.dot_general(parts, hot_ref[...], (((1,), (1,)), ((), ())), preferred_element_type=f32)
     )
     lower_ref[...] = sums[:, :groups]
     upper_ref[...] = sums[:, 2 * groups :]
-    slopes = [
-        back_ref[:, rows + half * size : rows + (half + 1) * size, :].reshape(-1, LANES)
-        for half in range(groups // LANES)
-    ]
+    slopes = []
+    for half in range(halves):
+        starts = [rows + (i * halves + half) * size for i in range(far)]
+        pieces = [back_ref[:, at : at + size, :].reshape(-1, LANES) for at in starts]
+        slopes.append(jnp.concatenate(pieces, axis=0))
     prior = jnp.dot(
         precision_ref[...],
         jnp.concatenate(slopes, axis=1),
@@ -171,7 +188,10 @@
     size, group_count = slopes.shape
     blocks = block_group.shape[0]
     covs, rows = lax.axis_size("cov"), lax.axis_size("rows")
-    share = blocks // covs
+    far = covs // NEAR
+    share = blocks // NEAR
+    near_groups = [[i * NEAR + j for j in range(NEAR)] for i in range(far)]
+    far_groups = [[i * NEAR + j for i in range(far)] for j in range(NEAR)]
     slope_rows = size * group_count // LANES
 
     from_lower = from_behind(slopes, "rows", 1)
@@ -196,7 +216,6 @@
             pltpu.VMEM((blocks // LANES, LANES), jnp.int32),
             pltpu.VMEM((share, LANES), jnp.int32),
             pltpu.VMEM((size, group_count), f32),
-            pltpu.VMEM((LANES, LANES), f32),
             pltpu.SemaphoreType.DMA((6,)),
         ],
         compiler_params=ROOM,
@@ -227,16 +246,25 @@
         name="predict",
     )(from_lower, from_upper, own_coefs, fixed_row, hot, design_here)
 
-    received = exchange(partial.reshape(covs, share, LANES), "cov")
+    received = exchange(partial.reshape(NEAR, share, LANES), "cov", near_groups)
+    spread = pl.pallas_call(
+        gather_kernel,
+        out_shape=shape(far, share + slope_rows, LANES),
+        in_specs=[VMEM] * 2,
+        out_specs=VMEM,
+        compiler_params=ROOM,
+        name="gather",
+    )(received, own_rows)
+    received = exchange(spread, "cov", far_groups)
     spread = pl.pallas_call(
         residual_kernel,
-        out_shape=shape(covs, share + slope_rows, LANES),
-        in_specs=[VMEM] * 4,
+        out_shape=shape(NEAR, share + far * slope_rows, LANES),
+        in_specs=[VMEM] * 3,
         out_specs=VMEM,
         compiler_params=ROOM,
         name="residual",
-    )(received, label, valid, own_rows)
-    back = exchange(spread, "cov")
+    )(received, label, valid)
+    back = exchange(spread, "cov", near_groups)
 
     fixed_parts, grads = pl.pallas_call(
         gradient_kernel,

time: 104 us -> 104 us (level)
  starting transfers between devices: 22.8 us -> 16.6 us
  blocking collectives: 71.9 us -> 77.4 us
    ppermute x4, starting transfers between devices: 22.8 us -> 16.6 us  [from_behind(): return lax.ppermute(shard, axis, pairs)]
    all_to_all x3 -> x4, blocking collectives: 71.9 us -> 77.4 us  [exchange(): lax.all_to_all(parts, axis, 0, 0, tiled=True, axis_index_groups=groups)]
where the time goes in v3:
time: 104 us
  blocking collectives  77.4 us (74%)
  starting transfers between devices  16.6 us (16%)
  Pallas kernels  8.69 us (8%)
    all_to_all x4, blocking collectives, exchange(): lax.all_to_all(parts, axis, 0, 0, tiled=True, axis_index_groups=groups)  77.4 us
    ppermute x4, starting transfers between devices, from_behind(): return lax.ppermute(shard, axis, pairs)  16.6 us
    pallas_call x1, Pallas kernels, body(): pl.pallas_call(predict_kernel, out_shape=shape(blocks, LANES), in_specs=[...  2.92 us
    pallas_call x1, Pallas kernels, body(): pl.pallas_call(gradient_kernel, out_shape=(shape(rows, LANES), shape(bloc...  2.34 us
    pallas_call x1, Pallas kernels, body(): pl.pallas_call(select_kernel, out_shape=(shape(3 * group_count, blocks, d...  2.29 us
  transfers between devices with their start and end apart: 4, of which 0 were waited for; matrix products, arithmetic and copies ran while one was open for 0% of the time, Pallas kernels for 2%

profile of v3, /device:TPU:1, one launch (start us, length us, event | category | flops | bytes accessed | tf_op | source)
XLA Modules:
  0.0 103.5 jit_solution(11398134197647047903)
XLA Ops:
  0.6 8.8 %collective-permute-start.1 = (f32[16,256]{1,0:T(8,128)}, f32[16,256]{1,0:T(8,128)S(1)}, u32[]{:S(2)}, u32[]{:S(2)}) collective-permute-start(f32[16,256]{1,0:T(8,128)} %slopes_hbm.1), channel_id=1, source_target_pairs={{16,0},{32,16},{48,32},{64,48},{80,64},{96,80},{112,96},{128,112},... | collective-permute-start | bytes 49160 | tf_op jit(solution)/shard_map/ppermute | solution.py:21
  9.4 1.9 %collective-permute-start = (f32[16,256]{1,0:T(8,128)}, f32[16,256]{1,0:T(8,128)S(1)}, u32[]{:S(2)}, u32[]{:S(2)}) collective-permute-start(f32[16,256]{1,0:T(8,128)} %slopes_hbm.1), channel_id=1, source_target_pairs={{0,16},{16,32},{32,48},{48,64},{64,80},{80,96},{96,112},{112,128},... | collective-permute-start | bytes 49160 | tf_op jit(solution)/shard_map/ppermute | solution.py:21
  11.4 0.1 pad_add_fusion.where_ref
  11.4 2.3 %select.1 = (bf16[768,512]{1,0:T(8,128)(2,1)S(1)}, f32[128,128]{1,0:T(8,128)S(1)}, f32[128,128]{1,0:T(8,128)S(1)}, f32[1,16]{1,0:T(1,128)S(1)}, f32[32,128]{1,0:...) custom-call(s32[2]{0:T(128)S(1)} %pad_add_fusion.where_ref, s32[1,512]{1,0:T(1,128)} %bitcast.14, ...), custom_call_target="tpu_custom_call" | custom-call | flops 10000000 | bytes 5000000 | tf_op jit(solution)/shard_map/select/pallas_call | solution.py:201
  13.7 0.0 collective-permute-done.1.upper_ref
  13.7 0.0 collective-permute-done.lower_ref
  13.8 2.9 %predict.1 = f32[512,128]{1,0:T(8,128)S(1)} custom-call(f32[16,256]{1,0:T(8,128)S(1)} %collective-permute-done.lower_ref, f32[16,256]{1,0:T(8,128)S(1)} %collective-permute-done.1.upper_ref, f32[16,512]{1,0:T(8,128)S(1)} %get-tuple-element.17.own_coef_ref, f32[1,16]{1,0:T(1,128)S(1)} %get-tuple-element.18.fixed_ref, ...), custom_call_target="tpu_custom_call" | custom-call | tf_op jit(solution)/shard_map/predict/pallas_call | solution.py:239
  16.7 9.5 %all_to_all.26.parts_ref = f32[4,128,128]{2,1,0:T(8,128)S(1)} all-to-all(f32[4,128,128]{2,1,0:T(8,128)S(1)} %bitcast.11), channel_id=1, replica_groups={{0,1,2,3},{4,5,6,7},{8,9,10,11},{12,13,14,15},{16,17,18,19},{20,21,22,2..., dimensions={0} | all-to-all | bytes 524288 | tf_op jit(solution)/shard_map/all_to_all | solution.py:25
  26.2 31.3 %all_to_all.27.parts_ref = f32[4,160,128]{2,1,0:T(8,128)S(1)} all-to-all(f32[4,160,128]{2,1,0:T(8,128)S(1)} %gather.1), channel_id=1, replica_groups={{0,4,8,12},{1,5,9,13},{2,6,10,14},{3,7,11,15},{16,20,24,28},{17,21,25,2..., dimensions={0} | all-to-all | bytes 655360 | tf_op jit(solution)/shard_map/all_to_all | solution.py:25
  57.6 0.0 copy-start
  57.6 19.2 %all_to_all.28.back_ref = f32[4,256,128]{2,1,0:T(8,128)S(1)} all-to-all(f32[4,256,128]{2,1,0:T(8,128)S(1)} %residual.1), channel_id=1, replica_groups={{0,1,2,3},{4,5,6,7},{8,9,10,11},{12,13,14,15},{16,17,18,19},{20,21,22,2..., dimensions={0} | all-to-all | bytes 1048576 | tf_op jit(solution)/shard_map/all_to_all | solution.py:25
  76.8 2.3 %gradient.1 = (f32[32,128]{1,0:T(8,128)S(1)}, f32[512,128]{1,0:T(8,128)S(1)}) custom-call(bf16[16,512,128]{2,1,0:T(8,128)(2,1)S(1)} %get-tuple-element.16.design_ref, f32[4,256,128]{2,1,0:T(8,128)S(1)} %all_to_all.28.back_ref), custom_call_target="tpu_custom_call" | custom-call | tf_op jit(solution)/shard_map/gradient/pallas_call | solution.py:269
  79.2 0.0 copy-done
  79.2 0.5 group.1
  79.7 4.0 %collective-permute-start.2 = (f32[16,256]{1,0:T(8,128)S(1)}, f32[16,256]{1,0:T(8,128)S(1)}, u32[]{:S(2)}, u32[]{:S(2)}) collective-permute-start(f32[16,256]{1,0:T(8,128)S(1)} %get-tuple-element.26), channel_id=1, source_target_pairs={{16,0},{32,16},{48,32},{64,48},{80,64},{96,80},{112,96},{128,112},... | collective-permute-start | bytes 49160 | tf_op jit(solution)/shard_map/ppermute | solution.py:21
  83.7 1.9 %collective-permute-start.3 = (f32[16,256]{1,0:T(8,128)S(1)}, f32[16,256]{1,0:T(8,128)S(1)}, u32[]{:S(2)}, u32[]{:S(2)}) collective-permute-start(f32[16,256]{1,0:T(8,128)S(1)} %get-tuple-element.27), channel_id=1, source_target_pairs={{0,16},{16,32},{32,48},{48,64},{64,80},{80,96},{96,112},{112,128},... | collective-permute-start | bytes 49160 | tf_op jit(solution)/shard_map/ppermute | solution.py:21
  85.6 17.3 %all_to_all.29 = f32[32,1,128]{2,1,0:T(1,128)S(1)} all-to-all(f32[32,1,128]{2,1,0:T(1,128)S(1)} %bitcast.13), channel_id=1, replica_groups=mesh['rows'=32,'cov'=16] {'rows'}, dimensions={0} | all-to-all | bytes 32768 | tf_op jit(solution)/shard_map/all_to_all | solution.py:25
  102.9 0.0 collective-permute-done.2.down_ref
  102.9 0.0 collective-permute-done.3.up_ref
  102.9 0.6 finish.1
  (2 shorter events, 0.1 us)
Async XLA Ops:
  0.6 13.1 %collective-permute-start.1 = (f32[16,256]{1,0:T(8,128)}, f32[16,256]{1,0:T(8,128)S(1)}, u32[]{:S(2)}, u32[]{:S(2)}) collective-permute-start(f32[16,256]{1,0:T(8,128)} %slopes_hbm.1), channel_id=1, source_target_pairs={{16,0},{32,16},{48,32},{64,48},{80,64},{96,80},{112,96},{128,112},... | collective-permute-start | bytes 49160 | tf_op jit(solution)/shard_map/ppermute | solution.py:21
  9.4 4.3 %collective-permute-start = (f32[16,256]{1,0:T(8,128)}, f32[16,256]{1,0:T(8,128)S(1)}, u32[]{:S(2)}, u32[]{:S(2)}) collective-permute-start(f32[16,256]{1,0:T(8,128)} %slopes_hbm.1), channel_id=1, source_target_pairs={{0,16},{16,32},{32,48},{48,64},{64,80},{80,96},{96,112},{112,128},... | collective-permute-start | bytes 49160 | tf_op jit(solution)/shard_map/ppermute | solution.py:21
  57.6 21.6 %copy-start = (f32[16,256]{1,0:T(8,128)S(1)}, f32[16,256]{1,0:T(8,128)}, u32[]{:S(2)}) copy-start(f32[16,256]{1,0:T(8,128)} %precision_ref.1) | copy-start | bytes 49156
  79.7 23.3 %collective-permute-start.2 = (f32[16,256]{1,0:T(8,128)S(1)}, f32[16,256]{1,0:T(8,128)S(1)}, u32[]{:S(2)}, u32[]{:S(2)}) collective-permute-start(f32[16,256]{1,0:T(8,128)S(1)} %get-tuple-element.26), channel_id=1, source_target_pairs={{16,0},{32,16},{48,32},{64,48},{80,64},{96,80},{112,96},{128,112},... | collective-permute-start | bytes 49160 | tf_op jit(solution)/shard_map/ppermute | solution.py:21
  83.7 19.3 %collective-permute-start.3 = (f32[16,256]{1,0:T(8,128)S(1)}, f32[16,256]{1,0:T(8,128)S(1)}, u32[]{:S(2)}, u32[]{:S(2)}) collective-permute-start(f32[16,256]{1,0:T(8,128)S(1)} %get-tuple-element.27), channel_id=1, source_target_pairs={{0,16},{16,32},{32,48},{48,64},{64,80},{80,96},{96,112},{112,128},... | collective-permute-start | bytes 49160 | tf_op jit(solution)/shard_map/ppermute | solution.py:21

commit v4 on v3

--- a/solution.py
+++ b/solution.py
@@ -42,10 +42,15 @@
     return x[:size] + x[size : 2 * size] + x[2 * size :]
 
 
+def in_rows(*arrays):
+    pieces = [x[:, at : at + LANES] for x in arrays for at in range(0, x.shape[1], LANES)]
+    return jnp.concatenate(pieces, axis=0)
+
+
 def select_kernel(
-    where_ref, group_hbm, fill_hbm, outcome_hbm, fixed_hbm, slopes_hbm, design_hbm,
-    hot_ref, label_ref, valid_ref, fixed_ref, slope_ref, coef_ref, design_ref,
-    group_ref, fill_ref, outcome_ref, own_ref, sems,
+    where_ref, group_hbm, fill_hbm, outcome_hbm, fixed_hbm, slopes_hbm, precision_hbm, design_hbm,
+    hot_ref, label_ref, valid_ref, fixed_ref, prior_ref, coef_ref, design_ref,
+    group_ref, fill_ref, outcome_ref, own_ref, precision_ref, sems,
 ):
     window, blocks = hot_ref.shape
     rows = label_ref.shape[0]
@@ -57,19 +62,19 @@
         pltpu.make_async_copy(fixed_hbm, fixed_ref, sems.at[2]),
         pltpu.make_async_copy(fill_hbm, fill_ref, sems.at[3]),
         pltpu.make_async_copy(outcome_hbm.at[pl.ds(start, rows)], outcome_ref, sems.at[4]),
-        pltpu.make_async_copy(design_hbm, design_ref, sems.at[5]),
+        pltpu.make_async_copy(precision_hbm, precision_ref, sems.at[5]),
+        pltpu.make_async_copy(design_hbm, design_ref, sems.at[6]),
     ]
     for copy in copies:
         copy.start()
-    for copy in copies[:5]:
+    for copy in copies[:6]:
         copy.wait()
     index = group_ref[...] - where_ref[0]
     for piece in range(0, window, groups):
         ids = lax.broadcasted_iota(jnp.int32, (groups, blocks), 0) + piece
         hot_ref[piece : piece + groups, :] = (ids == index).astype(f32).astype(bf16)
     own = own_ref[...]
-    for half in range(groups // LANES):
-        slope_ref[half * size : (half + 1) * size, :] = own[:, half * LANES : (half + 1) * LANES]
+    prior_ref[...] = in_rows(own, precision_ref[...])
     coef_ref[...] = add_parts(
         jnp.dot(three_parts(own), hot_ref[groups : 2 * groups, :], preferred_element_type=f32)
     )
@@ -78,12 +83,15 @@
     lane = lax.broadcasted_iota(jnp.int32, (rows, LANES), 1).astype(f32)
     valid_ref[...] = (lane < column).astype(f32)
     label_ref[...] = outcome_ref[...].astype(f32)
-    copies[5].wait()
-
-
-def predict_kernel(lower_ref, upper_ref, own_coef_ref, fixed_ref, hot_ref, design_ref, out_ref, coef_ref):
+    copies[6].wait()
+
+
+def predict_kernel(
+    lower_ref, upper_ref, own_coef_ref, fixed_ref, hot_ref, design_ref, prior_ref, out_ref, coef_ref
+):
     size, groups = lower_ref.shape
-    blocks = out_ref.shape[0]
+    blocks = hot_ref.shape[1]
+    share = blocks // NEAR
     coefs = own_coef_ref[...]
     coefs += add_parts(
         jnp.dot(three_parts(lower_ref[...]), hot_ref[:groups, :], preferred_element_type=f32)
@@ -94,36 +102,53 @@
     padded = jnp.concatenate([coefs, jnp.zeros((LANES - size, blocks), f32)], axis=0)
     coef_ref[...] = padded.T[:, :size] + fixed_ref[...]
     step = 32
-
-    def chunk(i, carry):
-        start = pl.multiple_of(i * step, step)
-        here = coef_ref[pl.ds(start, step), :]
-        total = jnp.zeros((step, LANES), f32)
-        for p in range(size):
-            total = total + here[:, p : p + 1] * design_ref[p, pl.ds(start, step), :].astype(f32)
-        out_ref[pl.ds(start, step), :] = total
-        return carry
-
-    lax.fori_loop(0, blocks // step, chunk, 0)
-
-
-def spread_rows(out_ref, *pieces):
-    at = 0
-    for piece in pieces:
-        size = piece.shape[0]
-        out_ref[:, at : at + size, :] = jnp.broadcast_to(piece[None], (out_ref.shape[0],) + piece.shape)
-        at += size
-
-
-def gather_kernel(parts_ref, slope_ref, out_ref):
-    spread_rows(out_ref, jnp.sum(parts_ref[...], axis=0), slope_ref[...])
-
-
-def residual_kernel(parts_ref, label_ref, valid_ref, out_ref):
+    for peer in range(NEAR):
+
+        def chunk(i, carry, peer=peer):
+            inner = pl.multiple_of(i * step, step)
+            start = pl.multiple_of(peer * share + i * step, step)
+            here = coef_ref[pl.ds(start, step), :]
+            total = jnp.zeros((step, LANES), f32)
+            for p in range(size):
+                total = total + here[:, p : p + 1] * design_ref[p, pl.ds(start, step), :].astype(f32)
+            out_ref[peer, pl.ds(inner, step), :] = total
+            return carry
+
+        lax.fori_loop(0, share // step, chunk, 0)
+        out_ref[peer, share:, :] = prior_ref[...]
+
+
+def gather_kernel(where_ref, parts_ref, out_ref, prior_ref):
+    size = prior_ref.shape[0] // (out_ref.shape[0] * NEAR)
+    rows = out_ref.shape[1] - size * (prior_ref.shape[1] // LANES)
+    total = jnp.sum(parts_ref[:, :rows, :], axis=0)
+    columns = [
+        parts_ref[:, at : at + size, :].reshape(-1, LANES)
+        for at in range(rows, parts_ref.shape[1], size)
+    ]
+    halves = prior_ref.shape[1] // LANES
+    slopes = jnp.concatenate(columns[:halves], axis=1)
+    precision = jnp.concatenate(columns[halves:], axis=1)
+    prior_ref[...] = lax.dot_general(
+        precision,
+        slopes,
+        (((0,), (0,)), ((), ())),
+        precision=lax.Precision.HIGHEST,
+        preferred_element_type=f32,
+    )
+    near = lax.rem(where_ref[1], NEAR)
+    for i in range(out_ref.shape[0]):
+        out_ref[i, :rows, :] = total
+        part = prior_ref[pl.ds(pl.multiple_of((i * NEAR + near) * size, size), size), :]
+        out_ref[i, rows:, :] = in_rows(part)
+
+
+def residual_kernel(parts_ref, label_ref, valid_ref, out_ref, prior_ref):
     rows = label_ref.shape[0]
     logits = jnp.sum(parts_ref[:, :rows, :], axis=0)
     residual = jnp.where(valid_ref[...] > 0.5, label_ref[...] - jax.nn.sigmoid(logits), 0.0)
-    spread_rows(out_ref, residual, *(parts_ref[i, rows:, :] for i in range(parts_ref.shape[0])))
+    out_ref[...] = jnp.broadcast_to(residual[None], out_ref.shape)
+    prior_ref[...] = jnp.sum(parts_ref[:, rows:, :], axis=0)
 
 
 def gradient_kernel(design_ref, back_ref, fixed_ref, grad_ref):
@@ -146,37 +171,24 @@
             return total + grads
 
         total = lax.fori_loop(0, share // step, chunk, total)
-    fixed_ref[...] = jnp.broadcast_to(jnp.sum(total, axis=0, keepdims=True), fixed_ref.shape)
-
-
-def group_kernel(grad_ref, hot_ref, back_ref, precision_ref, lower_ref, own_ref, upper_ref):
+    fixed_ref[...] = jnp.broadcast_to(jnp.sum(total, axis=0)[None, None], fixed_ref.shape)
+
+
+def group_kernel(grad_ref, hot_ref, prior_ref, lower_ref, own_ref, upper_ref):
     size, groups = own_ref.shape
-    halves = groups // LANES
-    far = precision_ref.shape[1] // (size * NEAR)
-    rows = back_ref.shape[1] - far * size * halves
     parts = three_parts(grad_ref[...].T[:size])
     sums = add_parts(
         lax.dot_general(parts, hot_ref[...], (((1,), (1,)), ((), ())), preferred_element_type=f32)
     )
     lower_ref[...] = sums[:, :groups]
     upper_ref[...] = sums[:, 2 * groups :]
-    slopes = []
-    for half in range(halves):
-        starts = [rows + (i * halves + half) * size for i in range(far)]
-        pieces = [back_ref[:, at : at + size, :].reshape(-1, LANES) for at in starts]
-        slopes.append(jnp.concatenate(pieces, axis=0))
-    prior = jnp.dot(
-        precision_ref[...],
-        jnp.concatenate(slopes, axis=1),
-        precision=lax.Precision.HIGHEST,
-        preferred_element_type=f32,
-    )
-    own_ref[...] = sums[:, groups : 2 * groups] - prior
+    halves = [prior_ref[at : at + size, :] for at in range(0, prior_ref.shape[0], size)]
+    own_ref[...] = sums[:, groups : 2 * groups] - jnp.concatenate(halves, axis=1)
 
 
 def finish_kernel(fixed_all_ref, fixed_ref, own_ref, down_ref, up_ref, fixed_out, slope_out):
     size = fixed_ref.shape[1]
-    fixed_out[...] = jnp.sum(fixed_all_ref[...], axis=0, keepdims=True)[:, :size] - fixed_ref[...]
+    fixed_out[...] = jnp.sum(fixed_all_ref[...], axis=0)[:1, :size] - fixed_ref[...]
     slope_out[...] = own_ref[...] + down_ref[...] + up_ref[...]
 
 
@@ -193,30 +205,32 @@
     near_groups = [[i * NEAR + j for j in range(NEAR)] for i in range(far)]
     far_groups = [[i * NEAR + j for i in range(far)] for j in range(NEAR)]
     slope_rows = size * group_count // LANES
+    precision_rows = size * size * covs // LANES
 
     from_lower = from_behind(slopes, "rows", 1)
     from_upper = from_behind(slopes, "rows", -1)
 
     where = jnp.stack([(lax.axis_index("rows") - 1) * group_count, lax.axis_index("cov")])
-    hot, label, valid, fixed_row, own_rows, own_coefs, design_here = pl.pallas_call(
+    hot, label, valid, fixed_row, prior_rows, own_coefs, design_here = pl.pallas_call(
         select_kernel,
         out_shape=(
             shape(3 * group_count, blocks, dtype=bf16),
             shape(share, LANES),
             shape(share, LANES),
             shape(1, size),
-            shape(slope_rows, LANES),
+            shape(slope_rows + precision_rows, LANES),
             shape(size, blocks),
             shape(*design.shape, dtype=bf16),
         ),
-        in_specs=[SMEM] + [HBM] * 6,
+        in_specs=[SMEM] + [HBM] * 7,
         out_specs=(VMEM,) * 7,
         scratch_shapes=[
             pltpu.VMEM((1, blocks), jnp.int32),
             pltpu.VMEM((blocks // LANES, LANES), jnp.int32),
             pltpu.VMEM((share, LANES), jnp.int32),
             pltpu.VMEM((size, group_count), f32),
-            pltpu.SemaphoreType.DMA((6,)),
+            pltpu.VMEM((size, covs * size), f32),
+            pltpu.SemaphoreType.DMA((7,)),
         ],
         compiler_params=ROOM,
         cost_estimate=cost(10_000_000, 5_000_000),
@@ -231,6 +245,7 @@
                 outcome,
                 fixed_coef.reshape(1, size),
                 slopes,
+                precision,
                 design,
             )
         ),
@@ -238,29 +253,30 @@
 
     partial = pl.pallas_call(
         predict_kernel,
-        out_shape=shape(blocks, LANES),
-        in_specs=[VMEM] * 6,
+        out_shape=shape(NEAR, share + slope_rows + precision_rows, LANES),
+        in_specs=[VMEM] * 7,
         out_specs=VMEM,
         scratch_shapes=[pltpu.VMEM((blocks, size), f32)],
         compiler_params=ROOM,
         name="predict",
-    )(from_lower, from_upper, own_coefs, fixed_row, hot, design_here)
-
-    received = exchange(partial.reshape(NEAR, share, LANES), "cov", near_groups)
+    )(from_lower, from_upper, own_coefs, fixed_row, hot, design_here, prior_rows)
+
+    received = exchange(partial, "cov", near_groups)
     spread = pl.pallas_call(
         gather_kernel,
         out_shape=shape(far, share + slope_rows, LANES),
-        in_specs=[VMEM] * 2,
+        in_specs=[SMEM, VMEM],
         out_specs=VMEM,
+        scratch_shapes=[pltpu.VMEM((covs * size, group_count), f32)],
         compiler_params=ROOM,
         name="gather",
-    )(received, own_rows)
+    )(where, received)
     received = exchange(spread, "cov", far_groups)
-    spread = pl.pallas_call(
+    spread, prior = pl.pallas_call(
         residual_kernel,
-        out_shape=shape(NEAR, share + far * slope_rows, LANES),
+        out_shape=(shape(NEAR, share, LANES), shape(slope_rows, LANES)),
         in_specs=[VMEM] * 3,
-        out_specs=VMEM,
+        out_specs=(VMEM, VMEM),
         compiler_params=ROOM,
         name="residual",
     )(received, label, valid)
@@ -268,7 +284,7 @@
 
     fixed_parts, grads = pl.pallas_call(
         gradient_kernel,
-        out_shape=(shape(rows, LANES), shape(blocks, LANES)),
+        out_shape=(shape(rows, 2, LANES), shape(blocks, LANES)),
         in_specs=[VMEM] * 2,
         out_specs=(VMEM,) * 2,
         compiler_params=ROOM,
@@ -279,12 +295,12 @@
     to_lower, own, to_upper = pl.pallas_call(
         group_kernel,
         out_shape=(shape(size, group_count),) * 3,
-        in_specs=[VMEM] * 4,
+        in_specs=[VMEM] * 3,
         out_specs=(VMEM,) * 3,
         compiler_params=ROOM,
         cost_estimate=cost(100_000_000, 5_000_000),
         name="group",
-    )(grads, hot, back, precision)
+    )(grads, hot, prior)
     given_down = from_behind(to_lower, "rows", -1)
     given_up = from_behind(to_upper, "rows", 1)
 

time: 104 us -> 101 us (0.971)
  the two profiles are of different devices: /device:TPU:1 before, /device:TPU:24 now
where the time goes in v4:
time: 101 us; the launch traced here: 100 us
  blocking collectives  55.1 us (55%)
  starting transfers between devices  26 us (26%)
  Pallas kernels  10.1 us (10%)
  waiting for transfers between devices  8.27 us (8%)
    all_to_all x3, blocking collectives, exchange(): lax.all_to_all(parts, axis, 0, 0, tiled=True, axis_index_groups=groups)  55.1 us
    all_to_all x1, starting transfers between devices, exchange(): lax.all_to_all(parts, axis, 0, 0, tiled=True, axis_index_groups=groups)  13.2 us
    ppermute x4, starting transfers between devices, from_behind(): return lax.ppermute(shard, axis, pairs)  12.8 us
    ppermute x4, waiting for transfers between devices, from_behind(): return lax.ppermute(shard, axis, pairs)  8.27 us
    pallas_call x1, Pallas kernels, body(): pl.pallas_call(gradient_kernel, out_shape=(shape(rows, 2, LANES), shape(b...  2.97 us
    pallas_call x1, Pallas kernels, body(): pl.pallas_call(predict_kernel, out_shape=shape(NEAR, share + slope_rows +...  2.9 us
    pallas_call x1, Pallas kernels, body(): pl.pallas_call(select_kernel, out_shape=(shape(3 * group_count, blocks, d...  2.31 us
  transfers between devices with their start and end apart: 5, of which 2 were waited for; matrix products, arithmetic and copies ran while one was open for 0% of the time, Pallas kernels for 3%

profile of v4, /device:TPU:24, one launch (start us, length us, event | category | flops | bytes accessed | tf_op | source)
XLA Modules:
  0.0 100.3 jit_solution(2184290771130748597)
XLA Ops:
  0.6 4.3 %collective-permute-start.1 = (f32[16,256]{1,0:T(8,128)}, f32[16,256]{1,0:T(8,128)S(1)}, u32[]{:S(2)}, u32[]{:S(2)}) collective-permute-start(f32[16,256]{1,0:T(8,128)} %slopes_hbm.1), channel_id=1, source_target_pairs={{16,0},{32,16},{48,32},{64,48},{80,64},{96,80},{112,96},{128,112},... | collective-permute-start | bytes 49160 | tf_op jit(solution)/shard_map/ppermute | solution.py:21
  4.9 1.9 %collective-permute-start = (f32[16,256]{1,0:T(8,128)}, f32[16,256]{1,0:T(8,128)S(1)}, u32[]{:S(2)}, u32[]{:S(2)}) collective-permute-start(f32[16,256]{1,0:T(8,128)} %slopes_hbm.1), channel_id=1, source_target_pairs={{0,16},{16,32},{32,48},{48,64},{64,80},{80,96},{96,112},{112,128},... | collective-permute-start | bytes 49160 | tf_op jit(solution)/shard_map/ppermute | solution.py:21
  6.9 0.1 pad_add_fusion.where_ref
  6.9 2.3 %select.1 = (bf16[768,512]{1,0:T(8,128)(2,1)S(1)}, f32[128,128]{1,0:T(8,128)S(1)}, f32[128,128]{1,0:T(8,128)S(1)}, f32[1,16]{1,0:T(1,128)S(1)}, f32[64,128]{1,0:...) custom-call(s32[2]{0:T(128)S(1)} %pad_add_fusion.where_ref, s32[1,512]{1,0:T(1,128)} %bitcast.6, ...), custom_call_target="tpu_custom_call" | custom-call | flops 10000000 | bytes 5000000 | tf_op jit(solution)/shard_map/select/pallas_call | solution.py:214
  9.3 0.0 collective-permute-done.1.upper_ref
  9.3 3.0 %collective-permute-done.lower_ref = f32[16,256]{1,0:T(8,128)S(1)} collective-permute-done((f32[16,256]{1,0:T(8,128)}, f32[16,256]{1,0:T(8,128)S(1)}, u32[]{:S(2)}, u32[]{:S(2)}) %collective-permute-start) | collective-permute-done | bytes 16416 | tf_op jit(solution)/shard_map/ppermute | solution.py:21
  12.3 2.9 %predict.1 = f32[4,192,128]{2,1,0:T(8,128)S(1)} custom-call(f32[16,256]{1,0:T(8,128)S(1)} %collective-permute-done.lower_ref, f32[16,256]{1,0:T(8,128)S(1)} %collective-permute-done.1.upper_ref, f32[16,512]{1,0:T(8,128)S(1)} %get-tuple-element.19.own_coef_ref, f32[1,16]{1,0:T(1,128)S(1)} %get-tuple-element.20.fixed_ref, ...), custom_call_target="tpu_custom_call" | custom-call | tf_op jit(solution)/shard_map/predict/pallas_call | solution.py:254
  15.2 14.6 %all_to_all.20.parts_ref = f32[4,192,128]{2,1,0:T(8,128)S(1)} all-to-all(f32[4,192,128]{2,1,0:T(8,128)S(1)} %predict.1), channel_id=1, replica_groups={{0,1,2,3},{4,5,6,7},{8,9,10,11},{12,13,14,15},{16,17,18,19},{20,21,22,2..., dimensions={0} | all-to-all | bytes 786432 | tf_op jit(solution)/shard_map/all_to_all | solution.py:25
  29.8 1.0 gather.1
  30.8 30.3 %all_to_all.21.parts_ref = f32[4,160,128]{2,1,0:T(8,128)S(1)} all-to-all(f32[4,160,128]{2,1,0:T(8,128)S(1)} %gather.1), channel_id=1, replica_groups={{0,4,8,12},{1,5,9,13},{2,6,10,14},{3,7,11,15},{16,20,24,28},{17,21,25,2..., dimensions={0} | all-to-all | bytes 655360 | tf_op jit(solution)/shard_map/all_to_all | solution.py:25
  61.1 10.3 %all_to_all.22.back_ref = f32[4,128,128]{2,1,0:T(8,128)S(1)} all-to-all(f32[4,128,128]{2,1,0:T(8,128)S(1)} %get-tuple-element.25), channel_id=1, replica_groups={{0,1,2,3},{4,5,6,7},{8,9,10,11},{12,13,14,15},{16,17,18,19},{20,21,22,2..., dimensions={0} | all-to-all | bytes 524288 | tf_op jit(solution)/shard_map/all_to_all | solution.py:25
  71.4 3.0 %gradient.1 = (f32[32,2,128]{2,1,0:T(2,128)}, f32[512,128]{1,0:T(8,128)S(1)}) custom-call(bf16[16,512,128]{2,1,0:T(8,128)(2,1)S(1)} %get-tuple-element.18.design_ref, f32[4,128,128]{2,1,0:T(8,128)S(1)} %all_to_all.22.back_ref), custom_call_target="tpu_custom_call" | custom-call | tf_op jit(solution)/shard_map/gradient/pallas_call | solution.py:285
  74.3 13.2 %all-to-all-start.3 = ((f32[32,2,128]{2,1,0:T(2,128)}), f32[32,2,128]{2,1,0:T(2,128)S(1)}, u32[]{:S(2)}, u32[]{:S(2)}) async-start(f32[32,2,128]{2,1,0:T(2,128)} %get-tuple-element.26), calls=%async_computation.3 | async-start | bytes 65536 | tf_op jit(solution)/shard_map/all_to_all | solution.py:25
  87.6 0.3 group.1
  87.9 4.6 %collective-permute-start.2 = (f32[16,256]{1,0:T(8,128)S(1)}, f32[16,256]{1,0:T(8,128)S(1)}, u32[]{:S(2)}, u32[]{:S(2)}) collective-permute-start(f32[16,256]{1,0:T(8,128)S(1)} %get-tuple-element.30), channel_id=1, source_target_pairs={{16,0},{32,16},{48,32},{64,48},{80,64},{96,80},{112,96},{128,112},... | collective-permute-start | bytes 49160 | tf_op jit(solution)/shard_map/ppermute | solution.py:21
  92.5 1.9 %collective-permute-start.3 = (f32[16,256]{1,0:T(8,128)S(1)}, f32[16,256]{1,0:T(8,128)S(1)}, u32[]{:S(2)}, u32[]{:S(2)}) collective-permute-start(f32[16,256]{1,0:T(8,128)S(1)} %get-tuple-element.31), channel_id=1, source_target_pairs={{0,16},{16,32},{32,48},{48,64},{64,80},{80,96},{96,112},{112,128},... | collective-permute-start | bytes 49160 | tf_op jit(solution)/shard_map/ppermute | solution.py:21
  94.5 0.0 collective-permute-done.2.down_ref
  94.5 5.2 %collective-permute-done.3.up_ref = f32[16,256]{1,0:T(8,128)S(1)} collective-permute-done((f32[16,256]{1,0:T(8,128)S(1)}, f32[16,256]{1,0:T(8,128)S(1)}, u32[]{:S(2)}, u32[]{:S(2)}) %collective-permute-start.3) | collective-permute-done | bytes 16416 | tf_op jit(solution)/shard_map/ppermute | solution.py:21
  99.7 0.0 all-to-all-done.3.fixed_all_ref
  99.7 0.6 finish.1
  (1 shorter events, 0.0 us)
Async XLA Ops:
  0.6 8.6 %collective-permute-start.1 = (f32[16,256]{1,0:T(8,128)}, f32[16,256]{1,0:T(8,128)S(1)}, u32[]{:S(2)}, u32[]{:S(2)}) collective-permute-start(f32[16,256]{1,0:T(8,128)} %slopes_hbm.1), channel_id=1, source_target_pairs={{16,0},{32,16},{48,32},{64,48},{80,64},{96,80},{112,96},{128,112},... | collective-permute-start | bytes 49160 | tf_op jit(solution)/shard_map/ppermute | solution.py:21
  4.9 7.4 %collective-permute-start = (f32[16,256]{1,0:T(8,128)}, f32[16,256]{1,0:T(8,128)S(1)}, u32[]{:S(2)}, u32[]{:S(2)}) collective-permute-start(f32[16,256]{1,0:T(8,128)} %slopes_hbm.1), channel_id=1, source_target_pairs={{0,16},{16,32},{32,48},{48,64},{64,80},{80,96},{96,112},{112,128},... | collective-permute-start | bytes 49160 | tf_op jit(solution)/shard_map/ppermute | solution.py:21
  74.3 25.4 %all-to-all-start.3 = ((f32[32,2,128]{2,1,0:T(2,128)}), f32[32,2,128]{2,1,0:T(2,128)S(1)}, u32[]{:S(2)}, u32[]{:S(2)}) async-start(f32[32,2,128]{2,1,0:T(2,128)} %get-tuple-element.26), calls=%async_computation.3 | async-start | bytes 65536 | tf_op jit(solution)/shard_map/all_to_all | solution.py:25
  87.9 6.6 %collective-permute-start.2 = (f32[16,256]{1,0:T(8,128)S(1)}, f32[16,256]{1,0:T(8,128)S(1)}, u32[]{:S(2)}, u32[]{:S(2)}) collective-permute-start(f32[16,256]{1,0:T(8,128)S(1)} %get-tuple-element.30), channel_id=1, source_target_pairs={{16,0},{32,16},{48,32},{64,48},{80,64},{96,80},{112,96},{128,112},... | collective-permute-start | bytes 49160 | tf_op jit(solution)/shard_map/ppermute | solution.py:21
  92.5 7.2 %collective-permute-start.3 = (f32[16,256]{1,0:T(8,128)S(1)}, f32[16,256]{1,0:T(8,128)S(1)}, u32[]{:S(2)}, u32[]{:S(2)}) collective-permute-start(f32[16,256]{1,0:T(8,128)S(1)} %get-tuple-element.31), channel_id=1, source_target_pairs={{0,16},{16,32},{32,48},{48,64},{64,80},{80,96},{96,112},{112,128},... | collective-permute-start | bytes 49160 | tf_op jit(solution)/shard_map/ppermute | solution.py:21

commit v5 on v4

v5 whole, which is shorter than its diff:
```python
import jax
import jax.numpy as jnp
from jax import lax
from jax.experimental import pallas as pl
from jax.experimental.pallas import tpu as pltpu
from jax.sharding import PartitionSpec as P

f32 = jnp.float32
bf16 = jnp.bfloat16
VMEM = pl.BlockSpec(memory_space=pltpu.VMEM)
HBM = pl.BlockSpec(memory_space=pltpu.HBM)
LANES = 128
NEAR = 4
ROOM = pltpu.CompilerParams(vmem_limit_bytes=16 << 20)


def swap(shard, axis, first):
    peers = lax.axis_size(axis)
    pairs = [(i, i + 1) for i in range(first, peers - 1, 2)]
    return lax.ppermute(shard, axis, pairs + [(j, i) for i, j in pairs])


def exchange(parts, axis, groups=None):
    return lax.all_to_all(parts, axis, 0, 0, tiled=True, axis_index_groups=groups)


def cost(flops, size):
    return pl.CostEstimate(flops=flops, bytes_accessed=size, transcendentals=0)


def three_parts(x):
    a = x.astype(bf16)
    rest = x - a.astype(f32)
    b = rest.astype(bf16)
    c = (rest - b.astype(f32)).astype(bf16)
    return jnp.concatenate([a, b, c], axis=0)


def add_parts(x):
    size = x.shape[0] // 3
    return x[:size] + x[size : 2 * size] + x[2 * size :]


def in_rows(x):
    return jnp.concatenate([x[:, at : at + LANES] for at in range(0, x.shape[1], LANES)], axis=0)


def select_kernel(
    group_hbm, fill_hbm, outcome_hbm, fixed_hbm, slopes_hbm, precision_hbm, design_hbm,
    hot_ref, label_ref, valid_ref, fixed_ref, prior_ref, coef_ref, design_ref,
    group_ref, fill_ref, outcome_ref, own_ref, precision_ref, sems,
):
    window, blocks = hot_ref.shape
    rows = label_ref.shape[0]
    size, groups = own_ref.shape
    near = lax.rem(lax.axis_index("cov"), NEAR)
    start = pl.multiple_of(near * rows, rows)
    copies = [
        pltpu.make_async_copy(group_hbm, group_ref, sems.at[0]),
        pltpu.make_async_copy(slopes_hbm, own_ref, sems.at[1]),
        pltpu.make_async_copy(precision_hbm, precision_ref, sems.at[2]),
        pltpu.make_async_copy(outcome_hbm.at[pl.ds(start, rows)], outcome_ref, sems.at[3]),
        pltpu.make_async_copy(fill_hbm, fill_ref, sems.at[4]),
        pltpu.make_async_copy(fixed_hbm, fixed_ref, sems.at[5]),
        pltpu.make_async_copy(design_hbm, design_ref, sems.at[6]),
    ]
    for copy in copies:
        copy.start()
    for copy in copies[:2]:
        copy.wait()
    index = group_ref[...] - (lax.axis_index("rows") - 1) * groups
    for piece in range(0, window, groups):
        ids = lax.broadcasted_iota(jnp.int32, (groups, blocks), 0) + piece
        hot_ref[piece : piece + groups, :] = (ids == index).astype(f32).astype(bf16)
    own = own_ref[...]
    coef_ref[...] = add_parts(
        jnp.dot(three_parts(own), hot_ref[groups : 2 * groups, :], preferred_element_type=f32)
    )
    for copy in copies[2:6]:
        copy.wait()
    slope_rows = in_rows(own)
    precision = precision_ref[...]
    place = lax.rem(lax.broadcasted_iota(jnp.int32, (size, LANES), 1) // size, NEAR)
    for peer in range(NEAR):
        kept = [
            jnp.where(place == peer, precision[:, at : at + LANES], 0.0)
            for at in range(0, precision.shape[1], LANES)
        ]
        prior_ref[peer, : slope_rows.shape[0], :] = slope_rows
        prior_ref[peer, slope_rows.shape[0] :, :] = kept[0] + pltpu.roll(kept[1], size, 1)
    fill = fill_ref[pl.ds(near, 1), :].astype(f32)
    column = jnp.broadcast_to(fill, (rows, rows)).T
    lane = lax.broadcasted_iota(jnp.int32, (rows, LANES), 1).astype(f32)
    valid_ref[...] = (lane < column).astype(f32)
    label_ref[...] = outcome_ref[...].astype(f32)
    copies[6].wait()


def predict_kernel(
    even_ref, odd_ref, own_coef_ref, fixed_ref, hot_ref, design_ref, prior_ref, out_ref, coef_ref
):
    size, groups = even_ref.shape
    blocks = hot_ref.shape[1]
    share = blocks // NEAR
    parity = lax.rem(lax.axis_index("rows"), 2)
    coefs = own_coef_ref[...]
    for ref, place in ((even_ref, 1 - parity), (odd_ref, parity)):
        piece = hot_ref[pl.ds(pl.multiple_of(place * 2 * groups, groups), groups), :]
        coefs += add_parts(jnp.dot(three_parts(ref[...]), piece, preferred_element_type=f32))
    padded = jnp.concatenate([coefs, jnp.zeros((LANES - size, blocks), f32)], axis=0)
    coef_ref[...] = padded.T[:, :size] + fixed_ref[...]

    def chunk(peer, carry):
        start = pl.multiple_of(peer * share, share)
        here = coef_ref[pl.ds(start, share), :]
        total = jnp.zeros((share, LANES), f32)
        for p in range(size):
            total = total + here[:, p : p + 1] * design_ref[p, pl.ds(start, share), :].astype(f32)
        out_ref[peer, :share, :] = total
        out_ref[peer, share:, :] = prior_ref[peer]
        return carry

    lax.fori_loop(0, NEAR, chunk, 0)


def gather_kernel(parts_ref, out_ref, prior_ref):
    groups = prior_ref.shape[1]
    halves = groups // LANES
    size = (parts_ref.shape[1] - out_ref.shape[1])
    rows = out_ref.shape[1] - size * halves
    far = out_ref.shape[0]
    total = jnp.sum(parts_ref[:, :rows, :], axis=0)
    columns = [
        parts_ref[:, at : at + size, :].reshape(-1, LANES)
        for at in range(rows, parts_ref.shape[1], size)
    ]
    prior_ref[...] = lax.dot_general(
        columns[halves],
        jnp.concatenate(columns[:halves], axis=1),
        (((0,), (0,)), ((), ())),
        precision=lax.Precision.HIGHEST,
        preferred_element_type=f32,
    )
    near = lax.rem(lax.axis_index("cov"), NEAR)
    pieces = LANES // size
    for i in range(far):
        place = lax.rem(near + i % 2 * NEAR + i // 2, pieces)
        out_ref[i, :rows, :] = total
        part = prior_ref[pl.ds(pl.multiple_of(place * size, size), size), :]
        out_ref[i, rows:, :] = in_rows(part)


def residual_kernel(parts_ref, label_ref, valid_ref, out_ref, prior_ref):
    rows = label_ref.shape[0]
    logits = jnp.sum(parts_ref[:, :rows, :], axis=0)
    residual = jnp.where(valid_ref[...] > 0.5, label_ref[...] - jax.nn.sigmoid(logits), 0.0)
    out_ref[...] = jnp.broadcast_to(residual[None], out_ref.shape)
    prior_ref[...] = jnp.sum(parts_ref[:, rows:, :], axis=0)


def gradient_kernel(design_ref, back_ref, fixed_ref, grad_ref):
    size, blocks, _ = design_ref.shape
    share = blocks // NEAR
    lane = lax.broadcasted_iota(jnp.int32, (share, LANES), 1)

    def chunk(peer, total):
        start = pl.multiple_of(peer * share, share)
        residual = back_ref[peer]
        grads = jnp.zeros((share, LANES), f32)
        for p in range(size):
            product = design_ref[p, pl.ds(start, share), :].astype(f32) * residual
            grads = jnp.where(lane == p, jnp.sum(product, axis=1, keepdims=True), grads)
        grad_ref[pl.ds(start, share), :] = grads
        return total + jnp.sum(grads, axis=0, keepdims=True)

    total = lax.fori_loop(0, NEAR, chunk, jnp.zeros((1, LANES), f32))
    fixed_ref[...] = jnp.broadcast_to(total[None], fixed_ref.shape)


def group_kernel(grad_ref, hot_ref, prior_ref, even_ref, odd_ref, own_ref):
    size, groups = own_ref.shape
    parts = three_parts(grad_ref[...].T[:size])
    sums = add_parts(
        lax.dot_general(parts, hot_ref[...], (((1,), (1,)), ((), ())), preferred_element_type=f32)
    )
    lower, upper = sums[:, :groups], sums[:, 2 * groups :]
    odd = lax.rem(lax.axis_index("rows"), 2) == 1
    even_ref[...] = jnp.where(odd, lower, upper)
    odd_ref[...] = jnp.where(odd, upper, lower)
    halves = [prior_ref[at : at + size, :] for at in range(0, prior_ref.shape[0], size)]
    own_ref[...] = sums[:, groups : 2 * groups] - jnp.concatenate(halves, axis=1)


def finish_kernel(fixed_all_ref, fixed_ref, own_ref, even_ref, odd_ref, fixed_out, slope_out):
    size = fixed_ref.shape[1]
    fixed_out[...] = jnp.sum(fixed_all_ref[...], axis=0)[:1, :size] - fixed_ref[...]
    slope_out[...] = own_ref[...] + even_ref[...] + odd_ref[...]


def shape(*dims, dtype=f32):
    return jax.ShapeDtypeStruct(dims, dtype)


def body(design, outcome, block_fill, block_group, fixed_coef, slopes, precision):
    size, group_count = slopes.shape
    blocks = block_group.shape[0]
    covs, rows = lax.axis_size("cov"), lax.axis_size("rows")
    far = covs // NEAR
    share = blocks // NEAR
    near_groups = [[i * NEAR + j for j in range(NEAR)] for i in range(far)]
    far_groups = [[i * NEAR + j for i in range(far)] for j in range(NEAR)]
    slope_rows = size * group_count // LANES

    from_even = swap(slopes, "rows", 0)
    from_odd = swap(slopes, "rows", 1)

    hot, label, valid, fixed_row, prior_rows, own_coefs, design_here = pl.pallas_call(
        select_kernel,
        out_shape=(
            shape(3 * group_count, blocks, dtype=bf16),
            shape(share, LANES),
            shape(share, LANES),
            shape(1, size),
            shape(NEAR, slope_rows + size, LANES),
            shape(size, blocks),
            shape(*design.shape, dtype=bf16),
        ),
        in_specs=[HBM] * 7,
        out_specs=(VMEM,) * 7,
        scratch_shapes=[
            pltpu.VMEM((1, blocks), jnp.int32),
            pltpu.VMEM((blocks // LANES, LANES), jnp.int32),
            pltpu.VMEM((share, LANES), jnp.int32),
            pltpu.VMEM((size, group_count), f32),
            pltpu.VMEM((size, covs * size), f32),
            pltpu.SemaphoreType.DMA((7,)),
        ],
        compiler_params=ROOM,
        cost_estimate=cost(10_000_000, 5_000_000),
        name="select",
    )(
        *(
            pltpu.with_memory_space_constraint(x, pltpu.HBM)
            for x in (
                block_group.reshape(1, blocks),
                block_fill.reshape(blocks // LANES, LANES),
                outcome,
                fixed_coef.reshape(1, size),
                slopes,
                precision,
                design,
            )
        ),
    )

    partial = pl.pallas_call(
        predict_kernel,
        out_shape=shape(NEAR, share + slope_rows + size, LANES),
        in_specs=[VMEM] * 7,
        out_specs=VMEM,
        scratch_shapes=[pltpu.VMEM((blocks, size), f32)],
        compiler_params=ROOM,
        name="predict",
    )(from_even, from_odd, own_coefs, fixed_row, hot, design_here, prior_rows)

    received = exchange(partial, "cov", near_groups)
    spread = pl.pallas_call(
        gather_kernel,
        out_shape=shape(far, share + slope_rows, LANES),
        in_specs=[VMEM],
        out_specs=VMEM,
        scratch_shapes=[pltpu.VMEM((LANES, group_count), f32)],
        compiler_params=ROOM,
        name="gather",
    )(received)
    received = exchange(spread, "cov", far_groups)
    spread, prior = pl.pallas_call(
        residual_kernel,
        out_shape=(shape(NEAR, share, LANES), shape(slope_rows, LANES)),
        in_specs=[VMEM] * 3,
        out_specs=(VMEM, VMEM),
        compiler_params=ROOM,
        name="residual",
    )(received, label, valid)
    back = exchange(spread, "cov", near_groups)

    fixed_parts, grads = pl.pallas_call(
        gradient_kernel,
        out_shape=(shape(rows, 2, LANES), shape(blocks, LANES)),
        in_specs=[VMEM] * 2,
        out_specs=(VMEM,) * 2,
        compiler_params=ROOM,
        name="gradient",
    )(design_here, back)
    fixed_all = exchange(fixed_parts, "rows")

    to_even, to_odd, own = pl.pallas_call(
        group_kernel,
        out_shape=(shape(size, group_count),) * 3,
        in_specs=[VMEM] * 3,
        out_specs=(VMEM,) * 3,
        compiler_params=ROOM,
        cost_estimate=cost(100_000_000, 5_000_000),
        name="group",
    )(grads, hot, prior)
    given_even = swap(to_even, "rows", 0)
    given_odd = swap(to_odd, "rows", 1)

    fixed_grad, slope_grad = pl.pallas_call(
        finish_kernel,
        out_shape=(shape(1, size), shape(size, group_count)),
        in_specs=[VMEM] * 5,
        out_specs=(VMEM, VMEM),
        compiler_params=ROOM,
        name="finish",
    )(fixed_all, fixed_row, own, given_even, given_odd)
    return (fixed_grad.reshape(size), slope_grad)


def solution(mesh):
    return jax.shard_map(
        body,
        mesh=mesh,
        in_specs=(
            P("cov", "rows", None),
            P("rows", None),
            P("rows"),
            P("rows"),
            P("cov"),
            P("cov", "rows"),
            P("cov", None),
        ),
        out_specs=(P("cov"), P("cov", "rows")),
        check_vma=False,
    )
```

time: 101 us -> 92.4 us (0.915)
  blocking collectives: 55.1 us -> 62.3 us
  starting transfers between devices: 26 us -> 18.9 us
  waiting for transfers between devices: 8.27 us -> 2.33 us
  Pallas kernels: 10.1 us -> 7.02 us
    all_to_all x1, starting transfers between devices: 13.2 us -> 5.76 us  [exchange(): lax.all_to_all(parts, axis, 0, 0, tiled=True, axis_index_groups=groups)]
    all_to_all x3, blocking collectives: 55.1 us -> 62.3 us  [exchange(): lax.all_to_all(parts, axis, 0, 0, tiled=True, axis_index_groups=groups)]
    ppermute x4, waiting for transfers between devices: 8.27 us -> 2.33 us  [swap(): return lax.ppermute(shard, axis, pairs + [(j, i) for i, j in pairs])]
    pallas_call x1, Pallas kernels: 2.9 us -> 1.88 us  [body(): pl.pallas_call(predict_kernel, out_shape=shape(NEAR, share + slope_rows +...]
  transfers between devices with their start and end apart: 5 -> 5, of which waited for: 2 -> 1; matrix products, arithmetic and copies ran while one was open for 0% -> 0% of each run, Pallas kernels for 3% -> 2%
where the time goes in v5:
time: 92.4 us; the launch traced here: 91.3 us
  blocking collectives  62.3 us (67%)
  starting transfers between devices  18.9 us (20%)
  Pallas kernels  7.02 us (8%)
  waiting for transfers between devices  2.33 us (3%)
    all_to_all x3, blocking collectives, exchange(): lax.all_to_all(parts, axis, 0, 0, tiled=True, axis_index_groups=groups)  62.3 us
    ppermute x4, starting transfers between devices, swap(): return lax.ppermute(shard, axis, pairs + [(j, i) for i, j in pairs])  13.1 us
    all_to_all x1, starting transfers between devices, exchange(): lax.all_to_all(parts, axis, 0, 0, tiled=True, axis_index_groups=groups)  5.76 us
    ppermute x4, waiting for transfers between devices, swap(): return lax.ppermute(shard, axis, pairs + [(j, i) for i, j in pairs])  2.33 us
    pallas_call x1, Pallas kernels, body(): pl.pallas_call(gradient_kernel, out_shape=(shape(rows, 2, LANES), shape(b...  2.06 us
    pallas_call x1, Pallas kernels, body(): pl.pallas_call(predict_kernel, out_shape=shape(NEAR, share + slope_rows +...  1.88 us
  transfers between devices with their start and end apart: 5, of which 1 were waited for; matrix products, arithmetic and copies ran while one was open for 0% of the time, Pallas kernels for 2%

profile of v5, /device:TPU:24, one launch (start us, length us, event | category | flops | bytes accessed | tf_op | source)
XLA Modules:
  0.0 91.3 jit_solution(9849442120013736894)
XLA Ops:
  0.6 4.3 %collective-permute-start.1 = (f32[16,256]{1,0:T(8,128)}, f32[16,256]{1,0:T(8,128)S(1)}, u32[]{:S(2)}, u32[]{:S(2)}) collective-permute-start(f32[16,256]{1,0:T(8,128)} %slopes_hbm.1), channel_id=1, source_target_pairs={{16,32},{48,64},{80,96},{112,128},{144,160},{176,192},{208,224},{2... | collective-permute-start | bytes 49160 | tf_op jit(solution)/shard_map/ppermute | solution.py:20
  4.9 1.9 %collective-permute-start = (f32[16,256]{1,0:T(8,128)}, f32[16,256]{1,0:T(8,128)S(1)}, u32[]{:S(2)}, u32[]{:S(2)}) collective-permute-start(f32[16,256]{1,0:T(8,128)} %slopes_hbm.1), channel_id=1, source_target_pairs={{0,16},{32,48},{64,80},{96,112},{128,144},{160,176},{192,208},{224... | collective-permute-start | bytes 49160 | tf_op jit(solution)/shard_map/ppermute | solution.py:20
  6.9 1.8 %select.1 = (bf16[768,512]{1,0:T(8,128)(2,1)S(1)}, f32[128,128]{1,0:T(8,128)S(1)}, f32[128,128]{1,0:T(8,128)S(1)}, f32[1,16]{1,0:T(1,128)S(1)}, f32[4,48,128]{2,...) custom-call(s32[1,512]{1,0:T(1,128)} %bitcast.4, s32[4,128]{1,0:T(4,128)} %bitcast.5, ...), custom_call_target="tpu_custom_call" | custom-call | flops 10000000 | bytes 5000000 | tf_op jit(solution)/shard_map/select/pallas_call | solution.py:217
  8.6 0.0 collective-permute-done.1.odd_ref
  8.6 0.0 collective-permute-done.even_ref
  8.7 1.9 %predict.1 = f32[4,176,128]{2,1,0:T(8,128)S(1)} custom-call(f32[16,256]{1,0:T(8,128)S(1)} %collective-permute-done.even_ref, f32[16,256]{1,0:T(8,128)S(1)} %collective-permute-done.1.odd_ref, f32[16,512]{1,0:T(8,128)S(1)} %get-tuple-element.19.own_coef_ref, f32[1,16]{1,0:T(1,128)S(1)} %get-tuple-element.20.fixed_ref, ...), custom_call_target="tpu_custom_call" | custom-call | tf_op jit(solution)/shard_map/predict/pallas_call | solution.py:256
  10.5 17.3 %all_to_all.20.parts_ref = f32[4,176,128]{2,1,0:T(8,128)S(1)} all-to-all(f32[4,176,128]{2,1,0:T(8,128)S(1)} %predict.1), channel_id=1, replica_groups={{0,1,2,3},{4,5,6,7},{8,9,10,11},{12,13,14,15},{16,17,18,19},{20,21,22,2..., dimensions={0} | all-to-all | bytes 720896 | tf_op jit(solution)/shard_map/all_to_all | solution.py:24
  27.9 0.3 gather.1
  28.2 33.9 %all_to_all.21.parts_ref = f32[4,160,128]{2,1,0:T(8,128)S(1)} all-to-all(f32[4,160,128]{2,1,0:T(8,128)S(1)} %gather.1), channel_id=1, replica_groups={{0,4,8,12},{1,5,9,13},{2,6,10,14},{3,7,11,15},{16,20,24,28},{17,21,25,2..., dimensions={0} | all-to-all | bytes 655360 | tf_op jit(solution)/shard_map/all_to_all | solution.py:24
  62.2 11.0 %all_to_all.22.back_ref = f32[4,128,128]{2,1,0:T(8,128)S(1)} all-to-all(f32[4,128,128]{2,1,0:T(8,128)S(1)} %get-tuple-element.25), channel_id=1, replica_groups={{0,1,2,3},{4,5,6,7},{8,9,10,11},{12,13,14,15},{16,17,18,19},{20,21,22,2..., dimensions={0} | all-to-all | bytes 524288 | tf_op jit(solution)/shard_map/all_to_all | solution.py:24
  73.2 2.1 %gradient.1 = (f32[32,2,128]{2,1,0:T(2,128)}, f32[512,128]{1,0:T(8,128)S(1)}) custom-call(bf16[16,512,128]{2,1,0:T(8,128)(2,1)S(1)} %get-tuple-element.18.design_ref, f32[4,128,128]{2,1,0:T(8,128)S(1)} %all_to_all.22.back_ref), custom_call_target="tpu_custom_call" | custom-call | tf_op jit(solution)/shard_map/gradient/pallas_call | solution.py:287
  75.3 5.8 %all-to-all-start.3 = ((f32[32,2,128]{2,1,0:T(2,128)}), f32[32,2,128]{2,1,0:T(2,128)S(1)}, u32[]{:S(2)}, u32[]{:S(2)}) async-start(f32[32,2,128]{2,1,0:T(2,128)} %get-tuple-element.26), calls=%async_computation.3 | async-start | bytes 65536 | tf_op jit(solution)/shard_map/all_to_all | solution.py:24
  81.0 0.3 group.1
  81.4 2.1 %collective-permute-start.2 = (f32[16,256]{1,0:T(8,128)S(1)}, f32[16,256]{1,0:T(8,128)S(1)}, u32[]{:S(2)}, u32[]{:S(2)}) collective-permute-start(f32[16,256]{1,0:T(8,128)S(1)} %get-tuple-element.30), channel_id=1, source_target_pairs={{0,16},{32,48},{64,80},{96,112},{128,144},{160,176},{192,208},{224... | collective-permute-start | bytes 49160 | tf_op jit(solution)/shard_map/ppermute | solution.py:20
  83.5 4.8 %collective-permute-start.3 = (f32[16,256]{1,0:T(8,128)S(1)}, f32[16,256]{1,0:T(8,128)S(1)}, u32[]{:S(2)}, u32[]{:S(2)}) collective-permute-start(f32[16,256]{1,0:T(8,128)S(1)} %get-tuple-element.31), channel_id=1, source_target_pairs={{16,32},{48,64},{80,96},{112,128},{144,160},{176,192},{208,224},{2... | collective-permute-start | bytes 49160 | tf_op jit(solution)/shard_map/ppermute | solution.py:20
  88.3 0.0 collective-permute-done.2.even_ref
  88.3 2.3 %collective-permute-done.3.odd_ref = f32[16,256]{1,0:T(8,128)S(1)} collective-permute-done((f32[16,256]{1,0:T(8,128)S(1)}, f32[16,256]{1,0:T(8,128)S(1)}, u32[]{:S(2)}, u32[]{:S(2)}) %collective-permute-start.3) | collective-permute-done | bytes 16416 | tf_op jit(solution)/shard_map/ppermute | solution.py:20
  90.6 0.0 all-to-all-done.3.fixed_all_ref
  90.6 0.6 finish.1
  (1 shorter events, 0.0 us)
Async XLA Ops:
  0.6 8.0 %collective-permute-start.1 = (f32[16,256]{1,0:T(8,128)}, f32[16,256]{1,0:T(8,128)S(1)}, u32[]{:S(2)}, u32[]{:S(2)}) collective-permute-start(f32[16,256]{1,0:T(8,128)} %slopes_hbm.1), channel_id=1, source_target_pairs={{16,32},{48,64},{80,96},{112,128},{144,160},{176,192},{208,224},{2... | collective-permute-start | bytes 49160 | tf_op jit(solution)/shard_map/ppermute | solution.py:20
  4.9 3.7 %collective-permute-start = (f32[16,256]{1,0:T(8,128)}, f32[16,256]{1,0:T(8,128)S(1)}, u32[]{:S(2)}, u32[]{:S(2)}) collective-permute-start(f32[16,256]{1,0:T(8,128)} %slopes_hbm.1), channel_id=1, source_target_pairs={{0,16},{32,48},{64,80},{96,112},{128,144},{160,176},{192,208},{224... | collective-permute-start | bytes 49160 | tf_op jit(solution)/shard_map/ppermute | solution.py:20
  75.3 15.4 %all-to-all-start.3 = ((f32[32,2,128]{2,1,0:T(2,128)}), f32[32,2,128]{2,1,0:T(2,128)S(1)}, u32[]{:S(2)}, u32[]{:S(2)}) async-start(f32[32,2,128]{2,1,0:T(2,128)} %get-tuple-element.26), calls=%async_computation.3 | async-start | bytes 65536 | tf_op jit(solution)/shard_map/all_to_all | solution.py:24
  81.4 6.9 %collective-permute-start.2 = (f32[16,256]{1,0:T(8,128)S(1)}, f32[16,256]{1,0:T(8,128)S(1)}, u32[]{:S(2)}, u32[]{:S(2)}) collective-permute-start(f32[16,256]{1,0:T(8,128)S(1)} %get-tuple-element.30), channel_id=1, source_target_pairs={{0,16},{32,48},{64,80},{96,112},{128,144},{160,176},{192,208},{224... | collective-permute-start | bytes 49160 | tf_op jit(solution)/shard_map/ppermute | solution.py:20
  83.5 7.2 %collective-permute-start.3 = (f32[16,256]{1,0:T(8,128)S(1)}, f32[16,256]{1,0:T(8,128)S(1)}, u32[]{:S(2)}, u32[]{:S(2)}) collective-permute-start(f32[16,256]{1,0:T(8,128)S(1)} %get-tuple-element.31), channel_id=1, source_target_pairs={{16,32},{48,64},{80,96},{112,128},{144,160},{176,192},{208,224},{2... | collective-permute-start | bytes 49160 | tf_op jit(solution)/shard_map/ppermute | solution.py:20

commit v6 on v5

--- a/solution.py
+++ b/solution.py
@@ -18,6 +18,22 @@
     peers = lax.axis_size(axis)
     pairs = [(i, i + 1) for i in range(first, peers - 1, 2)]
     return lax.ppermute(shard, axis, pairs + [(j, i) for i, j in pairs])
+
+
+def place_along_cov():
+    shift = lax.rem(lax.axis_index("rows"), 2) * (NEAR // 2)
+    covs = lax.axis_size("cov")
+    return lax.rem(lax.axis_index("cov") + covs - shift, covs), shift
+
+
+def cov_groups():
+    covs, rows = lax.axis_size("cov"), lax.axis_size("rows")
+    near, far = [], []
+    for row in range(rows):
+        members = [row * covs + (c + row % 2 * (NEAR // 2)) % covs for c in range(covs)]
+        near += [members[i : i + NEAR] for i in range(0, covs, NEAR)]
+        far += [members[j::NEAR] for j in range(NEAR)]
+    return near, far
 
 
 def exchange(parts, axis, groups=None):
@@ -53,7 +69,8 @@
     window, blocks = hot_ref.shape
     rows = label_ref.shape[0]
     size, groups = own_ref.shape
-    near = lax.rem(lax.axis_index("cov"), NEAR)
+    place, shift = place_along_cov()
+    near = lax.rem(place, NEAR)
     start = pl.multiple_of(near * rows, rows)
     copies = [
         pltpu.make_async_copy(group_hbm, group_ref, sems.at[0]),
@@ -80,10 +97,10 @@
         copy.wait()
     slope_rows = in_rows(own)
     precision = precision_ref[...]
-    place = lax.rem(lax.broadcasted_iota(jnp.int32, (size, LANES), 1) // size, NEAR)
+    columns = lax.rem(lax.broadcasted_iota(jnp.int32, (size, LANES), 1) // size, NEAR)
     for peer in range(NEAR):
         kept = [
-            jnp.where(place == peer, precision[:, at : at + LANES], 0.0)
+            jnp.where(columns == lax.rem(peer + shift, NEAR), precision[:, at : at + LANES], 0.0)
             for at in range(0, precision.shape[1], LANES)
         ]
         prior_ref[peer, : slope_rows.shape[0], :] = slope_rows
@@ -141,12 +158,14 @@
         precision=lax.Precision.HIGHEST,
         preferred_element_type=f32,
     )
-    near = lax.rem(lax.axis_index("cov"), NEAR)
+    place, shift = place_along_cov()
+    near = lax.rem(place, NEAR)
     pieces = LANES // size
     for i in range(far):
-        place = lax.rem(near + i % 2 * NEAR + i // 2, pieces)
+        cov = lax.rem(i * NEAR + near + shift, far * NEAR)
+        piece = lax.rem(lax.rem(cov, pieces) + cov // pieces, pieces)
         out_ref[i, :rows, :] = total
-        part = prior_ref[pl.ds(pl.multiple_of(place * size, size), size), :]
+        part = prior_ref[pl.ds(pl.multiple_of(piece * size, size), size), :]
         out_ref[i, rows:, :] = in_rows(part)
 
 
@@ -207,8 +226,7 @@
     covs, rows = lax.axis_size("cov"), lax.axis_size("rows")
     far = covs // NEAR
     share = blocks // NEAR
-    near_groups = [[i * NEAR + j for j in range(NEAR)] for i in range(far)]
-    far_groups = [[i * NEAR + j for i in range(far)] for j in range(NEAR)]
+    near_groups, far_groups = cov_groups()
     slope_rows = size * group_count // LANES
 
     from_even = swap(slopes, "rows", 0)
@@ -263,7 +281,7 @@
         name="predict",
     )(from_even, from_odd, own_coefs, fixed_row, hot, design_here, prior_rows)
 
-    received = exchange(partial, "cov", near_groups)
+    received = exchange(partial, ("rows", "cov"), near_groups)
     spread = pl.pallas_call(
         gather_kernel,
         out_shape=shape(far, share + slope_rows, LANES),
@@ -273,7 +291,7 @@
         compiler_params=ROOM,
         name="gather",
     )(received)
-    received = exchange(spread, "cov", far_groups)
+    received = exchange(spread, ("rows", "cov"), far_groups)
     spread, prior = pl.pallas_call(
         residual_kernel,
         out_shape=(shape(NEAR, share, LANES), shape(slope_rows, LANES)),
@@ -282,7 +300,7 @@
         compiler_params=ROOM,
         name="residual",
     )(received, label, valid)
-    back = exchange(spread, "cov", near_groups)
+    back = exchange(spread, ("rows", "cov"), near_groups)
 
     fixed_parts, grads = pl.pallas_call(
         gradient_kernel,

time: 92.4 us -> 91.8 us (level)
  starting transfers between devices: 18.9 us -> 17.9 us
    all_to_all x1, starting transfers between devices: 5.76 us -> 4.8 us  [exchange(): lax.all_to_all(parts, axis, 0, 0, tiled=True, axis_index_groups=groups)]
where the time goes in v6:
time: 91.8 us; the launch traced here: 90.7 us
  blocking collectives  62.7 us (68%)
  starting transfers between devices  17.9 us (19%)
  Pallas kernels  7.02 us (8%)
  waiting for transfers between devices  2.33 us (3%)
    all_to_all x3, blocking collectives, exchange(): lax.all_to_all(parts, axis, 0, 0, tiled=True, axis_index_groups=groups)  62.7 us
    ppermute x4, starting transfers between devices, swap(): return lax.ppermute(shard, axis, pairs + [(j, i) for i, j in pairs])  13.1 us
    all_to_all x1, starting transfers between devices, exchange(): lax.all_to_all(parts, axis, 0, 0, tiled=True, axis_index_groups=groups)  4.8 us
    ppermute x4, waiting for transfers between devices, swap(): return lax.ppermute(shard, axis, pairs + [(j, i) for i, j in pairs])  2.33 us
    pallas_call x1, Pallas kernels, body(): pl.pallas_call(gradient_kernel, out_shape=(shape(rows, 2, LANES), shape(b...  2.06 us
    pallas_call x1, Pallas kernels, body(): pl.pallas_call(predict_kernel, out_shape=shape(NEAR, share + slope_rows +...  1.88 us
  transfers between devices with their start and end apart: 5, of which 1 were waited for; matrix products, arithmetic and copies ran while one was open for 0% of the time, Pallas kernels for 2%

profile of v6, /device:TPU:24, one launch (start us, length us, event | category | flops | bytes accessed | tf_op | source)
XLA Modules:
  0.0 90.7 jit_solution(4420427157058036425)
XLA Ops:
  0.6 4.3 %collective-permute-start.1 = (f32[16,256]{1,0:T(8,128)}, f32[16,256]{1,0:T(8,128)S(1)}, u32[]{:S(2)}, u32[]{:S(2)}) collective-permute-start(f32[16,256]{1,0:T(8,128)} %slopes_hbm.1), channel_id=1, source_target_pairs={{16,32},{48,64},{80,96},{112,128},{144,160},{176,192},{208,224},{2... | collective-permute-start | bytes 49160 | tf_op jit(solution)/shard_map/ppermute | solution.py:20
  4.9 1.9 %collective-permute-start = (f32[16,256]{1,0:T(8,128)}, f32[16,256]{1,0:T(8,128)S(1)}, u32[]{:S(2)}, u32[]{:S(2)}) collective-permute-start(f32[16,256]{1,0:T(8,128)} %slopes_hbm.1), channel_id=1, source_target_pairs={{0,16},{32,48},{64,80},{96,112},{128,144},{160,176},{192,208},{224... | collective-permute-start | bytes 49160 | tf_op jit(solution)/shard_map/ppermute | solution.py:20
  6.9 1.8 %select.1 = (bf16[768,512]{1,0:T(8,128)(2,1)S(1)}, f32[128,128]{1,0:T(8,128)S(1)}, f32[128,128]{1,0:T(8,128)S(1)}, f32[1,16]{1,0:T(1,128)S(1)}, f32[4,48,128]{2,...) custom-call(s32[1,512]{1,0:T(1,128)} %bitcast.4, s32[4,128]{1,0:T(4,128)} %bitcast.5, ...), custom_call_target="tpu_custom_call" | custom-call | flops 10000000 | bytes 5000000 | tf_op jit(solution)/shard_map/select/pallas_call | solution.py:235
  8.6 0.0 collective-permute-done.1.odd_ref
  8.6 0.0 collective-permute-done.even_ref
  8.7 1.9 %predict.1 = f32[4,176,128]{2,1,0:T(8,128)S(1)} custom-call(f32[16,256]{1,0:T(8,128)S(1)} %collective-permute-done.even_ref, f32[16,256]{1,0:T(8,128)S(1)} %collective-permute-done.1.odd_ref, f32[16,512]{1,0:T(8,128)S(1)} %get-tuple-element.19.own_coef_ref, f32[1,16]{1,0:T(1,128)S(1)} %get-tuple-element.20.fixed_ref, ...), custom_call_target="tpu_custom_call" | custom-call | tf_op jit(solution)/shard_map/predict/pallas_call | solution.py:274
  10.5 14.6 %all_to_all.20.parts_ref = f32[4,176,128]{2,1,0:T(8,128)S(1)} all-to-all(f32[4,176,128]{2,1,0:T(8,128)S(1)} %predict.1), channel_id=1, replica_groups={{0,1,2,3},{4,5,6,7},{8,9,10,11},{12,13,14,15},{18,19,20,21},{22,23,24,2..., dimensions={0} | all-to-all | bytes 720896 | tf_op jit(solution)/shard_map/all_to_all | solution.py:40
  25.1 0.3 gather.1
  25.4 31.4 %all_to_all.21.parts_ref = f32[4,160,128]{2,1,0:T(8,128)S(1)} all-to-all(f32[4,160,128]{2,1,0:T(8,128)S(1)} %gather.1), channel_id=1, replica_groups={{0,4,8,12},{1,5,9,13},{2,6,10,14},{3,7,11,15},{18,22,26,30},{19,23,27,3..., dimensions={0} | all-to-all | bytes 655360 | tf_op jit(solution)/shard_map/all_to_all | solution.py:40
  56.9 16.7 %all_to_all.22.back_ref = f32[4,128,128]{2,1,0:T(8,128)S(1)} all-to-all(f32[4,128,128]{2,1,0:T(8,128)S(1)} %get-tuple-element.25), channel_id=1, replica_groups={{0,1,2,3},{4,5,6,7},{8,9,10,11},{12,13,14,15},{18,19,20,21},{22,23,24,2..., dimensions={0} | all-to-all | bytes 524288 | tf_op jit(solution)/shard_map/all_to_all | solution.py:40
  73.6 2.1 %gradient.1 = (f32[32,2,128]{2,1,0:T(2,128)}, f32[512,128]{1,0:T(8,128)S(1)}) custom-call(bf16[16,512,128]{2,1,0:T(8,128)(2,1)S(1)} %get-tuple-element.18.design_ref, f32[4,128,128]{2,1,0:T(8,128)S(1)} %all_to_all.22.back_ref), custom_call_target="tpu_custom_call" | custom-call | tf_op jit(solution)/shard_map/gradient/pallas_call | solution.py:305
  75.6 4.8 %all-to-all-start.3 = ((f32[32,2,128]{2,1,0:T(2,128)}), f32[32,2,128]{2,1,0:T(2,128)S(1)}, u32[]{:S(2)}, u32[]{:S(2)}) async-start(f32[32,2,128]{2,1,0:T(2,128)} %get-tuple-element.26), calls=%async_computation.3 | async-start | bytes 65536 | tf_op jit(solution)/shard_map/all_to_all | solution.py:40
  80.4 0.3 group.1
  80.8 2.1 %collective-permute-start.2 = (f32[16,256]{1,0:T(8,128)S(1)}, f32[16,256]{1,0:T(8,128)S(1)}, u32[]{:S(2)}, u32[]{:S(2)}) collective-permute-start(f32[16,256]{1,0:T(8,128)S(1)} %get-tuple-element.30), channel_id=1, source_target_pairs={{0,16},{32,48},{64,80},{96,112},{128,144},{160,176},{192,208},{224... | collective-permute-start | bytes 49160 | tf_op jit(solution)/shard_map/ppermute | solution.py:20
  82.9 4.8 %collective-permute-start.3 = (f32[16,256]{1,0:T(8,128)S(1)}, f32[16,256]{1,0:T(8,128)S(1)}, u32[]{:S(2)}, u32[]{:S(2)}) collective-permute-start(f32[16,256]{1,0:T(8,128)S(1)} %get-tuple-element.31), channel_id=1, source_target_pairs={{16,32},{48,64},{80,96},{112,128},{144,160},{176,192},{208,224},{2... | collective-permute-start | bytes 49160 | tf_op jit(solution)/shard_map/ppermute | solution.py:20
  87.7 0.0 collective-permute-done.2.even_ref
  87.7 2.3 %collective-permute-done.3.odd_ref = f32[16,256]{1,0:T(8,128)S(1)} collective-permute-done((f32[16,256]{1,0:T(8,128)S(1)}, f32[16,256]{1,0:T(8,128)S(1)}, u32[]{:S(2)}, u32[]{:S(2)}) %collective-permute-start.3) | collective-permute-done | bytes 16416 | tf_op jit(solution)/shard_map/ppermute | solution.py:20
  90.0 0.0 all-to-all-done.3.fixed_all_ref
  90.0 0.6 finish.1
  (1 shorter events, 0.0 us)
Async XLA Ops:
  0.6 8.0 %collective-permute-start.1 = (f32[16,256]{1,0:T(8,128)}, f32[16,256]{1,0:T(8,128)S(1)}, u32[]{:S(2)}, u32[]{:S(2)}) collective-permute-start(f32[16,256]{1,0:T(8,128)} %slopes_hbm.1), channel_id=1, source_target_pairs={{16,32},{48,64},{80,96},{112,128},{144,160},{176,192},{208,224},{2... | collective-permute-start | bytes 49160 | tf_op jit(solution)/shard_map/ppermute | solution.py:20
  4.9 3.7 %collective-permute-start = (f32[16,256]{1,0:T(8,128)}, f32[16,256]{1,0:T(8,128)S(1)}, u32[]{:S(2)}, u32[]{:S(2)}) collective-permute-start(f32[16,256]{1,0:T(8,128)} %slopes_hbm.1), channel_id=1, source_target_pairs={{0,16},{32,48},{64,80},{96,112},{128,144},{160,176},{192,208},{224... | collective-permute-start | bytes 49160 | tf_op jit(solution)/shard_map/ppermute | solution.py:20
  75.6 14.4 %all-to-all-start.3 = ((f32[32,2,128]{2,1,0:T(2,128)}), f32[32,2,128]{2,1,0:T(2,128)S(1)}, u32[]{:S(2)}, u32[]{:S(2)}) async-start(f32[32,2,128]{2,1,0:T(2,128)} %get-tuple-element.26), calls=%async_computation.3 | async-start | bytes 65536 | tf_op jit(solution)/shard_map/all_to_all | solution.py:40
  80.8 6.9 %collective-permute-start.2 = (f32[16,256]{1,0:T(8,128)S(1)}, f32[16,256]{1,0:T(8,128)S(1)}, u32[]{:S(2)}, u32[]{:S(2)}) collective-permute-start(f32[16,256]{1,0:T(8,128)S(1)} %get-tuple-element.30), channel_id=1, source_target_pairs={{0,16},{32,48},{64,80},{96,112},{128,144},{160,176},{192,208},{224... | collective-permute-start | bytes 49160 | tf_op jit(solution)/shard_map/ppermute | solution.py:20
  82.9 7.2 %collective-permute-start.3 = (f32[16,256]{1,0:T(8,128)S(1)}, f32[16,256]{1,0:T(8,128)S(1)}, u32[]{:S(2)}, u32[]{:S(2)}) collective-permute-start(f32[16,256]{1,0:T(8,128)S(1)} %get-tuple-element.31), channel_id=1, source_target_pairs={{16,32},{48,64},{80,96},{112,128},{144,160},{176,192},{208,224},{2... | collective-permute-start | bytes 49160 | tf_op jit(solution)/shard_map/ppermute | solution.py:20

commit v7 on v6

--- a/solution.py
+++ b/solution.py
@@ -63,7 +63,7 @@
 
 def select_kernel(
     group_hbm, fill_hbm, outcome_hbm, fixed_hbm, slopes_hbm, precision_hbm, design_hbm,
-    hot_ref, label_ref, valid_ref, fixed_ref, prior_ref, coef_ref, design_ref,
+    hot_ref, label_ref, valid_ref, fixed_ref, prior_ref, coef_ref, spread_ref, design_ref,
     group_ref, fill_ref, outcome_ref, own_ref, precision_ref, sems,
 ):
     window, blocks = hot_ref.shape
@@ -95,6 +95,14 @@
     )
     for copy in copies[2:6]:
         copy.wait()
+    across = lax.broadcasted_iota(jnp.int32, (size, size), 0)
+    along = lax.broadcasted_iota(jnp.int32, (size, size), 1)
+    fixed = jnp.where(across == along, jnp.broadcast_to(fixed_ref[...], (size, size)), 0.0)
+    coef_ref[...] += jnp.sum(fixed, axis=1, keepdims=True)
+    part = lax.broadcasted_iota(jnp.int32, (LANES, LANES), 0)
+    for p in range(size):
+        ones = (lax.rem(part, size) == p) & (part < 3 * size)
+        spread_ref[:, p * LANES : (p + 1) * LANES] = ones.astype(f32).astype(bf16)
     slope_rows = in_rows(own)
     precision = precision_ref[...]
     columns = lax.rem(lax.broadcasted_iota(jnp.int32, (size, LANES), 1) // size, NEAR)
@@ -114,7 +122,7 @@
 
 
 def predict_kernel(
-    even_ref, odd_ref, own_coef_ref, fixed_ref, hot_ref, design_ref, prior_ref, out_ref, coef_ref
+    even_ref, odd_ref, own_coef_ref, hot_ref, spread_ref, design_ref, prior_ref, out_ref, coef_ref
 ):
     size, groups = even_ref.shape
     blocks = hot_ref.shape[1]
@@ -124,15 +132,20 @@
     for ref, place in ((even_ref, 1 - parity), (odd_ref, parity)):
         piece = hot_ref[pl.ds(pl.multiple_of(place * 2 * groups, groups), groups), :]
         coefs += add_parts(jnp.dot(three_parts(ref[...]), piece, preferred_element_type=f32))
-    padded = jnp.concatenate([coefs, jnp.zeros((LANES - size, blocks), f32)], axis=0)
-    coef_ref[...] = padded.T[:, :size] + fixed_ref[...]
+    parts = three_parts(coefs).astype(f32)
+    padded = jnp.concatenate([parts, jnp.zeros((LANES - 3 * size, blocks), f32)], axis=0)
+    coef_ref[...] = padded.T.astype(bf16)
 
     def chunk(peer, carry):
         start = pl.multiple_of(peer * share, share)
         here = coef_ref[pl.ds(start, share), :]
         total = jnp.zeros((share, LANES), f32)
-        for p in range(size):
-            total = total + here[:, p : p + 1] * design_ref[p, pl.ds(start, share), :].astype(f32)
+        for p in range(0, size, 2):
+            wide = jnp.dot(
+                here, spread_ref[:, p * LANES : (p + 2) * LANES], preferred_element_type=f32
+            )
+            total = total + wide[:, :LANES] * design_ref[p, pl.ds(start, share), :].astype(f32)
+            total = total + wide[:, LANES:] * design_ref[p + 1, pl.ds(start, share), :].astype(f32)
         out_ref[peer, :share, :] = total
         out_ref[peer, share:, :] = prior_ref[peer]
         return carry
@@ -177,12 +190,38 @@
     prior_ref[...] = jnp.sum(parts_ref[:, rows:, :], axis=0)
 
 
-def gradient_kernel(design_ref, back_ref, fixed_ref, grad_ref):
+def fixed_kernel(design_ref, back_ref, fixed_ref):
     size, blocks, _ = design_ref.shape
     share = blocks // NEAR
+    step = 64
+
+    def chunk(i, totals):
+        start = pl.multiple_of(i * step, step)
+        inner = pl.multiple_of(lax.rem(start, share), step)
+        residual = back_ref[start // share, pl.ds(inner, step), :]
+        new = []
+        for p in range(size):
+            product = design_ref[p, pl.ds(start, step), :].astype(f32) * residual
+            new.append(totals[p] + jnp.sum(product.reshape(step // 8, 8, LANES), axis=0))
+        return tuple(new)
+
+    zero = jnp.zeros((8, LANES), f32)
+    totals = lax.fori_loop(0, blocks // step, chunk, (zero,) * size)
+    lane = lax.broadcasted_iota(jnp.int32, (8, LANES), 1)
+    row = zero
+    for p in range(size):
+        row = jnp.where(lane == p, jnp.sum(totals[p], axis=1, keepdims=True), row)
+    row = jnp.sum(row, axis=0, keepdims=True)
+    fixed_ref[...] = jnp.broadcast_to(row[None], fixed_ref.shape)
+
+
+def group_kernel(design_ref, back_ref, hot_ref, prior_ref, even_ref, odd_ref, own_ref, grad_ref):
+    size, groups = own_ref.shape
+    blocks = design_ref.shape[1]
+    share = blocks // NEAR
     lane = lax.broadcasted_iota(jnp.int32, (share, LANES), 1)
 
-    def chunk(peer, total):
+    def chunk(peer, carry):
         start = pl.multiple_of(peer * share, share)
         residual = back_ref[peer]
         grads = jnp.zeros((share, LANES), f32)
@@ -190,14 +229,9 @@
             product = design_ref[p, pl.ds(start, share), :].astype(f32) * residual
             grads = jnp.where(lane == p, jnp.sum(product, axis=1, keepdims=True), grads)
         grad_ref[pl.ds(start, share), :] = grads
-        return total + jnp.sum(grads, axis=0, keepdims=True)
-
-    total = lax.fori_loop(0, NEAR, chunk, jnp.zeros((1, LANES), f32))
-    fixed_ref[...] = jnp.broadcast_to(total[None], fixed_ref.shape)
-
-
-def group_kernel(grad_ref, hot_ref, prior_ref, even_ref, odd_ref, own_ref):
-    size, groups = own_ref.shape
+        return carry
+
+    lax.fori_loop(0, NEAR, chunk, 0)
     parts = three_parts(grad_ref[...].T[:size])
     sums = add_parts(
         lax.dot_general(parts, hot_ref[...], (((1,), (1,)), ((), ())), preferred_element_type=f32)
@@ -232,7 +266,7 @@
     from_even = swap(slopes, "rows", 0)
     from_odd = swap(slopes, "rows", 1)
 
-    hot, label, valid, fixed_row, prior_rows, own_coefs, design_here = pl.pallas_call(
+    hot, label, valid, fixed_row, prior_rows, own_coefs, spread_hot, design_here = pl.pallas_call(
         select_kernel,
         out_shape=(
             shape(3 * group_count, blocks, dtype=bf16),
@@ -241,10 +275,11 @@
             shape(1, size),
             shape(NEAR, slope_rows + size, LANES),
             shape(size, blocks),
+            shape(LANES, size * LANES, dtype=bf16),
             shape(*design.shape, dtype=bf16),
         ),
         in_specs=[HBM] * 7,
-        out_specs=(VMEM,) * 7,
+        out_specs=(VMEM,) * 8,
         scratch_shapes=[
             pltpu.VMEM((1, blocks), jnp.int32),
             pltpu.VMEM((blocks // LANES, LANES), jnp.int32),
@@ -276,10 +311,10 @@
         out_shape=shape(NEAR, share + slope_rows + size, LANES),
         in_specs=[VMEM] * 7,
         out_specs=VMEM,
-        scratch_shapes=[pltpu.VMEM((blocks, size), f32)],
+        scratch_shapes=[pltpu.VMEM((blocks, LANES), bf16)],
         compiler_params=ROOM,
         name="predict",
-    )(from_even, from_odd, own_coefs, fixed_row, hot, design_here, prior_rows)
+    )(from_even, from_odd, own_coefs, hot, spread_hot, design_here, prior_rows)
 
     received = exchange(partial, ("rows", "cov"), near_groups)
     spread = pl.pallas_call(
@@ -302,25 +337,26 @@
     )(received, label, valid)
     back = exchange(spread, ("rows", "cov"), near_groups)
 
-    fixed_parts, grads = pl.pallas_call(
-        gradient_kernel,
-        out_shape=(shape(rows, 2, LANES), shape(blocks, LANES)),
+    fixed_parts = pl.pallas_call(
+        fixed_kernel,
+        out_shape=shape(rows, 2, LANES),
         in_specs=[VMEM] * 2,
-        out_specs=(VMEM,) * 2,
-        compiler_params=ROOM,
-        name="gradient",
+        out_specs=VMEM,
+        compiler_params=ROOM,
+        name="fixed",
     )(design_here, back)
     fixed_all = exchange(fixed_parts, "rows")
 
     to_even, to_odd, own = pl.pallas_call(
         group_kernel,
         out_shape=(shape(size, group_count),) * 3,
-        in_specs=[VMEM] * 3,
+        in_specs=[VMEM] * 4,
         out_specs=(VMEM,) * 3,
+        scratch_shapes=[pltpu.VMEM((blocks, LANES), f32)],
         compiler_params=ROOM,
         cost_estimate=cost(100_000_000, 5_000_000),
         name="group",
-    )(grads, hot, prior)
+    )(design_here, back, hot, prior)
     given_even = swap(to_even, "rows", 0)
     given_odd = swap(to_odd, "rows", 1)
 

time: 91.8 us -> 92 us (level)
    pallas_call x1, Pallas kernels: 0.35 us -> 1.74 us  [body(): pl.pallas_call(group_kernel, out_shape=(shape(size, group_count),) * 3, i...]
  transfers between devices with their start and end apart: 5 -> 5, of which waited for: 1 -> 1; matrix products, arithmetic and copies ran while one was open for 0% -> 0% of each run, Pallas kernels for 2% -> 4%
where the time goes in v7:
time: 92 us; the launch traced here: 90.9 us
  blocking collectives  62.7 us (68%)
  starting transfers between devices  18 us (20%)
  Pallas kernels  7.19 us (8%)
  waiting for transfers between devices  2.33 us (3%)
    all_to_all x3, blocking collectives, exchange(): lax.all_to_all(parts, axis, 0, 0, tiled=True, axis_index_groups=groups)  62.7 us
    ppermute x4, starting transfers between devices, swap(): return lax.ppermute(shard, axis, pairs + [(j, i) for i, j in pairs])  13.1 us
    all_to_all x1, starting transfers between devices, exchange(): lax.all_to_all(parts, axis, 0, 0, tiled=True, axis_index_groups=groups)  4.88 us
    ppermute x4, waiting for transfers between devices, swap(): return lax.ppermute(shard, axis, pairs + [(j, i) for i, j in pairs])  2.33 us
  transfers between devices with their start and end apart: 5, of which 1 were waited for; matrix products, arithmetic and copies ran while one was open for 0% of the time, Pallas kernels for 4%

profile of v7, /device:TPU:24, one launch (start us, length us, event | category | flops | bytes accessed | tf_op | source)
XLA Modules:
  0.0 90.9 jit_solution(12217513693829522718)
XLA Ops:
  0.6 4.3 %collective-permute-start.1 = (f32[16,256]{1,0:T(8,128)}, f32[16,256]{1,0:T(8,128)S(1)}, u32[]{:S(2)}, u32[]{:S(2)}) collective-permute-start(f32[16,256]{1,0:T(8,128)} %slopes_hbm.1), channel_id=1, source_target_pairs={{16,32},{48,64},{80,96},{112,128},{144,160},{176,192},{208,224},{2... | collective-permute-start | bytes 49160 | tf_op jit(solution)/shard_map/ppermute | solution.py:20
  4.9 1.9 %collective-permute-start = (f32[16,256]{1,0:T(8,128)}, f32[16,256]{1,0:T(8,128)S(1)}, u32[]{:S(2)}, u32[]{:S(2)}) collective-permute-start(f32[16,256]{1,0:T(8,128)} %slopes_hbm.1), channel_id=1, source_target_pairs={{0,16},{32,48},{64,80},{96,112},{128,144},{160,176},{192,208},{224... | collective-permute-start | bytes 49160 | tf_op jit(solution)/shard_map/ppermute | solution.py:20
  6.9 1.8 %select.1 = (bf16[768,512]{1,0:T(8,128)(2,1)S(1)}, f32[128,128]{1,0:T(8,128)S(1)}, f32[128,128]{1,0:T(8,128)S(1)}, f32[1,16]{1,0:T(1,128)S(1)}, f32[4,48,128]{2,...) custom-call(s32[1,512]{1,0:T(1,128)} %bitcast.4, ...), custom_call_target="tpu_custom_call" | custom-call | flops 10000000 | bytes 5000000 | tf_op jit(solution)/shard_map/select/pallas_call | solution.py:269
  8.6 0.0 collective-permute-done.1.odd_ref
  8.6 0.0 collective-permute-done.even_ref
  8.7 1.5 %predict.1 = f32[4,176,128]{2,1,0:T(8,128)S(1)} custom-call(f32[16,256]{1,0:T(8,128)S(1)} %collective-permute-done.even_ref, f32[16,256]{1,0:T(8,128)S(1)} %collective-permute-done.1.odd_ref, f32[16,512]{1,0:T(8,128)S(1)} %get-tuple-element.18.own_coef_ref, bf16[768,512]{1,0:T(8,128)(2,1)S(1)} %get-tuple-element.19.hot_ref, ...), custom_call_target="tpu_custom_call" | custom-call | tf_op jit(solution)/shard_map/predict/pallas_call | solution.py:309
  10.2 14.6 %all_to_all.20.parts_ref = f32[4,176,128]{2,1,0:T(8,128)S(1)} all-to-all(f32[4,176,128]{2,1,0:T(8,128)S(1)} %predict.1), channel_id=1, replica_groups={{0,1,2,3},{4,5,6,7},{8,9,10,11},{12,13,14,15},{18,19,20,21},{22,23,24,2..., dimensions={0} | all-to-all | bytes 720896 | tf_op jit(solution)/shard_map/all_to_all | solution.py:40
  24.8 0.3 gather.1
  25.1 31.5 %all_to_all.21.parts_ref = f32[4,160,128]{2,1,0:T(8,128)S(1)} all-to-all(f32[4,160,128]{2,1,0:T(8,128)S(1)} %gather.1), channel_id=1, replica_groups={{0,4,8,12},{1,5,9,13},{2,6,10,14},{3,7,11,15},{18,22,26,30},{19,23,27,3..., dimensions={0} | all-to-all | bytes 655360 | tf_op jit(solution)/shard_map/all_to_all | solution.py:40
  56.7 16.5 %all_to_all.22.back_ref = f32[4,128,128]{2,1,0:T(8,128)S(1)} all-to-all(f32[4,128,128]{2,1,0:T(8,128)S(1)} %get-tuple-element.24), channel_id=1, replica_groups={{0,1,2,3},{4,5,6,7},{8,9,10,11},{12,13,14,15},{18,19,20,21},{22,23,24,2..., dimensions={0} | all-to-all | bytes 524288 | tf_op jit(solution)/shard_map/all_to_all | solution.py:40
  73.2 1.2 %fixed.1 = f32[32,2,128]{2,1,0:T(2,128)} custom-call(bf16[16,512,128]{2,1,0:T(8,128)(2,1)S(1)} %get-tuple-element.17.design_ref, f32[4,128,128]{2,1,0:T(8,128)S(1)} %all_to_all.22.back_ref), custom_call_target="tpu_custom_call" | custom-call | tf_op jit(solution)/shard_map/fixed/pallas_call | solution.py:340
  74.4 4.9 %all-to-all-start.3 = ((f32[32,2,128]{2,1,0:T(2,128)}), f32[32,2,128]{2,1,0:T(2,128)S(1)}, u32[]{:S(2)}, u32[]{:S(2)}) async-start(f32[32,2,128]{2,1,0:T(2,128)} %fixed.1), calls=%async_computation.3 | async-start | bytes 65536 | tf_op jit(solution)/shard_map/all_to_all | solution.py:40
  79.3 1.7 %group.1 = (f32[16,256]{1,0:T(8,128)S(1)}, f32[16,256]{1,0:T(8,128)S(1)}, f32[16,256]{1,0:T(8,128)S(1)}) custom-call(bf16[16,512,128]{2,1,0:T(8,128)(2,1)S(1)} %get-tuple-element.17.design_ref, f32[4,128,128]{2,1,0:T(8,128)S(1)} %all_to_all.22.back_ref, bf16[768,512]{1,0:T(8,128)(2,1)S(1)} %get-tuple-element.19.hot_ref, ...), custom_call_target="tpu_custom_call" | custom-call | flops 100000000 | bytes 5000000 | tf_op jit(solution)/shard_map/group/pallas_call | solution.py:350
  81.0 2.1 %collective-permute-start.2 = (f32[16,256]{1,0:T(8,128)S(1)}, f32[16,256]{1,0:T(8,128)S(1)}, u32[]{:S(2)}, u32[]{:S(2)}) collective-permute-start(f32[16,256]{1,0:T(8,128)S(1)} %get-tuple-element.28), channel_id=1, source_target_pairs={{0,16},{32,48},{64,80},{96,112},{128,144},{160,176},{192,208},{224... | collective-permute-start | bytes 49160 | tf_op jit(solution)/shard_map/ppermute | solution.py:20
  83.1 4.8 %collective-permute-start.3 = (f32[16,256]{1,0:T(8,128)S(1)}, f32[16,256]{1,0:T(8,128)S(1)}, u32[]{:S(2)}, u32[]{:S(2)}) collective-permute-start(f32[16,256]{1,0:T(8,128)S(1)} %get-tuple-element.29), channel_id=1, source_target_pairs={{16,32},{48,64},{80,96},{112,128},{144,160},{176,192},{208,224},{2... | collective-permute-start | bytes 49160 | tf_op jit(solution)/shard_map/ppermute | solution.py:20
  88.0 0.0 collective-permute-done.2.even_ref
  88.0 2.3 %collective-permute-done.3.odd_ref = f32[16,256]{1,0:T(8,128)S(1)} collective-permute-done((f32[16,256]{1,0:T(8,128)S(1)}, f32[16,256]{1,0:T(8,128)S(1)}, u32[]{:S(2)}, u32[]{:S(2)}) %collective-permute-start.3) | collective-permute-done | bytes 16416 | tf_op jit(solution)/shard_map/ppermute | solution.py:20
  90.3 0.0 all-to-all-done.3.fixed_all_ref
  90.3 0.6 finish.1
  (1 shorter events, 0.0 us)
Async XLA Ops:
  0.6 8.0 %collective-permute-start.1 = (f32[16,256]{1,0:T(8,128)}, f32[16,256]{1,0:T(8,128)S(1)}, u32[]{:S(2)}, u32[]{:S(2)}) collective-permute-start(f32[16,256]{1,0:T(8,128)} %slopes_hbm.1), channel_id=1, source_target_pairs={{16,32},{48,64},{80,96},{112,128},{144,160},{176,192},{208,224},{2... | collective-permute-start | bytes 49160 | tf_op jit(solution)/shard_map/ppermute | solution.py:20
  4.9 3.7 %collective-permute-start = (f32[16,256]{1,0:T(8,128)}, f32[16,256]{1,0:T(8,128)S(1)}, u32[]{:S(2)}, u32[]{:S(2)}) collective-permute-start(f32[16,256]{1,0:T(8,128)} %slopes_hbm.1), channel_id=1, source_target_pairs={{0,16},{32,48},{64,80},{96,112},{128,144},{160,176},{192,208},{224... | collective-permute-start | bytes 49160 | tf_op jit(solution)/shard_map/ppermute | solution.py:20
  74.4 15.9 %all-to-all-start.3 = ((f32[32,2,128]{2,1,0:T(2,128)}), f32[32,2,128]{2,1,0:T(2,128)S(1)}, u32[]{:S(2)}, u32[]{:S(2)}) async-start(f32[32,2,128]{2,1,0:T(2,128)} %fixed.1), calls=%async_computation.3 | async-start | bytes 65536 | tf_op jit(solution)/shard_map/all_to_all | solution.py:40
  81.0 6.9 %collective-permute-start.2 = (f32[16,256]{1,0:T(8,128)S(1)}, f32[16,256]{1,0:T(8,128)S(1)}, u32[]{:S(2)}, u32[]{:S(2)}) collective-permute-start(f32[16,256]{1,0:T(8,128)S(1)} %get-tuple-element.28), channel_id=1, source_target_pairs={{0,16},{32,48},{64,80},{96,112},{128,144},{160,176},{192,208},{224... | collective-permute-start | bytes 49160 | tf_op jit(solution)/shard_map/ppermute | solution.py:20
  83.1 7.2 %collective-permute-start.3 = (f32[16,256]{1,0:T(8,128)S(1)}, f32[16,256]{1,0:T(8,128)S(1)}, u32[]{:S(2)}, u32[]{:S(2)}) collective-permute-start(f32[16,256]{1,0:T(8,128)S(1)} %get-tuple-element.29), channel_id=1, source_target_pairs={{16,32},{48,64},{80,96},{112,128},{144,160},{176,192},{208,224},{2... | collective-permute-start | bytes 49160 | tf_op jit(solution)/shard_map/ppermute | solution.py:20

commit v8 on v6

--- a/solution.py
+++ b/solution.py
@@ -26,14 +26,21 @@
     return lax.rem(lax.axis_index("cov") + covs - shift, covs), shift
 
 
+def far_partners(i, odd):
+    a, b = i + 1 - 2 * (i % 2), 3 - i
+    return a + odd * (b - a), b + odd * (a - b)
+
+
 def cov_groups():
     covs, rows = lax.axis_size("cov"), lax.axis_size("rows")
-    near, far = [], []
+    near, first, second = [], [], []
     for row in range(rows):
         members = [row * covs + (c + row % 2 * (NEAR // 2)) % covs for c in range(covs)]
         near += [members[i : i + NEAR] for i in range(0, covs, NEAR)]
-        far += [members[j::NEAR] for j in range(NEAR)]
-    return near, far
+        for i in (0, 2):
+            for pairs, partner in zip((first, second), far_partners(i, row % 2)):
+                pairs += [[members[i * NEAR + j], members[partner * NEAR + j]] for j in range(NEAR)]
+    return near, first, second
 
 
 def exchange(parts, axis, groups=None):
@@ -63,7 +70,7 @@
 
 def select_kernel(
     group_hbm, fill_hbm, outcome_hbm, fixed_hbm, slopes_hbm, precision_hbm, design_hbm,
-    hot_ref, label_ref, valid_ref, fixed_ref, prior_ref, coef_ref, design_ref,
+    hot_ref, label_ref, valid_ref, fixed_ref, prior_ref, coef_ref, spread_ref, design_ref,
     group_ref, fill_ref, outcome_ref, own_ref, precision_ref, sems,
 ):
     window, blocks = hot_ref.shape
@@ -95,6 +102,14 @@
     )
     for copy in copies[2:6]:
         copy.wait()
+    across = lax.broadcasted_iota(jnp.int32, (size, size), 0)
+    along = lax.broadcasted_iota(jnp.int32, (size, size), 1)
+    fixed = jnp.where(across == along, jnp.broadcast_to(fixed_ref[...], (size, size)), 0.0)
+    coef_ref[...] += jnp.sum(fixed, axis=1, keepdims=True)
+    part = lax.broadcasted_iota(jnp.int32, (LANES, LANES), 0)
+    for p in range(size):
+        ones = (lax.rem(part, size) == p) & (part < 3 * size)
+        spread_ref[:, p * LANES : (p + 1) * LANES] = ones.astype(f32).astype(bf16)
     slope_rows = in_rows(own)
     precision = precision_ref[...]
     columns = lax.rem(lax.broadcasted_iota(jnp.int32, (size, LANES), 1) // size, NEAR)
@@ -114,7 +129,7 @@
 
 
 def predict_kernel(
-    even_ref, odd_ref, own_coef_ref, fixed_ref, hot_ref, design_ref, prior_ref, out_ref, coef_ref
+    even_ref, odd_ref, own_coef_ref, hot_ref, spread_ref, design_ref, prior_ref, out_ref, coef_ref
 ):
     size, groups = even_ref.shape
     blocks = hot_ref.shape[1]
@@ -124,15 +139,20 @@
     for ref, place in ((even_ref, 1 - parity), (odd_ref, parity)):
         piece = hot_ref[pl.ds(pl.multiple_of(place * 2 * groups, groups), groups), :]
         coefs += add_parts(jnp.dot(three_parts(ref[...]), piece, preferred_element_type=f32))
-    padded = jnp.concatenate([coefs, jnp.zeros((LANES - size, blocks), f32)], axis=0)
-    coef_ref[...] = padded.T[:, :size] + fixed_ref[...]
+    parts = three_parts(coefs).astype(f32)
+    padded = jnp.concatenate([parts, jnp.zeros((LANES - 3 * size, blocks), f32)], axis=0)
+    coef_ref[...] = padded.T.astype(bf16)
 
     def chunk(peer, carry):
         start = pl.multiple_of(peer * share, share)
         here = coef_ref[pl.ds(start, share), :]
         total = jnp.zeros((share, LANES), f32)
-        for p in range(size):
-            total = total + here[:, p : p + 1] * design_ref[p, pl.ds(start, share), :].astype(f32)
+        for p in range(0, size, 2):
+            wide = jnp.dot(
+                here, spread_ref[:, p * LANES : (p + 2) * LANES], preferred_element_type=f32
+            )
+            total = total + wide[:, :LANES] * design_ref[p, pl.ds(start, share), :].astype(f32)
+            total = total + wide[:, LANES:] * design_ref[p + 1, pl.ds(start, share), :].astype(f32)
         out_ref[peer, :share, :] = total
         out_ref[peer, share:, :] = prior_ref[peer]
         return carry
@@ -143,9 +163,8 @@
 def gather_kernel(parts_ref, out_ref, prior_ref):
     groups = prior_ref.shape[1]
     halves = groups // LANES
-    size = (parts_ref.shape[1] - out_ref.shape[1])
-    rows = out_ref.shape[1] - size * halves
-    far = out_ref.shape[0]
+    size = out_ref.shape[1] - parts_ref.shape[1]
+    rows = parts_ref.shape[1] - size * (halves + 1)
     total = jnp.sum(parts_ref[:, :rows, :], axis=0)
     columns = [
         parts_ref[:, at : at + size, :].reshape(-1, LANES)
@@ -159,14 +178,33 @@
         preferred_element_type=f32,
     )
     place, shift = place_along_cov()
-    near = lax.rem(place, NEAR)
+    near, group = lax.rem(place, NEAR), place // NEAR
+    odd = lax.rem(lax.axis_index("rows"), 2)
+    parity = lax.rem(group, 2)
+    partner, _ = far_partners(group, odd)
     pieces = LANES // size
-    for i in range(far):
-        cov = lax.rem(i * NEAR + near + shift, far * NEAR)
-        piece = lax.rem(lax.rem(cov, pieces) + cov // pieces, pieces)
-        out_ref[i, :rows, :] = total
-        part = prior_ref[pl.ds(pl.multiple_of(piece * size, size), size), :]
-        out_ref[i, rows:, :] = in_rows(part)
+    for k in range(out_ref.shape[0]):
+        target = jnp.where(parity == k, group, partner)
+        _, beyond = far_partners(target, odd)
+        out_ref[k, :rows, :] = total
+        for at, member in ((rows, target), (rows + halves * size, beyond)):
+            cov = lax.rem(member * NEAR + near + shift, lax.axis_size("cov"))
+            piece = lax.rem(lax.rem(cov, pieces) + cov // pieces, pieces)
+            part = prior_ref[pl.ds(pl.multiple_of(piece * size, size), size), :]
+            out_ref[k, at : at + halves * size, :] = in_rows(part)
+
+
+def relay_kernel(parts_ref, out_ref):
+    rows = 2 * out_ref.shape[1] - parts_ref.shape[1]
+    size = out_ref.shape[1] - rows
+    total = jnp.sum(parts_ref[...], axis=0)
+    place, _ = place_along_cov()
+    parity = lax.rem(place // NEAR, 2)
+    for k in range(out_ref.shape[0]):
+        out_ref[k, :rows, :] = total[:rows]
+        out_ref[k, rows:, :] = jnp.where(
+            parity == k, total[rows : rows + size], total[rows + size :]
+        )
 
 
 def residual_kernel(parts_ref, label_ref, valid_ref, out_ref, prior_ref):
@@ -224,15 +262,14 @@
     size, group_count = slopes.shape
     blocks = block_group.shape[0]
     covs, rows = lax.axis_size("cov"), lax.axis_size("rows")
-    far = covs // NEAR
     share = blocks // NEAR
-    near_groups, far_groups = cov_groups()
+    near_groups, first_pairs, second_pairs = cov_groups()
     slope_rows = size * group_count // LANES
 
     from_even = swap(slopes, "rows", 0)
     from_odd = swap(slopes, "rows", 1)
 
-    hot, label, valid, fixed_row, prior_rows, own_coefs, design_here = pl.pallas_call(
+    hot, label, valid, fixed_row, prior_rows, own_coefs, spread_hot, design_here = pl.pallas_call(
         select_kernel,
         out_shape=(
             shape(3 * group_count, blocks, dtype=bf16),
@@ -241,10 +278,11 @@
             shape(1, size),
             shape(NEAR, slope_rows + size, LANES),
             shape(size, blocks),
+            shape(LANES, size * LANES, dtype=bf16),
             shape(*design.shape, dtype=bf16),
         ),
         in_specs=[HBM] * 7,
-        out_specs=(VMEM,) * 7,
+        out_specs=(VMEM,) * 8,
         scratch_shapes=[
             pltpu.VMEM((1, blocks), jnp.int32),
             pltpu.VMEM((blocks // LANES, LANES), jnp.int32),
@@ -276,22 +314,31 @@
         out_shape=shape(NEAR, share + slope_rows + size, LANES),
         in_specs=[VMEM] * 7,
         out_specs=VMEM,
-        scratch_shapes=[pltpu.VMEM((blocks, size), f32)],
+        scratch_shapes=[pltpu.VMEM((blocks, LANES), bf16)],
         compiler_params=ROOM,
         name="predict",
-    )(from_even, from_odd, own_coefs, fixed_row, hot, design_here, prior_rows)
+    )(from_even, from_odd, own_coefs, hot, spread_hot, design_here, prior_rows)
 
     received = exchange(partial, ("rows", "cov"), near_groups)
     spread = pl.pallas_call(
         gather_kernel,
-        out_shape=shape(far, share + slope_rows, LANES),
+        out_shape=shape(2, share + 2 * slope_rows, LANES),
         in_specs=[VMEM],
         out_specs=VMEM,
         scratch_shapes=[pltpu.VMEM((LANES, group_count), f32)],
         compiler_params=ROOM,
         name="gather",
     )(received)
-    received = exchange(spread, ("rows", "cov"), far_groups)
+    received = exchange(spread, ("rows", "cov"), first_pairs)
+    spread = pl.pallas_call(
+        relay_kernel,
+        out_shape=shape(2, share + slope_rows, LANES),
+        in_specs=[VMEM],
+        out_specs=VMEM,
+        compiler_params=ROOM,
+        name="relay",
+    )(received)
+    received = exchange(spread, ("rows", "cov"), second_pairs)
     spread, prior = pl.pallas_call(
         residual_kernel,
         out_shape=(shape(NEAR, share, LANES), shape(slope_rows, LANES)),

time: 91.8 us -> 89.1 us (0.971)
  blocking collectives: 62.7 us -> 56.7 us
  starting transfers between devices: 17.9 us -> 21.5 us
    all_to_all x3 -> x4, blocking collectives: 62.7 us -> 56.7 us  [exchange(): lax.all_to_all(parts, axis, 0, 0, tiled=True, axis_index_groups=groups)]
    all_to_all x1, starting transfers between devices: 4.8 us -> 8.4 us  [exchange(): lax.all_to_all(parts, axis, 0, 0, tiled=True, axis_index_groups=groups)]
where the time goes in v8:
time: 89.1 us; the launch traced here: 87.9 us
  blocking collectives  56.7 us (64%)
  starting transfers between devices  21.5 us (24%)
  Pallas kernels  6.65 us (7%)
  waiting for transfers between devices  2.33 us (3%)
    all_to_all x4, blocking collectives, exchange(): lax.all_to_all(parts, axis, 0, 0, tiled=True, axis_index_groups=groups)  56.7 us
    ppermute x4, starting transfers between devices, swap(): return lax.ppermute(shard, axis, pairs + [(j, i) for i, j in pairs])  13.1 us
    all_to_all x1, starting transfers between devices, exchange(): lax.all_to_all(parts, axis, 0, 0, tiled=True, axis_index_groups=groups)  8.4 us
    ppermute x4, waiting for transfers between devices, swap(): return lax.ppermute(shard, axis, pairs + [(j, i) for i, j in pairs])  2.33 us
    pallas_call x1, Pallas kernels, body(): pl.pallas_call(gradient_kernel, out_shape=(shape(rows, 2, LANES), shape(b...  2.05 us
  transfers between devices with their start and end apart: 5, of which 1 were waited for; matrix products, arithmetic and copies ran while one was open for 0% of the time, Pallas kernels for 2%

profile of v8, /device:TPU:24, one launch (start us, length us, event | category | flops | bytes accessed | tf_op | source)
XLA Modules:
  0.0 87.9 jit_solution(11819946052823245705)
XLA Ops:
  0.6 4.3 %collective-permute-start.1 = (f32[16,256]{1,0:T(8,128)}, f32[16,256]{1,0:T(8,128)S(1)}, u32[]{:S(2)}, u32[]{:S(2)}) collective-permute-start(f32[16,256]{1,0:T(8,128)} %slopes_hbm.1), channel_id=1, source_target_pairs={{16,32},{48,64},{80,96},{112,128},{144,160},{176,192},{208,224},{2... | collective-permute-start | bytes 49160 | tf_op jit(solution)/shard_map/ppermute | solution.py:20
  4.9 1.9 %collective-permute-start = (f32[16,256]{1,0:T(8,128)}, f32[16,256]{1,0:T(8,128)S(1)}, u32[]{:S(2)}, u32[]{:S(2)}) collective-permute-start(f32[16,256]{1,0:T(8,128)} %slopes_hbm.1), channel_id=1, source_target_pairs={{0,16},{32,48},{64,80},{96,112},{128,144},{160,176},{192,208},{224... | collective-permute-start | bytes 49160 | tf_op jit(solution)/shard_map/ppermute | solution.py:20
  6.9 1.8 %select.1 = (bf16[768,512]{1,0:T(8,128)(2,1)S(1)}, f32[128,128]{1,0:T(8,128)S(1)}, f32[128,128]{1,0:T(8,128)S(1)}, f32[1,16]{1,0:T(1,128)S(1)}, f32[4,48,128]{2,...) custom-call(s32[1,512]{1,0:T(1,128)} %bitcast.4, ...), custom_call_target="tpu_custom_call" | custom-call | flops 10000000 | bytes 5000000 | tf_op jit(solution)/shard_map/select/pallas_call | solution.py:272
  8.6 0.0 collective-permute-done.1.odd_ref
  8.6 0.0 collective-permute-done.even_ref
  8.7 1.5 %predict.1 = f32[4,176,128]{2,1,0:T(8,128)S(1)} custom-call(f32[16,256]{1,0:T(8,128)S(1)} %collective-permute-done.even_ref, f32[16,256]{1,0:T(8,128)S(1)} %collective-permute-done.1.odd_ref, f32[16,512]{1,0:T(8,128)S(1)} %get-tuple-element.20.own_coef_ref, bf16[768,512]{1,0:T(8,128)(2,1)S(1)} %get-tuple-element.21.hot_ref, ...), custom_call_target="tpu_custom_call" | custom-call | tf_op jit(solution)/shard_map/predict/pallas_call | solution.py:312
  10.2 14.6 %all_to_all.25.parts_ref = f32[4,176,128]{2,1,0:T(8,128)S(1)} all-to-all(f32[4,176,128]{2,1,0:T(8,128)S(1)} %predict.1), channel_id=1, replica_groups={{0,1,2,3},{4,5,6,7},{8,9,10,11},{12,13,14,15},{18,19,20,21},{22,23,24,2..., dimensions={0} | all-to-all | bytes 720896 | tf_op jit(solution)/shard_map/all_to_all | solution.py:47
  24.7 0.3 gather.1
  25.1 21.2 %all_to_all.26.parts_ref = f32[2,192,128]{2,1,0:T(8,128)S(1)} all-to-all(f32[2,192,128]{2,1,0:T(8,128)S(1)} %gather.1), channel_id=1, replica_groups={{0,4},{1,5},{2,6},{3,7},{8,12},{9,13},{10,14},{11,15},{18,30},{19,31},{..., dimensions={0} | all-to-all | bytes 393216 | tf_op jit(solution)/shard_map/all_to_all | solution.py:47
  46.3 10.9 %all_to_all.27.parts_ref = f32[2,160,128]{2,1,0:T(8,128)S(1)} all-to-all(f32[2,160,128]{2,1,0:T(8,128)S(1)} %relay.1), channel_id=1, replica_groups={{0,12},{1,13},{2,14},{3,15},{8,4},{9,5},{10,6},{11,7},{18,22},{19,23},{..., dimensions={0} | all-to-all | bytes 327680 | tf_op jit(solution)/shard_map/all_to_all | solution.py:47
  57.2 10.1 %all_to_all.28.back_ref = f32[4,128,128]{2,1,0:T(8,128)S(1)} all-to-all(f32[4,128,128]{2,1,0:T(8,128)S(1)} %get-tuple-element.26), channel_id=1, replica_groups={{0,1,2,3},{4,5,6,7},{8,9,10,11},{12,13,14,15},{18,19,20,21},{22,23,24,2..., dimensions={0} | all-to-all | bytes 524288 | tf_op jit(solution)/shard_map/all_to_all | solution.py:47
  67.3 2.1 %gradient.1 = (f32[32,2,128]{2,1,0:T(2,128)}, f32[512,128]{1,0:T(8,128)S(1)}) custom-call(bf16[16,512,128]{2,1,0:T(8,128)(2,1)S(1)} %get-tuple-element.19.design_ref, f32[4,128,128]{2,1,0:T(8,128)S(1)} %all_to_all.28.back_ref), custom_call_target="tpu_custom_call" | custom-call | tf_op jit(solution)/shard_map/gradient/pallas_call | solution.py:352
  69.3 8.4 %all-to-all-start.4 = ((f32[32,2,128]{2,1,0:T(2,128)}), f32[32,2,128]{2,1,0:T(2,128)S(1)}, u32[]{:S(2)}, u32[]{:S(2)}) async-start(f32[32,2,128]{2,1,0:T(2,128)} %get-tuple-element.27), calls=%async_computation.4 | async-start | bytes 65536 | tf_op jit(solution)/shard_map/all_to_all | solution.py:47
  77.7 0.3 group.1
  78.1 2.1 %collective-permute-start.2 = (f32[16,256]{1,0:T(8,128)S(1)}, f32[16,256]{1,0:T(8,128)S(1)}, u32[]{:S(2)}, u32[]{:S(2)}) collective-permute-start(f32[16,256]{1,0:T(8,128)S(1)} %get-tuple-element.32), channel_id=1, source_target_pairs={{0,16},{32,48},{64,80},{96,112},{128,144},{160,176},{192,208},{224... | collective-permute-start | bytes 49160 | tf_op jit(solution)/shard_map/ppermute | solution.py:20
  80.2 4.8 %collective-permute-start.3 = (f32[16,256]{1,0:T(8,128)S(1)}, f32[16,256]{1,0:T(8,128)S(1)}, u32[]{:S(2)}, u32[]{:S(2)}) collective-permute-start(f32[16,256]{1,0:T(8,128)S(1)} %get-tuple-element.33), channel_id=1, source_target_pairs={{16,32},{48,64},{80,96},{112,128},{144,160},{176,192},{208,224},{2... | collective-permute-start | bytes 49160 | tf_op jit(solution)/shard_map/ppermute | solution.py:20
  85.0 0.0 collective-permute-done.2.even_ref
  85.0 2.3 %collective-permute-done.3.odd_ref = f32[16,256]{1,0:T(8,128)S(1)} collective-permute-done((f32[16,256]{1,0:T(8,128)S(1)}, f32[16,256]{1,0:T(8,128)S(1)}, u32[]{:S(2)}, u32[]{:S(2)}) %collective-permute-start.3) | collective-permute-done | bytes 16416 | tf_op jit(solution)/shard_map/ppermute | solution.py:20
  87.3 0.0 all-to-all-done.4.fixed_all_ref
  87.3 0.6 finish.1
  (2 shorter events, 0.1 us)
Async XLA Ops:
  0.6 8.0 %collective-permute-start.1 = (f32[16,256]{1,0:T(8,128)}, f32[16,256]{1,0:T(8,128)S(1)}, u32[]{:S(2)}, u32[]{:S(2)}) collective-permute-start(f32[16,256]{1,0:T(8,128)} %slopes_hbm.1), channel_id=1, source_target_pairs={{16,32},{48,64},{80,96},{112,128},{144,160},{176,192},{208,224},{2... | collective-permute-start | bytes 49160 | tf_op jit(solution)/shard_map/ppermute | solution.py:20
  4.9 3.7 %collective-permute-start = (f32[16,256]{1,0:T(8,128)}, f32[16,256]{1,0:T(8,128)S(1)}, u32[]{:S(2)}, u32[]{:S(2)}) collective-permute-start(f32[16,256]{1,0:T(8,128)} %slopes_hbm.1), channel_id=1, source_target_pairs={{0,16},{32,48},{64,80},{96,112},{128,144},{160,176},{192,208},{224... | collective-permute-start | bytes 49160 | tf_op jit(solution)/shard_map/ppermute | solution.py:20
  69.3 18.0 %all-to-all-start.4 = ((f32[32,2,128]{2,1,0:T(2,128)}), f32[32,2,128]{2,1,0:T(2,128)S(1)}, u32[]{:S(2)}, u32[]{:S(2)}) async-start(f32[32,2,128]{2,1,0:T(2,128)} %get-tuple-element.27), calls=%async_computation.4 | async-start | bytes 65536 | tf_op jit(solution)/shard_map/all_to_all | solution.py:47
  78.1 6.9 %collective-permute-start.2 = (f32[16,256]{1,0:T(8,128)S(1)}, f32[16,256]{1,0:T(8,128)S(1)}, u32[]{:S(2)}, u32[]{:S(2)}) collective-permute-start(f32[16,256]{1,0:T(8,128)S(1)} %get-tuple-element.32), channel_id=1, source_target_pairs={{0,16},{32,48},{64,80},{96,112},{128,144},{160,176},{192,208},{224... | collective-permute-start | bytes 49160 | tf_op jit(solution)/shard_map/ppermute | solution.py:20
  80.2 7.2 %collective-permute-start.3 = (f32[16,256]{1,0:T(8,128)S(1)}, f32[16,256]{1,0:T(8,128)S(1)}, u32[]{:S(2)}, u32[]{:S(2)}) collective-permute-start(f32[16,256]{1,0:T(8,128)S(1)} %get-tuple-element.33), channel_id=1, source_target_pairs={{16,32},{48,64},{80,96},{112,128},{144,160},{176,192},{208,224},{2... | collective-permute-start | bytes 49160 | tf_op jit(solution)/shard_map/ppermute | solution.py:20

commit v9 on v8

--- a/solution.py
+++ b/solution.py
@@ -39,7 +39,9 @@
         near += [members[i : i + NEAR] for i in range(0, covs, NEAR)]
         for i in (0, 2):
             for pairs, partner in zip((first, second), far_partners(i, row % 2)):
-                pairs += [[members[i * NEAR + j], members[partner * NEAR + j]] for j in range(NEAR)]
+                for j in range(NEAR):
+                    a, b = members[i * NEAR + j], members[partner * NEAR + j]
+                    pairs += [(a, b), (b, a)]
     return near, first, second
 
 
@@ -160,10 +162,10 @@
     lax.fori_loop(0, NEAR, chunk, 0)
 
 
-def gather_kernel(parts_ref, out_ref, prior_ref):
+def gather_kernel(parts_ref, keep_ref, send_ref, prior_ref):
     groups = prior_ref.shape[1]
     halves = groups // LANES
-    size = out_ref.shape[1] - parts_ref.shape[1]
+    size = keep_ref.shape[0] - parts_ref.shape[1]
     rows = parts_ref.shape[1] - size * (halves + 1)
     total = jnp.sum(parts_ref[:, :rows, :], axis=0)
     columns = [
@@ -180,39 +182,33 @@
     place, shift = place_along_cov()
     near, group = lax.rem(place, NEAR), place // NEAR
     odd = lax.rem(lax.axis_index("rows"), 2)
-    parity = lax.rem(group, 2)
     partner, _ = far_partners(group, odd)
     pieces = LANES // size
-    for k in range(out_ref.shape[0]):
-        target = jnp.where(parity == k, group, partner)
+    for ref, target in ((keep_ref, group), (send_ref, partner)):
         _, beyond = far_partners(target, odd)
-        out_ref[k, :rows, :] = total
+        ref[:rows, :] = total
         for at, member in ((rows, target), (rows + halves * size, beyond)):
             cov = lax.rem(member * NEAR + near + shift, lax.axis_size("cov"))
             piece = lax.rem(lax.rem(cov, pieces) + cov // pieces, pieces)
             part = prior_ref[pl.ds(pl.multiple_of(piece * size, size), size), :]
-            out_ref[k, at : at + halves * size, :] = in_rows(part)
-
-
-def relay_kernel(parts_ref, out_ref):
-    rows = 2 * out_ref.shape[1] - parts_ref.shape[1]
-    size = out_ref.shape[1] - rows
-    total = jnp.sum(parts_ref[...], axis=0)
-    place, _ = place_along_cov()
-    parity = lax.rem(place // NEAR, 2)
-    for k in range(out_ref.shape[0]):
-        out_ref[k, :rows, :] = total[:rows]
-        out_ref[k, rows:, :] = jnp.where(
-            parity == k, total[rows : rows + size], total[rows + size :]
-        )
-
-
-def residual_kernel(parts_ref, label_ref, valid_ref, out_ref, prior_ref):
+            ref[at : at + halves * size, :] = in_rows(part)
+
+
+def relay_kernel(kept_ref, received_ref, keep_ref, send_ref):
+    rows = 2 * keep_ref.shape[0] - kept_ref.shape[0]
+    last = keep_ref.shape[0]
+    total = kept_ref[...] + received_ref[...]
+    keep_ref[...] = total[:last]
+    send_ref[:rows, :] = total[:rows]
+    send_ref[rows:, :] = total[last:]
+
+
+def residual_kernel(kept_ref, received_ref, label_ref, valid_ref, out_ref, prior_ref):
     rows = label_ref.shape[0]
-    logits = jnp.sum(parts_ref[:, :rows, :], axis=0)
-    residual = jnp.where(valid_ref[...] > 0.5, label_ref[...] - jax.nn.sigmoid(logits), 0.0)
+    total = kept_ref[...] + received_ref[...]
+    residual = jnp.where(valid_ref[...] > 0.5, label_ref[...] - jax.nn.sigmoid(total[:rows]), 0.0)
     out_ref[...] = jnp.broadcast_to(residual[None], out_ref.shape)
-    prior_ref[...] = jnp.sum(parts_ref[:, rows:, :], axis=0)
+    prior_ref[...] = total[rows:]
 
 
 def gradient_kernel(design_ref, back_ref, fixed_ref, grad_ref):
@@ -320,33 +316,33 @@
     )(from_even, from_odd, own_coefs, hot, spread_hot, design_here, prior_rows)
 
     received = exchange(partial, ("rows", "cov"), near_groups)
-    spread = pl.pallas_call(
+    kept, sent = pl.pallas_call(
         gather_kernel,
-        out_shape=shape(2, share + 2 * slope_rows, LANES),
+        out_shape=(shape(share + 2 * slope_rows, LANES),) * 2,
         in_specs=[VMEM],
-        out_specs=VMEM,
+        out_specs=(VMEM, VMEM),
         scratch_shapes=[pltpu.VMEM((LANES, group_count), f32)],
         compiler_params=ROOM,
         name="gather",
     )(received)
-    received = exchange(spread, ("rows", "cov"), first_pairs)
-    spread = pl.pallas_call(
+    received = lax.ppermute(sent, ("rows", "cov"), first_pairs)
+    kept, sent = pl.pallas_call(
         relay_kernel,
-        out_shape=shape(2, share + slope_rows, LANES),
-        in_specs=[VMEM],
-        out_specs=VMEM,
+        out_shape=(shape(share + slope_rows, LANES),) * 2,
+        in_specs=[VMEM] * 2,
+        out_specs=(VMEM, VMEM),
         compiler_params=ROOM,
         name="relay",
-    )(received)
-    received = exchange(spread, ("rows", "cov"), second_pairs)
+    )(kept, received)
+    received = lax.ppermute(sent, ("rows", "cov"), second_pairs)
     spread, prior = pl.pallas_call(
         residual_kernel,
         out_shape=(shape(NEAR, share, LANES), shape(slope_rows, LANES)),
-        in_specs=[VMEM] * 3,
+        in_specs=[VMEM] * 4,
         out_specs=(VMEM, VMEM),
         compiler_params=ROOM,
         name="residual",
-    )(received, label, valid)
+    )(kept, received, label, valid)
     back = exchange(spread, ("rows", "cov"), near_groups)
 
     fixed_parts, grads = pl.pallas_call(

time: 89.1 us -> 85.6 us (0.961)
  blocking collectives: 56.7 us -> 25.9 us
  starting transfers between devices: 21.5 us -> 36.5 us
  waiting for transfers between devices: 2.33 us -> 14.7 us
    all_to_all x4 -> x2, blocking collectives: 56.7 us -> 25.9 us  [exchange(): lax.all_to_all(parts, axis, 0, 0, tiled=True, axis_index_groups=groups)]
    ppermute x0 -> x2, starting transfers between devices: none -> 16.4 us  [the longest x1 10.1 us: body(): received = lax.ppermute(sent, ('rows', 'cov'), first_pairs)]
    ppermute x0 -> x2, waiting for transfers between devices: none -> 12.4 us  [the longest x1 7.18 us: body(): received = lax.ppermute(sent, ('rows', 'cov'), first_pairs)]
    all_to_all x1, starting transfers between devices: 8.4 us -> 6.96 us  [exchange(): lax.all_to_all(parts, axis, 0, 0, tiled=True, axis_index_groups=groups)]
  transfers between devices with their start and end apart: 5 -> 7, of which waited for: 1 -> 3; matrix products, arithmetic and copies ran while one was open for 0% -> 0% of each run, Pallas kernels for 2% -> 3%
where the time goes in v9:
time: 85.6 us; the launch traced here: 84.4 us
  starting transfers between devices  36.5 us (43%)
  blocking collectives  25.9 us (30%)
  waiting for transfers between devices  14.7 us (17%)
  Pallas kernels  6.63 us (8%)
    all_to_all x2, blocking collectives, exchange(): lax.all_to_all(parts, axis, 0, 0, tiled=True, axis_index_groups=groups)  25.9 us
    ppermute x4, starting transfers between devices, swap(): return lax.ppermute(shard, axis, pairs + [(j, i) for i, j in pairs])  13.1 us
    ppermute x1, starting transfers between devices, body(): received = lax.ppermute(sent, ('rows', 'cov'), first_pairs)  10.1 us
    ppermute x1, waiting for transfers between devices, body(): received = lax.ppermute(sent, ('rows', 'cov'), first_pairs)  7.18 us
    all_to_all x1, starting transfers between devices, exchange(): lax.all_to_all(parts, axis, 0, 0, tiled=True, axis_index_groups=groups)  6.96 us
    ppermute x1, starting transfers between devices, body(): received = lax.ppermute(sent, ('rows', 'cov'), second_pairs)  6.29 us
    ppermute x1, waiting for transfers between devices, body(): received = lax.ppermute(sent, ('rows', 'cov'), second_pairs)  5.19 us
    ppermute x4, waiting for transfers between devices, swap(): return lax.ppermute(shard, axis, pairs + [(j, i) for i, j in pairs])  2.33 us
  transfers between devices with their start and end apart: 7, of which 3 were waited for; matrix products, arithmetic and copies ran while one was open for 0% of the time, Pallas kernels for 3%

profile of v9, /device:TPU:24, one launch (start us, length us, event | category | flops | bytes accessed | tf_op | source)
XLA Modules:
  0.0 84.4 jit_solution(13165556493497991725)
XLA Ops:
  0.6 4.3 %collective-permute-start.1 = (f32[16,256]{1,0:T(8,128)}, f32[16,256]{1,0:T(8,128)S(1)}, u32[]{:S(2)}, u32[]{:S(2)}) collective-permute-start(f32[16,256]{1,0:T(8,128)} %slopes_hbm.1), channel_id=1, source_target_pairs={{16,32},{48,64},{80,96},{112,128},{144,160},{176,192},{208,224},{2... | collective-permute-start | bytes 49160 | tf_op jit(solution)/shard_map/ppermute | solution.py:20
  4.9 1.9 %collective-permute-start = (f32[16,256]{1,0:T(8,128)}, f32[16,256]{1,0:T(8,128)S(1)}, u32[]{:S(2)}, u32[]{:S(2)}) collective-permute-start(f32[16,256]{1,0:T(8,128)} %slopes_hbm.1), channel_id=1, source_target_pairs={{0,16},{32,48},{64,80},{96,112},{128,144},{160,176},{192,208},{224... | collective-permute-start | bytes 49160 | tf_op jit(solution)/shard_map/ppermute | solution.py:20
  6.9 1.8 %select.1 = (bf16[768,512]{1,0:T(8,128)(2,1)S(1)}, f32[128,128]{1,0:T(8,128)S(1)}, f32[128,128]{1,0:T(8,128)S(1)}, f32[1,16]{1,0:T(1,128)S(1)}, f32[4,48,128]{2,...) custom-call(s32[1,512]{1,0:T(1,128)} %bitcast.4, ...), custom_call_target="tpu_custom_call" | custom-call | flops 10000000 | bytes 5000000 | tf_op jit(solution)/shard_map/select/pallas_call | solution.py:268
  8.6 0.0 collective-permute-done.1.odd_ref
  8.6 0.0 collective-permute-done.even_ref
  8.7 1.5 %predict.1 = f32[4,176,128]{2,1,0:T(8,128)S(1)} custom-call(f32[16,256]{1,0:T(8,128)S(1)} %collective-permute-done.even_ref, f32[16,256]{1,0:T(8,128)S(1)} %collective-permute-done.1.odd_ref, f32[16,512]{1,0:T(8,128)S(1)} %get-tuple-element.24.own_coef_ref, bf16[768,512]{1,0:T(8,128)(2,1)S(1)} %get-tuple-element.25.hot_ref, ...), custom_call_target="tpu_custom_call" | custom-call | tf_op jit(solution)/shard_map/predict/pallas_call | solution.py:308
  10.2 14.6 %all_to_all.15.parts_ref = f32[4,176,128]{2,1,0:T(8,128)S(1)} all-to-all(f32[4,176,128]{2,1,0:T(8,128)S(1)} %predict.1), channel_id=1, replica_groups={{0,1,2,3},{4,5,6,7},{8,9,10,11},{12,13,14,15},{18,19,20,21},{22,23,24,2..., dimensions={0} | all-to-all | bytes 720896 | tf_op jit(solution)/shard_map/all_to_all | solution.py:49
  24.7 0.3 gather.1
  25.1 10.1 %collective-permute-start.2 = (f32[192,128]{1,0:T(8,128)S(1)}, f32[192,128]{1,0:T(8,128)S(1)}, u32[]{:S(2)}, u32[]{:S(2)}) collective-permute-start(f32[192,128]{1,0:T(8,128)S(1)} %get-tuple-element.29), channel_id=1, source_target_pairs={{0,4},{4,0},{1,5},{5,1},{2,6},{6,2},{3,7},{7,3},{8,12},{12,8},{9,1... | collective-permute-start | bytes 294920 | tf_op jit(solution)/shard_map/ppermute | solution.py:328
  35.2 7.2 %collective-permute-done.2.received_ref = f32[192,128]{1,0:T(8,128)S(1)} collective-permute-done((f32[192,128]{1,0:T(8,128)S(1)}, f32[192,128]{1,0:T(8,128)S(1)}, u32[]{:S(2)}, u32[]{:S(2)}) %collective-permute-start.2) | collective-permute-done | bytes 98336 | tf_op jit(solution)/shard_map/ppermute | solution.py:328
  42.4 6.3 %collective-permute-start.3 = (f32[160,128]{1,0:T(8,128)S(1)}, f32[160,128]{1,0:T(8,128)S(1)}, u32[]{:S(2)}, u32[]{:S(2)}) collective-permute-start(f32[160,128]{1,0:T(8,128)S(1)} %get-tuple-element.31), channel_id=1, source_target_pairs={{0,12},{12,0},{1,13},{13,1},{2,14},{14,2},{3,15},{15,3},{8,4},{4,8... | collective-permute-start | bytes 245768 | tf_op jit(solution)/shard_map/ppermute | solution.py:337
  48.7 5.2 %collective-permute-done.3.received_ref = f32[160,128]{1,0:T(8,128)S(1)} collective-permute-done((f32[160,128]{1,0:T(8,128)S(1)}, f32[160,128]{1,0:T(8,128)S(1)}, u32[]{:S(2)}, u32[]{:S(2)}) %collective-permute-start.3) | collective-permute-done | bytes 81952 | tf_op jit(solution)/shard_map/ppermute | solution.py:337
  53.9 11.3 %all_to_all.16.back_ref = f32[4,128,128]{2,1,0:T(8,128)S(1)} all-to-all(f32[4,128,128]{2,1,0:T(8,128)S(1)} %get-tuple-element.34), channel_id=1, replica_groups={{0,1,2,3},{4,5,6,7},{8,9,10,11},{12,13,14,15},{18,19,20,21},{22,23,24,2..., dimensions={0} | all-to-all | bytes 524288 | tf_op jit(solution)/shard_map/all_to_all | solution.py:49
  65.2 2.0 %gradient.1 = (f32[32,2,128]{2,1,0:T(2,128)}, f32[512,128]{1,0:T(8,128)S(1)}) custom-call(bf16[16,512,128]{2,1,0:T(8,128)(2,1)S(1)} %get-tuple-element.23.design_ref, f32[4,128,128]{2,1,0:T(8,128)S(1)} %all_to_all.16.back_ref), custom_call_target="tpu_custom_call" | custom-call | tf_op jit(solution)/shard_map/gradient/pallas_call | solution.py:348
  67.3 7.0 %all-to-all-start.2 = ((f32[32,2,128]{2,1,0:T(2,128)}), f32[32,2,128]{2,1,0:T(2,128)S(1)}, u32[]{:S(2)}, u32[]{:S(2)}) async-start(f32[32,2,128]{2,1,0:T(2,128)} %get-tuple-element.35), calls=%async_computation.2 | async-start | bytes 65536 | tf_op jit(solution)/shard_map/all_to_all | solution.py:49
  74.2 0.3 group.1
  74.6 2.1 %collective-permute-start.4 = (f32[16,256]{1,0:T(8,128)S(1)}, f32[16,256]{1,0:T(8,128)S(1)}, u32[]{:S(2)}, u32[]{:S(2)}) collective-permute-start(f32[16,256]{1,0:T(8,128)S(1)} %get-tuple-element.40), channel_id=1, source_target_pairs={{0,16},{32,48},{64,80},{96,112},{128,144},{160,176},{192,208},{224... | collective-permute-start | bytes 49160 | tf_op jit(solution)/shard_map/ppermute | solution.py:20
  76.7 4.8 %collective-permute-start.5 = (f32[16,256]{1,0:T(8,128)S(1)}, f32[16,256]{1,0:T(8,128)S(1)}, u32[]{:S(2)}, u32[]{:S(2)}) collective-permute-start(f32[16,256]{1,0:T(8,128)S(1)} %get-tuple-element.41), channel_id=1, source_target_pairs={{16,32},{48,64},{80,96},{112,128},{144,160},{176,192},{208,224},{2... | collective-permute-start | bytes 49160 | tf_op jit(solution)/shard_map/ppermute | solution.py:20
  81.5 0.0 collective-permute-done.4.even_ref
  81.5 2.3 %collective-permute-done.5.odd_ref = f32[16,256]{1,0:T(8,128)S(1)} collective-permute-done((f32[16,256]{1,0:T(8,128)S(1)}, f32[16,256]{1,0:T(8,128)S(1)}, u32[]{:S(2)}, u32[]{:S(2)}) %collective-permute-start.5) | collective-permute-done | bytes 16416 | tf_op jit(solution)/shard_map/ppermute | solution.py:20
  83.8 0.0 all-to-all-done.2.fixed_all_ref
  83.8 0.6 finish.1
  (2 shorter events, 0.0 us)
Async XLA Ops:
  0.6 8.0 %collective-permute-start.1 = (f32[16,256]{1,0:T(8,128)}, f32[16,256]{1,0:T(8,128)S(1)}, u32[]{:S(2)}, u32[]{:S(2)}) collective-permute-start(f32[16,256]{1,0:T(8,128)} %slopes_hbm.1), channel_id=1, source_target_pairs={{16,32},{48,64},{80,96},{112,128},{144,160},{176,192},{208,224},{2... | collective-permute-start | bytes 49160 | tf_op jit(solution)/shard_map/ppermute | solution.py:20
  4.9 3.7 %collective-permute-start = (f32[16,256]{1,0:T(8,128)}, f32[16,256]{1,0:T(8,128)S(1)}, u32[]{:S(2)}, u32[]{:S(2)}) collective-permute-start(f32[16,256]{1,0:T(8,128)} %slopes_hbm.1), channel_id=1, source_target_pairs={{0,16},{32,48},{64,80},{96,112},{128,144},{160,176},{192,208},{224... | collective-permute-start | bytes 49160 | tf_op jit(solution)/shard_map/ppermute | solution.py:20
  25.1 17.3 %collective-permute-start.2 = (f32[192,128]{1,0:T(8,128)S(1)}, f32[192,128]{1,0:T(8,128)S(1)}, u32[]{:S(2)}, u32[]{:S(2)}) collective-permute-start(f32[192,128]{1,0:T(8,128)S(1)} %get-tuple-element.29), channel_id=1, source_target_pairs={{0,4},{4,0},{1,5},{5,1},{2,6},{6,2},{3,7},{7,3},{8,12},{12,8},{9,1... | collective-permute-start | bytes 294920 | tf_op jit(solution)/shard_map/ppermute | solution.py:328
  42.4 11.5 %collective-permute-start.3 = (f32[160,128]{1,0:T(8,128)S(1)}, f32[160,128]{1,0:T(8,128)S(1)}, u32[]{:S(2)}, u32[]{:S(2)}) collective-permute-start(f32[160,128]{1,0:T(8,128)S(1)} %get-tuple-element.31), channel_id=1, source_target_pairs={{0,12},{12,0},{1,13},{13,1},{2,14},{14,2},{3,15},{15,3},{8,4},{4,8... | collective-permute-start | bytes 245768 | tf_op jit(solution)/shard_map/ppermute | solution.py:337
  67.3 16.6 %all-to-all-start.2 = ((f32[32,2,128]{2,1,0:T(2,128)}), f32[32,2,128]{2,1,0:T(2,128)S(1)}, u32[]{:S(2)}, u32[]{:S(2)}) async-start(f32[32,2,128]{2,1,0:T(2,128)} %get-tuple-element.35), calls=%async_computation.2 | async-start | bytes 65536 | tf_op jit(solution)/shard_map/all_to_all | solution.py:49
  74.6 6.9 %collective-permute-start.4 = (f32[16,256]{1,0:T(8,128)S(1)}, f32[16,256]{1,0:T(8,128)S(1)}, u32[]{:S(2)}, u32[]{:S(2)}) collective-permute-start(f32[16,256]{1,0:T(8,128)S(1)} %get-tuple-element.40), channel_id=1, source_target_pairs={{0,16},{32,48},{64,80},{96,112},{128,144},{160,176},{192,208},{224... | collective-permute-start | bytes 49160 | tf_op jit(solution)/shard_map/ppermute | solution.py:20
  76.7 7.2 %collective-permute-start.5 = (f32[16,256]{1,0:T(8,128)S(1)}, f32[16,256]{1,0:T(8,128)S(1)}, u32[]{:S(2)}, u32[]{:S(2)}) collective-permute-start(f32[16,256]{1,0:T(8,128)S(1)} %get-tuple-element.41), channel_id=1, source_target_pairs={{16,32},{48,64},{80,96},{112,128},{144,160},{176,192},{208,224},{2... | collective-permute-start | bytes 49160 | tf_op jit(solution)/shard_map/ppermute | solution.py:20

commit v10 on v9

--- a/solution.py
+++ b/solution.py
@@ -88,7 +88,15 @@
         pltpu.make_async_copy(outcome_hbm.at[pl.ds(start, rows)], outcome_ref, sems.at[3]),
         pltpu.make_async_copy(fill_hbm, fill_ref, sems.at[4]),
         pltpu.make_async_copy(fixed_hbm, fixed_ref, sems.at[5]),
-        pltpu.make_async_copy(design_hbm, design_ref, sems.at[6]),
+    ]
+    quarter = size // 4
+    copies += [
+        pltpu.make_async_copy(
+            design_hbm.at[pl.ds(i * quarter, quarter)],
+            design_ref.at[pl.ds(i * quarter, quarter)],
+            sems.at[6 + i],
+        )
+        for i in range(4)
     ]
     for copy in copies:
         copy.start()
@@ -127,7 +135,8 @@
     lane = lax.broadcasted_iota(jnp.int32, (rows, LANES), 1).astype(f32)
     valid_ref[...] = (lane < column).astype(f32)
     label_ref[...] = outcome_ref[...].astype(f32)
-    copies[6].wait()
+    for copy in copies[6:]:
+        copy.wait()
 
 
 def predict_kernel(
@@ -145,21 +154,24 @@
     padded = jnp.concatenate([parts, jnp.zeros((LANES - 3 * size, blocks), f32)], axis=0)
     coef_ref[...] = padded.T.astype(bf16)
 
-    def chunk(peer, carry):
-        start = pl.multiple_of(peer * share, share)
-        here = coef_ref[pl.ds(start, share), :]
-        total = jnp.zeros((share, LANES), f32)
+    step = 2 * share
+
+    def chunk(i, carry):
+        start = pl.multiple_of(i * step, step)
+        here = coef_ref[pl.ds(start, step), :]
+        total = jnp.zeros((step, LANES), f32)
         for p in range(0, size, 2):
             wide = jnp.dot(
                 here, spread_ref[:, p * LANES : (p + 2) * LANES], preferred_element_type=f32
             )
-            total = total + wide[:, :LANES] * design_ref[p, pl.ds(start, share), :].astype(f32)
-            total = total + wide[:, LANES:] * design_ref[p + 1, pl.ds(start, share), :].astype(f32)
-        out_ref[peer, :share, :] = total
-        out_ref[peer, share:, :] = prior_ref[peer]
+            total = total + wide[:, :LANES] * design_ref[p, pl.ds(start, step), :].astype(f32)
+            total = total + wide[:, LANES:] * design_ref[p + 1, pl.ds(start, step), :].astype(f32)
+        for k in range(2):
+            out_ref[2 * i + k, :share, :] = total[k * share : (k + 1) * share]
+            out_ref[2 * i + k, share:, :] = prior_ref[2 * i + k]
         return carry
 
-    lax.fori_loop(0, NEAR, chunk, 0)
+    lax.fori_loop(0, NEAR // 2, chunk, 0)
 
 
 def gather_kernel(parts_ref, keep_ref, send_ref, prior_ref):
@@ -285,7 +297,7 @@
             pltpu.VMEM((share, LANES), jnp.int32),
             pltpu.VMEM((size, group_count), f32),
             pltpu.VMEM((size, covs * size), f32),
-            pltpu.SemaphoreType.DMA((7,)),
+            pltpu.SemaphoreType.DMA((10,)),
         ],
         compiler_params=ROOM,
         cost_estimate=cost(10_000_000, 5_000_000),

time: 85.6 us -> 85.2 us (level)
  transfers between devices with their start and end apart: 7 -> 7, of which waited for: 3 -> 3; matrix products, arithmetic and copies ran while one was open for 0% -> 0% of each run, Pallas kernels for 3% -> 2%
where the time goes in v10:
time: 85.2 us; the launch traced here: 84.1 us
  starting transfers between devices  36.4 us (43%)
  blocking collectives  26 us (31%)
  waiting for transfers between devices  14.7 us (17%)
  Pallas kernels  6.27 us (7%)
    all_to_all x2, blocking collectives, exchange(): lax.all_to_all(parts, axis, 0, 0, tiled=True, axis_index_groups=groups)  26 us
    ppermute x4, starting transfers between devices, swap(): return lax.ppermute(shard, axis, pairs + [(j, i) for i, j in pairs])  13.1 us
    ppermute x1, starting transfers between devices, body(): received = lax.ppermute(sent, ('rows', 'cov'), first_pairs)  10.1 us
    ppermute x1, waiting for transfers between devices, body(): received = lax.ppermute(sent, ('rows', 'cov'), first_pairs)  7.18 us
    all_to_all x1, starting transfers between devices, exchange(): lax.all_to_all(parts, axis, 0, 0, tiled=True, axis_index_groups=groups)  6.89 us
    ppermute x1, starting transfers between devices, body(): received = lax.ppermute(sent, ('rows', 'cov'), second_pairs)  6.29 us
    ppermute x1, waiting for transfers between devices, body(): received = lax.ppermute(sent, ('rows', 'cov'), second_pairs)  5.2 us
    ppermute x4, waiting for transfers between devices, swap(): return lax.ppermute(shard, axis, pairs + [(j, i) for i, j in pairs])  2.33 us
  transfers between devices with their start and end apart: 7, of which 3 were waited for; matrix products, arithmetic and copies ran while one was open for 0% of the time, Pallas kernels for 2%

profile of v10, /device:TPU:24, one launch (start us, length us, event | category | flops | bytes accessed | tf_op | source)
XLA Modules:
  0.0 84.1 jit_solution(7273006502921047749)
XLA Ops:
  0.6 4.3 %collective-permute-start.1 = (f32[16,256]{1,0:T(8,128)}, f32[16,256]{1,0:T(8,128)S(1)}, u32[]{:S(2)}, u32[]{:S(2)}) collective-permute-start(f32[16,256]{1,0:T(8,128)} %slopes_hbm.1), channel_id=1, source_target_pairs={{16,32},{48,64},{80,96},{112,128},{144,160},{176,192},{208,224},{2... | collective-permute-start | bytes 49160 | tf_op jit(solution)/shard_map/ppermute | solution.py:20
  4.9 1.9 %collective-permute-start = (f32[16,256]{1,0:T(8,128)}, f32[16,256]{1,0:T(8,128)S(1)}, u32[]{:S(2)}, u32[]{:S(2)}) collective-permute-start(f32[16,256]{1,0:T(8,128)} %slopes_hbm.1), channel_id=1, source_target_pairs={{0,16},{32,48},{64,80},{96,112},{128,144},{160,176},{192,208},{224... | collective-permute-start | bytes 49160 | tf_op jit(solution)/shard_map/ppermute | solution.py:20
  6.9 1.7 %select.1 = (bf16[768,512]{1,0:T(8,128)(2,1)S(1)}, f32[128,128]{1,0:T(8,128)S(1)}, f32[128,128]{1,0:T(8,128)S(1)}, f32[1,16]{1,0:T(1,128)S(1)}, f32[4,48,128]{2,...) custom-call(s32[1,512]{1,0:T(1,128)} %bitcast.4, ...), custom_call_target="tpu_custom_call" | custom-call | flops 10000000 | bytes 5000000 | tf_op jit(solution)/shard_map/select/pallas_call | solution.py:280
  8.6 0.0 collective-permute-done.1.odd_ref
  8.6 0.0 collective-permute-done.even_ref
  8.6 1.2 %predict.1 = f32[4,176,128]{2,1,0:T(8,128)S(1)} custom-call(f32[16,256]{1,0:T(8,128)S(1)} %collective-permute-done.even_ref, f32[16,256]{1,0:T(8,128)S(1)} %collective-permute-done.1.odd_ref, f32[16,512]{1,0:T(8,128)S(1)} %get-tuple-element.24.own_coef_ref, bf16[768,512]{1,0:T(8,128)(2,1)S(1)} %get-tuple-element.25.hot_ref, ...), custom_call_target="tpu_custom_call" | custom-call | tf_op jit(solution)/shard_map/predict/pallas_call | solution.py:320
  9.8 14.6 %all_to_all.15.parts_ref = f32[4,176,128]{2,1,0:T(8,128)S(1)} all-to-all(f32[4,176,128]{2,1,0:T(8,128)S(1)} %predict.1), channel_id=1, replica_groups={{0,1,2,3},{4,5,6,7},{8,9,10,11},{12,13,14,15},{18,19,20,21},{22,23,24,2..., dimensions={0} | all-to-all | bytes 720896 | tf_op jit(solution)/shard_map/all_to_all | solution.py:49
  24.4 0.3 gather.1
  24.7 10.1 %collective-permute-start.2 = (f32[192,128]{1,0:T(8,128)S(1)}, f32[192,128]{1,0:T(8,128)S(1)}, u32[]{:S(2)}, u32[]{:S(2)}) collective-permute-start(f32[192,128]{1,0:T(8,128)S(1)} %get-tuple-element.29), channel_id=1, source_target_pairs={{0,4},{4,0},{1,5},{5,1},{2,6},{6,2},{3,7},{7,3},{8,12},{12,8},{9,1... | collective-permute-start | bytes 294920 | tf_op jit(solution)/shard_map/ppermute | solution.py:340
  34.8 7.2 %collective-permute-done.2.received_ref = f32[192,128]{1,0:T(8,128)S(1)} collective-permute-done((f32[192,128]{1,0:T(8,128)S(1)}, f32[192,128]{1,0:T(8,128)S(1)}, u32[]{:S(2)}, u32[]{:S(2)}) %collective-permute-start.2) | collective-permute-done | bytes 98336 | tf_op jit(solution)/shard_map/ppermute | solution.py:340
  42.0 6.3 %collective-permute-start.3 = (f32[160,128]{1,0:T(8,128)S(1)}, f32[160,128]{1,0:T(8,128)S(1)}, u32[]{:S(2)}, u32[]{:S(2)}) collective-permute-start(f32[160,128]{1,0:T(8,128)S(1)} %get-tuple-element.31), channel_id=1, source_target_pairs={{0,12},{12,0},{1,13},{13,1},{2,14},{14,2},{3,15},{15,3},{8,4},{4,8... | collective-permute-start | bytes 245768 | tf_op jit(solution)/shard_map/ppermute | solution.py:349
  48.3 5.2 %collective-permute-done.3.received_ref = f32[160,128]{1,0:T(8,128)S(1)} collective-permute-done((f32[160,128]{1,0:T(8,128)S(1)}, f32[160,128]{1,0:T(8,128)S(1)}, u32[]{:S(2)}, u32[]{:S(2)}) %collective-permute-start.3) | collective-permute-done | bytes 81952 | tf_op jit(solution)/shard_map/ppermute | solution.py:349
  53.5 11.4 %all_to_all.16.back_ref = f32[4,128,128]{2,1,0:T(8,128)S(1)} all-to-all(f32[4,128,128]{2,1,0:T(8,128)S(1)} %get-tuple-element.34), channel_id=1, replica_groups={{0,1,2,3},{4,5,6,7},{8,9,10,11},{12,13,14,15},{18,19,20,21},{22,23,24,2..., dimensions={0} | all-to-all | bytes 524288 | tf_op jit(solution)/shard_map/all_to_all | solution.py:49
  64.9 2.0 %gradient.1 = (f32[32,2,128]{2,1,0:T(2,128)}, f32[512,128]{1,0:T(8,128)S(1)}) custom-call(bf16[16,512,128]{2,1,0:T(8,128)(2,1)S(1)} %get-tuple-element.23.design_ref, f32[4,128,128]{2,1,0:T(8,128)S(1)} %all_to_all.16.back_ref), custom_call_target="tpu_custom_call" | custom-call | tf_op jit(solution)/shard_map/gradient/pallas_call | solution.py:360
  66.9 6.9 %all-to-all-start.2 = ((f32[32,2,128]{2,1,0:T(2,128)}), f32[32,2,128]{2,1,0:T(2,128)S(1)}, u32[]{:S(2)}, u32[]{:S(2)}) async-start(f32[32,2,128]{2,1,0:T(2,128)} %get-tuple-element.35), calls=%async_computation.2 | async-start | bytes 65536 | tf_op jit(solution)/shard_map/all_to_all | solution.py:49
  73.8 0.3 group.1
  74.2 2.1 %collective-permute-start.4 = (f32[16,256]{1,0:T(8,128)S(1)}, f32[16,256]{1,0:T(8,128)S(1)}, u32[]{:S(2)}, u32[]{:S(2)}) collective-permute-start(f32[16,256]{1,0:T(8,128)S(1)} %get-tuple-element.40), channel_id=1, source_target_pairs={{0,16},{32,48},{64,80},{96,112},{128,144},{160,176},{192,208},{224... | collective-permute-start | bytes 49160 | tf_op jit(solution)/shard_map/ppermute | solution.py:20
  76.3 4.8 %collective-permute-start.5 = (f32[16,256]{1,0:T(8,128)S(1)}, f32[16,256]{1,0:T(8,128)S(1)}, u32[]{:S(2)}, u32[]{:S(2)}) collective-permute-start(f32[16,256]{1,0:T(8,128)S(1)} %get-tuple-element.41), channel_id=1, source_target_pairs={{16,32},{48,64},{80,96},{112,128},{144,160},{176,192},{208,224},{2... | collective-permute-start | bytes 49160 | tf_op jit(solution)/shard_map/ppermute | solution.py:20
  81.1 0.0 collective-permute-done.4.even_ref
  81.1 2.3 %collective-permute-done.5.odd_ref = f32[16,256]{1,0:T(8,128)S(1)} collective-permute-done((f32[16,256]{1,0:T(8,128)S(1)}, f32[16,256]{1,0:T(8,128)S(1)}, u32[]{:S(2)}, u32[]{:S(2)}) %collective-permute-start.5) | collective-permute-done | bytes 16416 | tf_op jit(solution)/shard_map/ppermute | solution.py:20
  83.4 0.0 all-to-all-done.2.fixed_all_ref
  83.4 0.6 finish.1
  (2 shorter events, 0.0 us)
Async XLA Ops:
  0.6 8.0 %collective-permute-start.1 = (f32[16,256]{1,0:T(8,128)}, f32[16,256]{1,0:T(8,128)S(1)}, u32[]{:S(2)}, u32[]{:S(2)}) collective-permute-start(f32[16,256]{1,0:T(8,128)} %slopes_hbm.1), channel_id=1, source_target_pairs={{16,32},{48,64},{80,96},{112,128},{144,160},{176,192},{208,224},{2... | collective-permute-start | bytes 49160 | tf_op jit(solution)/shard_map/ppermute | solution.py:20
  4.9 3.7 %collective-permute-start = (f32[16,256]{1,0:T(8,128)}, f32[16,256]{1,0:T(8,128)S(1)}, u32[]{:S(2)}, u32[]{:S(2)}) collective-permute-start(f32[16,256]{1,0:T(8,128)} %slopes_hbm.1), channel_id=1, source_target_pairs={{0,16},{32,48},{64,80},{96,112},{128,144},{160,176},{192,208},{224... | collective-permute-start | bytes 49160 | tf_op jit(solution)/shard_map/ppermute | solution.py:20
  24.7 17.3 %collective-permute-start.2 = (f32[192,128]{1,0:T(8,128)S(1)}, f32[192,128]{1,0:T(8,128)S(1)}, u32[]{:S(2)}, u32[]{:S(2)}) collective-permute-start(f32[192,128]{1,0:T(8,128)S(1)} %get-tuple-element.29), channel_id=1, source_target_pairs={{0,4},{4,0},{1,5},{5,1},{2,6},{6,2},{3,7},{7,3},{8,12},{12,8},{9,1... | collective-permute-start | bytes 294920 | tf_op jit(solution)/shard_map/ppermute | solution.py:340
  42.0 11.5 %collective-permute-start.3 = (f32[160,128]{1,0:T(8,128)S(1)}, f32[160,128]{1,0:T(8,128)S(1)}, u32[]{:S(2)}, u32[]{:S(2)}) collective-permute-start(f32[160,128]{1,0:T(8,128)S(1)} %get-tuple-element.31), channel_id=1, source_target_pairs={{0,12},{12,0},{1,13},{13,1},{2,14},{14,2},{3,15},{15,3},{8,4},{4,8... | collective-permute-start | bytes 245768 | tf_op jit(solution)/shard_map/ppermute | solution.py:349
  66.9 16.5 %all-to-all-start.2 = ((f32[32,2,128]{2,1,0:T(2,128)}), f32[32,2,128]{2,1,0:T(2,128)S(1)}, u32[]{:S(2)}, u32[]{:S(2)}) async-start(f32[32,2,128]{2,1,0:T(2,128)} %get-tuple-element.35), calls=%async_computation.2 | async-start | bytes 65536 | tf_op jit(solution)/shard_map/all_to_all | solution.py:49
  74.2 6.9 %collective-permute-start.4 = (f32[16,256]{1,0:T(8,128)S(1)}, f32[16,256]{1,0:T(8,128)S(1)}, u32[]{:S(2)}, u32[]{:S(2)}) collective-permute-start(f32[16,256]{1,0:T(8,128)S(1)} %get-tuple-element.40), channel_id=1, source_target_pairs={{0,16},{32,48},{64,80},{96,112},{128,144},{160,176},{192,208},{224... | collective-permute-start | bytes 49160 | tf_op jit(solution)/shard_map/ppermute | solution.py:20
  76.3 7.2 %collective-permute-start.5 = (f32[16,256]{1,0:T(8,128)S(1)}, f32[16,256]{1,0:T(8,128)S(1)}, u32[]{:S(2)}, u32[]{:S(2)}) collective-permute-start(f32[16,256]{1,0:T(8,128)S(1)} %get-tuple-element.41), channel_id=1, source_target_pairs={{16,32},{48,64},{80,96},{112,128},{144,160},{176,192},{208,224},{2... | collective-permute-start | bytes 49160 | tf_op jit(solution)/shard_map/ppermute | solution.py:20

commit v11 on v10

--- a/solution.py
+++ b/solution.py
@@ -33,16 +33,18 @@
 
 def cov_groups():
     covs, rows = lax.axis_size("cov"), lax.axis_size("rows")
-    near, first, second = [], [], []
+    near, first, second, across, beside = [], [], [], [], []
     for row in range(rows):
         members = [row * covs + (c + row % 2 * (NEAR // 2)) % covs for c in range(covs)]
         near += [members[i : i + NEAR] for i in range(0, covs, NEAR)]
+        across += [(m, members[c ^ 2]) for c, m in enumerate(members)]
+        beside += [(m, members[c ^ 1]) for c, m in enumerate(members)]
         for i in (0, 2):
             for pairs, partner in zip((first, second), far_partners(i, row % 2)):
                 for j in range(NEAR):
                     a, b = members[i * NEAR + j], members[partner * NEAR + j]
                     pairs += [(a, b), (b, a)]
-    return near, first, second
+    return near, first, second, across, beside
 
 
 def exchange(parts, axis, groups=None):
@@ -219,26 +221,55 @@
     rows = label_ref.shape[0]
     total = kept_ref[...] + received_ref[...]
     residual = jnp.where(valid_ref[...] > 0.5, label_ref[...] - jax.nn.sigmoid(total[:rows]), 0.0)
-    out_ref[...] = jnp.broadcast_to(residual[None], out_ref.shape)
+    out_ref[...] = residual
     prior_ref[...] = total[rows:]
 
 
-def gradient_kernel(design_ref, back_ref, fixed_ref, grad_ref):
-    size, blocks, _ = design_ref.shape
-    share = blocks // NEAR
+def join_kernel(own_ref, across_ref, out_ref):
+    share = own_ref.shape[0]
+    out_ref[:share, :] = own_ref[...]
+    out_ref[share:, :] = across_ref[...]
+
+
+def block_gradients(design_ref, residual, start):
+    size = design_ref.shape[0]
+    share = residual.shape[0]
     lane = lax.broadcasted_iota(jnp.int32, (share, LANES), 1)
-
-    def chunk(peer, total):
-        start = pl.multiple_of(peer * share, share)
-        residual = back_ref[peer]
-        grads = jnp.zeros((share, LANES), f32)
-        for p in range(size):
-            product = design_ref[p, pl.ds(start, share), :].astype(f32) * residual
-            grads = jnp.where(lane == p, jnp.sum(product, axis=1, keepdims=True), grads)
+    grads = jnp.zeros((share, LANES), f32)
+    for p in range(size):
+        product = design_ref[p, pl.ds(start, share), :].astype(f32) * residual
+        grads = jnp.where(lane == p, jnp.sum(product, axis=1, keepdims=True), grads)
+    return grads
+
+
+def half_kernel(design_ref, residual_ref, grad_ref):
+    share = grad_ref.shape[1]
+    near = lax.rem(place_along_cov()[0], NEAR)
+
+    def chunk(k, carry):
+        start = pl.multiple_of(lax.rem(near + 2 * k, NEAR) * share, share)
+        residual = residual_ref[pl.ds(pl.multiple_of(k * share, share), share), :]
+        grad_ref[k] = block_gradients(design_ref, residual, start)
+        return carry
+
+    lax.fori_loop(0, 2, chunk, 0)
+
+
+def rest_kernel(design_ref, residual_ref, half_ref, fixed_ref, grad_ref):
+    share = half_ref.shape[1]
+    near = lax.rem(place_along_cov()[0], NEAR)
+    beside = near + 1 - 2 * lax.rem(near, 2)
+
+    def chunk(k, total):
+        start = pl.multiple_of(lax.rem(beside + 2 * k, NEAR) * share, share)
+        residual = residual_ref[pl.ds(pl.multiple_of(k * share, share), share), :]
+        grads = block_gradients(design_ref, residual, start)
         grad_ref[pl.ds(start, share), :] = grads
-        return total + jnp.sum(grads, axis=0, keepdims=True)
-
-    total = lax.fori_loop(0, NEAR, chunk, jnp.zeros((1, LANES), f32))
+        half = half_ref[k]
+        grad_ref[pl.ds(pl.multiple_of(lax.rem(near + 2 * k, NEAR) * share, share), share), :] = half
+        return total + jnp.sum(grads + half, axis=0, keepdims=True)
+
+    total = lax.fori_loop(0, 2, chunk, jnp.zeros((1, LANES), f32))
     fixed_ref[...] = jnp.broadcast_to(total[None], fixed_ref.shape)
 
 
@@ -271,7 +302,7 @@
     blocks = block_group.shape[0]
     covs, rows = lax.axis_size("cov"), lax.axis_size("rows")
     share = blocks // NEAR
-    near_groups, first_pairs, second_pairs = cov_groups()
+    near_groups, first_pairs, second_pairs, across_pairs, beside_pairs = cov_groups()
     slope_rows = size * group_count // LANES
 
     from_even = swap(slopes, "rows", 0)
@@ -347,24 +378,41 @@
         name="relay",
     )(kept, received)
     received = lax.ppermute(sent, ("rows", "cov"), second_pairs)
-    spread, prior = pl.pallas_call(
+    residual, prior = pl.pallas_call(
         residual_kernel,
-        out_shape=(shape(NEAR, share, LANES), shape(slope_rows, LANES)),
+        out_shape=(shape(share, LANES), shape(slope_rows, LANES)),
         in_specs=[VMEM] * 4,
         out_specs=(VMEM, VMEM),
         compiler_params=ROOM,
         name="residual",
     )(kept, received, label, valid)
-    back = exchange(spread, ("rows", "cov"), near_groups)
-
+    across = lax.ppermute(residual, ("rows", "cov"), across_pairs)
+    joined = pl.pallas_call(
+        join_kernel,
+        out_shape=shape(2 * share, LANES),
+        in_specs=[VMEM] * 2,
+        out_specs=VMEM,
+        compiler_params=ROOM,
+        name="join",
+    )(residual, across)
+    beside = lax.ppermute(joined, ("rows", "cov"), beside_pairs)
+    half = pl.pallas_call(
+        half_kernel,
+        out_shape=shape(2, share, LANES),
+        in_specs=[VMEM] * 2,
+        out_specs=VMEM,
+        compiler_params=ROOM,
+        cost_estimate=cost(10_000_000, 2_000_000),
+        name="half",
+    )(design_here, joined)
     fixed_parts, grads = pl.pallas_call(
-        gradient_kernel,
+        rest_kernel,
         out_shape=(shape(rows, 2, LANES), shape(blocks, LANES)),
-        in_specs=[VMEM] * 2,
+        in_specs=[VMEM] * 3,
         out_specs=(VMEM,) * 2,
         compiler_params=ROOM,
-        name="gradient",
-    )(design_here, back)
+        name="rest",
+    )(design_here, beside, half)
     fixed_all = exchange(fixed_parts, "rows")
 
     to_even, to_odd, own = pl.pallas_call(

time: 85.2 us -> 86.5 us (1.015)
  blocking collectives: 26 us -> 14.6 us
  waiting for transfers between devices: 14.7 us -> 21.8 us
  starting transfers between devices: 36.4 us -> 41.9 us
    all_to_all x2 -> x1, blocking collectives: 26 us -> 14.6 us  [exchange(): lax.all_to_all(parts, axis, 0, 0, tiled=True, axis_index_groups=groups)]
    ppermute x0 -> x2, waiting for transfers between devices: none -> 7.04 us  [the longest x1 4.58 us: body(): across = lax.ppermute(residual, ('rows', 'cov'), across_pairs)]
    ppermute x0 -> x2, starting transfers between devices: none -> 6.65 us  [the longest x1 4.18 us: body(): beside = lax.ppermute(joined, ('rows', 'cov'), beside_pairs)]
    all_to_all x1, starting transfers between devices: 6.89 us -> 5.71 us  [exchange(): lax.all_to_all(parts, axis, 0, 0, tiled=True, axis_index_groups=groups)]
    pallas_call x2 -> x4, Pallas kernels: 2.07 us -> 2.07 us  [the longest x1 1.33 us: body(): pl.pallas_call(rest_kernel, out_shape=(shape(rows, 2, LANES), shape(block...]
  transfers between devices with their start and end apart: 7 -> 9, of which waited for: 3 -> 5; matrix products, arithmetic and copies ran while one was open for 0% -> 0% of each run, Pallas kernels for 2% -> 3%
where the time goes in v11:
time: 86.5 us; the launch traced here: 85.2 us
  starting transfers between devices  41.9 us (48%)
  waiting for transfers between devices  21.8 us (25%)
  blocking collectives  14.6 us (17%)
  Pallas kernels  6.27 us (7%)
    all_to_all x1, blocking collectives, exchange(): lax.all_to_all(parts, axis, 0, 0, tiled=True, axis_index_groups=groups)  14.6 us
    ppermute x4, starting transfers between devices, swap(): return lax.ppermute(shard, axis, pairs + [(j, i) for i, j in pairs])  13.1 us
    ppermute x1, starting transfers between devices, body(): received = lax.ppermute(sent, ('rows', 'cov'), first_pairs)  10.1 us
    ppermute x1, waiting for transfers between devices, body(): received = lax.ppermute(sent, ('rows', 'cov'), first_pairs)  7.18 us
    ppermute x1, starting transfers between devices, body(): received = lax.ppermute(sent, ('rows', 'cov'), second_pairs)  6.29 us
    all_to_all x1, starting transfers between devices, exchange(): lax.all_to_all(parts, axis, 0, 0, tiled=True, axis_index_groups=groups)  5.71 us
    ppermute x1, waiting for transfers between devices, body(): received = lax.ppermute(sent, ('rows', 'cov'), second_pairs)  5.2 us
    ppermute x1, waiting for transfers between devices, body(): across = lax.ppermute(residual, ('rows', 'cov'), across_pairs)  4.58 us
  transfers between devices with their start and end apart: 9, of which 5 were waited for; matrix products, arithmetic and copies ran while one was open for 0% of the time, Pallas kernels for 3%

profile of v11, /device:TPU:24, one launch (start us, length us, event | category | flops | bytes accessed | tf_op | source)
XLA Modules:
  0.0 85.2 jit_solution(14249607882029956057)
XLA Ops:
  0.6 4.3 %collective-permute-start.1 = (f32[16,256]{1,0:T(8,128)}, f32[16,256]{1,0:T(8,128)S(1)}, u32[]{:S(2)}, u32[]{:S(2)}) collective-permute-start(f32[16,256]{1,0:T(8,128)} %slopes_hbm.1), channel_id=1, source_target_pairs={{16,32},{48,64},{80,96},{112,128},{144,160},{176,192},{208,224},{2... | collective-permute-start | bytes 49160 | tf_op jit(solution)/shard_map/ppermute | solution.py:20
  4.9 1.9 %collective-permute-start = (f32[16,256]{1,0:T(8,128)}, f32[16,256]{1,0:T(8,128)S(1)}, u32[]{:S(2)}, u32[]{:S(2)}) collective-permute-start(f32[16,256]{1,0:T(8,128)} %slopes_hbm.1), channel_id=1, source_target_pairs={{0,16},{32,48},{64,80},{96,112},{128,144},{160,176},{192,208},{224... | collective-permute-start | bytes 49160 | tf_op jit(solution)/shard_map/ppermute | solution.py:20
  6.9 1.7 %select.1 = (bf16[768,512]{1,0:T(8,128)(2,1)S(1)}, f32[128,128]{1,0:T(8,128)S(1)}, f32[128,128]{1,0:T(8,128)S(1)}, f32[1,16]{1,0:T(1,128)S(1)}, f32[4,48,128]{2,...) custom-call(s32[1,512]{1,0:T(1,128)} %bitcast.4, ...), custom_call_target="tpu_custom_call" | custom-call | flops 10000000 | bytes 5000000 | tf_op jit(solution)/shard_map/select/pallas_call | solution.py:311
  8.6 0.0 collective-permute-done.1.odd_ref
  8.6 0.0 collective-permute-done.even_ref
  8.6 1.2 %predict.1 = f32[4,176,128]{2,1,0:T(8,128)S(1)} custom-call(f32[16,256]{1,0:T(8,128)S(1)} %collective-permute-done.even_ref, f32[16,256]{1,0:T(8,128)S(1)} %collective-permute-done.1.odd_ref, f32[16,512]{1,0:T(8,128)S(1)} %get-tuple-element.24.own_coef_ref, bf16[768,512]{1,0:T(8,128)(2,1)S(1)} %get-tuple-element.25.hot_ref, ...), custom_call_target="tpu_custom_call" | custom-call | tf_op jit(solution)/shard_map/predict/pallas_call | solution.py:351
  9.8 14.6 %all_to_all.10.parts_ref = f32[4,176,128]{2,1,0:T(8,128)S(1)} all-to-all(f32[4,176,128]{2,1,0:T(8,128)S(1)} %predict.1), channel_id=1, replica_groups={{0,1,2,3},{4,5,6,7},{8,9,10,11},{12,13,14,15},{18,19,20,21},{22,23,24,2..., dimensions={0} | all-to-all | bytes 720896 | tf_op jit(solution)/shard_map/all_to_all | solution.py:51
  24.4 0.3 gather.1
  24.7 10.1 %collective-permute-start.2 = (f32[192,128]{1,0:T(8,128)S(1)}, f32[192,128]{1,0:T(8,128)S(1)}, u32[]{:S(2)}, u32[]{:S(2)}) collective-permute-start(f32[192,128]{1,0:T(8,128)S(1)} %get-tuple-element.29), channel_id=1, source_target_pairs={{0,4},{4,0},{1,5},{5,1},{2,6},{6,2},{3,7},{7,3},{8,12},{12,8},{9,1... | collective-permute-start | bytes 294920 | tf_op jit(solution)/shard_map/ppermute | solution.py:371
  34.8 7.2 %collective-permute-done.2.received_ref = f32[192,128]{1,0:T(8,128)S(1)} collective-permute-done((f32[192,128]{1,0:T(8,128)S(1)}, f32[192,128]{1,0:T(8,128)S(1)}, u32[]{:S(2)}, u32[]{:S(2)}) %collective-permute-start.2) | collective-permute-done | bytes 98336 | tf_op jit(solution)/shard_map/ppermute | solution.py:371
  42.0 6.3 %collective-permute-start.3 = (f32[160,128]{1,0:T(8,128)S(1)}, f32[160,128]{1,0:T(8,128)S(1)}, u32[]{:S(2)}, u32[]{:S(2)}) collective-permute-start(f32[160,128]{1,0:T(8,128)S(1)} %get-tuple-element.31), channel_id=1, source_target_pairs={{0,12},{12,0},{1,13},{13,1},{2,14},{14,2},{3,15},{15,3},{8,4},{4,8... | collective-permute-start | bytes 245768 | tf_op jit(solution)/shard_map/ppermute | solution.py:380
  48.3 5.2 %collective-permute-done.3.received_ref = f32[160,128]{1,0:T(8,128)S(1)} collective-permute-done((f32[160,128]{1,0:T(8,128)S(1)}, f32[160,128]{1,0:T(8,128)S(1)}, u32[]{:S(2)}, u32[]{:S(2)}) %collective-permute-start.3) | collective-permute-done | bytes 81952 | tf_op jit(solution)/shard_map/ppermute | solution.py:380
  53.5 2.5 %collective-permute-start.4 = (f32[128,128]{1,0:T(8,128)S(1)}, f32[128,128]{1,0:T(8,128)S(1)}, u32[]{:S(2)}, u32[]{:S(2)}) collective-permute-start(f32[128,128]{1,0:T(8,128)S(1)} %get-tuple-element.34.own_ref), channel_id=1, source_target_pairs={{0,2},{1,3},{2,0},{3,1},{4,6},{5,7},{6,4},{7,5},{8,10},{9,11},{10,... | collective-permute-start | bytes 196616 | tf_op jit(solution)/shard_map/ppermute | solution.py:389
  56.0 4.6 %collective-permute-done.4.across_ref = f32[128,128]{1,0:T(8,128)S(1)} collective-permute-done((f32[128,128]{1,0:T(8,128)S(1)}, f32[128,128]{1,0:T(8,128)S(1)}, u32[]{:S(2)}, u32[]{:S(2)}) %collective-permute-start.4) | collective-permute-done | bytes 65568 | tf_op jit(solution)/shard_map/ppermute | solution.py:389
  60.6 4.2 %collective-permute-start.5 = (f32[256,128]{1,0:T(8,128)S(1)}, f32[256,128]{1,0:T(8,128)S(1)}, u32[]{:S(2)}, u32[]{:S(2)}) collective-permute-start(f32[256,128]{1,0:T(8,128)S(1)} %join.1.residual_ref), channel_id=1, source_target_pairs={{0,1},{1,0},{2,3},{3,2},{4,5},{5,4},{6,7},{7,6},{8,9},{9,8},{10,11... | collective-permute-start | bytes 393224 | tf_op jit(solution)/shard_map/ppermute | solution.py:398
  64.8 0.7 half.1.half_ref
  65.5 2.5 %collective-permute-done.5.residual_ref = f32[256,128]{1,0:T(8,128)S(1)} collective-permute-done((f32[256,128]{1,0:T(8,128)S(1)}, f32[256,128]{1,0:T(8,128)S(1)}, u32[]{:S(2)}, u32[]{:S(2)}) %collective-permute-start.5) | collective-permute-done | bytes 131104 | tf_op jit(solution)/shard_map/ppermute | solution.py:398
  68.0 1.3 %rest.1 = (f32[32,2,128]{2,1,0:T(2,128)}, f32[512,128]{1,0:T(8,128)S(1)}) custom-call(bf16[16,512,128]{2,1,0:T(8,128)(2,1)S(1)} %get-tuple-element.23.design_ref, f32[256,128]{1,0:T(8,128)S(1)} %collective-permute-done.5.residual_ref, f32[2,128,128]{2,1,0:T(8,128)S(1)} %half.1.half_ref), custom_call_target="tpu_custom_call" | custom-call | tf_op jit(solution)/shard_map/rest/pallas_call | solution.py:408
  69.3 5.7 %all-to-all-start.1 = ((f32[32,2,128]{2,1,0:T(2,128)}), f32[32,2,128]{2,1,0:T(2,128)S(1)}, u32[]{:S(2)}, u32[]{:S(2)}) async-start(f32[32,2,128]{2,1,0:T(2,128)} %get-tuple-element.35), calls=%async_computation.1 | async-start | bytes 65536 | tf_op jit(solution)/shard_map/all_to_all | solution.py:51
  75.0 0.3 group.1
  75.4 2.1 %collective-permute-start.6 = (f32[16,256]{1,0:T(8,128)S(1)}, f32[16,256]{1,0:T(8,128)S(1)}, u32[]{:S(2)}, u32[]{:S(2)}) collective-permute-start(f32[16,256]{1,0:T(8,128)S(1)} %get-tuple-element.40), channel_id=1, source_target_pairs={{0,16},{32,48},{64,80},{96,112},{128,144},{160,176},{192,208},{224... | collective-permute-start | bytes 49160 | tf_op jit(solution)/shard_map/ppermute | solution.py:20
  77.4 4.8 %collective-permute-start.7 = (f32[16,256]{1,0:T(8,128)S(1)}, f32[16,256]{1,0:T(8,128)S(1)}, u32[]{:S(2)}, u32[]{:S(2)}) collective-permute-start(f32[16,256]{1,0:T(8,128)S(1)} %get-tuple-element.41), channel_id=1, source_target_pairs={{16,32},{48,64},{80,96},{112,128},{144,160},{176,192},{208,224},{2... | collective-permute-start | bytes 49160 | tf_op jit(solution)/shard_map/ppermute | solution.py:20
  82.3 0.0 collective-permute-done.6.even_ref
  82.3 2.3 %collective-permute-done.7.odd_ref = f32[16,256]{1,0:T(8,128)S(1)} collective-permute-done((f32[16,256]{1,0:T(8,128)S(1)}, f32[16,256]{1,0:T(8,128)S(1)}, u32[]{:S(2)}, u32[]{:S(2)}) %collective-permute-start.7) | collective-permute-done | bytes 16416 | tf_op jit(solution)/shard_map/ppermute | solution.py:20
  84.6 0.0 all-to-all-done.1.fixed_all_ref
  84.6 0.6 finish.1
  (3 shorter events, 0.0 us)
Async XLA Ops:
  0.6 8.0 %collective-permute-start.1 = (f32[16,256]{1,0:T(8,128)}, f32[16,256]{1,0:T(8,128)S(1)}, u32[]{:S(2)}, u32[]{:S(2)}) collective-permute-start(f32[16,256]{1,0:T(8,128)} %slopes_hbm.1), channel_id=1, source_target_pairs={{16,32},{48,64},{80,96},{112,128},{144,160},{176,192},{208,224},{2... | collective-permute-start | bytes 49160 | tf_op jit(solution)/shard_map/ppermute | solution.py:20
  4.9 3.7 %collective-permute-start = (f32[16,256]{1,0:T(8,128)}, f32[16,256]{1,0:T(8,128)S(1)}, u32[]{:S(2)}, u32[]{:S(2)}) collective-permute-start(f32[16,256]{1,0:T(8,128)} %slopes_hbm.1), channel_id=1, source_target_pairs={{0,16},{32,48},{64,80},{96,112},{128,144},{160,176},{192,208},{224... | collective-permute-start | bytes 49160 | tf_op jit(solution)/shard_map/ppermute | solution.py:20
  24.7 17.3 %collective-permute-start.2 = (f32[192,128]{1,0:T(8,128)S(1)}, f32[192,128]{1,0:T(8,128)S(1)}, u32[]{:S(2)}, u32[]{:S(2)}) collective-permute-start(f32[192,128]{1,0:T(8,128)S(1)} %get-tuple-element.29), channel_id=1, source_target_pairs={{0,4},{4,0},{1,5},{5,1},{2,6},{6,2},{3,7},{7,3},{8,12},{12,8},{9,1... | collective-permute-start | bytes 294920 | tf_op jit(solution)/shard_map/ppermute | solution.py:371
  42.0 11.5 %collective-permute-start.3 = (f32[160,128]{1,0:T(8,128)S(1)}, f32[160,128]{1,0:T(8,128)S(1)}, u32[]{:S(2)}, u32[]{:S(2)}) collective-permute-start(f32[160,128]{1,0:T(8,128)S(1)} %get-tuple-element.31), channel_id=1, source_target_pairs={{0,12},{12,0},{1,13},{13,1},{2,14},{14,2},{3,15},{15,3},{8,4},{4,8... | collective-permute-start | bytes 245768 | tf_op jit(solution)/shard_map/ppermute | solution.py:380
  53.5 7.1 %collective-permute-start.4 = (f32[128,128]{1,0:T(8,128)S(1)}, f32[128,128]{1,0:T(8,128)S(1)}, u32[]{:S(2)}, u32[]{:S(2)}) collective-permute-start(f32[128,128]{1,0:T(8,128)S(1)} %get-tuple-element.34.own_ref), channel_id=1, source_target_pairs={{0,2},{1,3},{2,0},{3,1},{4,6},{5,7},{6,4},{7,5},{8,10},{9,11},{10,... | collective-permute-start | bytes 196616 | tf_op jit(solution)/shard_map/ppermute | solution.py:389
  60.6 7.4 %collective-permute-start.5 = (f32[256,128]{1,0:T(8,128)S(1)}, f32[256,128]{1,0:T(8,128)S(1)}, u32[]{:S(2)}, u32[]{:S(2)}) collective-permute-start(f32[256,128]{1,0:T(8,128)S(1)} %join.1.residual_ref), channel_id=1, source_target_pairs={{0,1},{1,0},{2,3},{3,2},{4,5},{5,4},{6,7},{7,6},{8,9},{9,8},{10,11... | collective-permute-start | bytes 393224 | tf_op jit(solution)/shard_map/ppermute | solution.py:398
  69.3 15.3 %all-to-all-start.1 = ((f32[32,2,128]{2,1,0:T(2,128)}), f32[32,2,128]{2,1,0:T(2,128)S(1)}, u32[]{:S(2)}, u32[]{:S(2)}) async-start(f32[32,2,128]{2,1,0:T(2,128)} %get-tuple-element.35), calls=%async_computation.1 | async-start | bytes 65536 | tf_op jit(solution)/shard_map/all_to_all | solution.py:51
  75.4 6.9 %collective-permute-start.6 = (f32[16,256]{1,0:T(8,128)S(1)}, f32[16,256]{1,0:T(8,128)S(1)}, u32[]{:S(2)}, u32[]{:S(2)}) collective-permute-start(f32[16,256]{1,0:T(8,128)S(1)} %get-tuple-element.40), channel_id=1, source_target_pairs={{0,16},{32,48},{64,80},{96,112},{128,144},{160,176},{192,208},{224... | collective-permute-start | bytes 49160 | tf_op jit(solution)/shard_map/ppermute | solution.py:20
  77.4 7.2 %collective-permute-start.7 = (f32[16,256]{1,0:T(8,128)S(1)}, f32[16,256]{1,0:T(8,128)S(1)}, u32[]{:S(2)}, u32[]{:S(2)}) collective-permute-start(f32[16,256]{1,0:T(8,128)S(1)} %get-tuple-element.41), channel_id=1, source_target_pairs={{16,32},{48,64},{80,96},{112,128},{144,160},{176,192},{208,224},{2... | collective-permute-start | bytes 49160 | tf_op jit(solution)/shard_map/ppermute | solution.py:20

commit v12 on v10

--- a/solution.py
+++ b/solution.py
@@ -129,7 +129,9 @@
             for at in range(0, precision.shape[1], LANES)
         ]
         prior_ref[peer, : slope_rows.shape[0], :] = slope_rows
-        prior_ref[peer, slope_rows.shape[0] :, :] = kept[0] + pltpu.roll(kept[1], size, 1)
+        both = kept[0] + pltpu.roll(kept[1], size, 1)
+        packed = both[: size // 2] + pltpu.roll(both[size // 2 :], 2 * size, 1)
+        prior_ref[peer, slope_rows.shape[0] :, :] = packed
     fill = fill_ref[pl.ds(near, 1), :].astype(f32)
     column = jnp.broadcast_to(fill, (rows, rows)).T
     lane = lax.broadcasted_iota(jnp.int32, (rows, LANES), 1).astype(f32)
@@ -177,16 +179,18 @@
 def gather_kernel(parts_ref, keep_ref, send_ref, prior_ref):
     groups = prior_ref.shape[1]
     halves = groups // LANES
-    size = keep_ref.shape[0] - parts_ref.shape[1]
-    rows = parts_ref.shape[1] - size * (halves + 1)
+    size = 2 * (keep_ref.shape[0] - parts_ref.shape[1]) // (2 * halves - 1)
+    rows = keep_ref.shape[0] - 2 * size * halves
     total = jnp.sum(parts_ref[:, :rows, :], axis=0)
     columns = [
         parts_ref[:, at : at + size, :].reshape(-1, LANES)
-        for at in range(rows, parts_ref.shape[1], size)
+        for at in range(rows, rows + size * halves, size)
     ]
+    packed = [parts_ref[n, rows + size * halves :, :] for n in range(parts_ref.shape[0])]
+    unpacked = [x for y in packed for x in (y, pltpu.roll(y, LANES - 2 * size, 1))]
     prior_ref[...] = lax.dot_general(
-        columns[halves],
-        jnp.concatenate(columns[:halves], axis=1),
+        jnp.concatenate(unpacked, axis=0),
+        jnp.concatenate(columns, axis=1),
         (((0,), (0,)), ((), ())),
         precision=lax.Precision.HIGHEST,
         preferred_element_type=f32,
@@ -284,7 +288,7 @@
             shape(share, LANES),
             shape(share, LANES),
             shape(1, size),
-            shape(NEAR, slope_rows + size, LANES),
+            shape(NEAR, slope_rows + size // 2, LANES),
             shape(size, blocks),
             shape(LANES, size * LANES, dtype=bf16),
             shape(*design.shape, dtype=bf16),
@@ -319,7 +323,7 @@
 
     partial = pl.pallas_call(
         predict_kernel,
-        out_shape=shape(NEAR, share + slope_rows + size, LANES),
+        out_shape=shape(NEAR, share + slope_rows + size // 2, LANES),
         in_specs=[VMEM] * 7,
         out_specs=VMEM,
         scratch_shapes=[pltpu.VMEM((blocks, LANES), bf16)],

time: 85.2 us -> 85.1 us (level)
  starting transfers between devices: 36.4 us -> 38 us
  blocking collectives: 26 us -> 25 us
  waiting for transfers between devices: 14.7 us -> 13.8 us
    all_to_all x1, starting transfers between devices: 6.89 us -> 8.23 us  [exchange(): lax.all_to_all(parts, axis, 0, 0, tiled=True, axis_index_groups=groups)]
    all_to_all x2, blocking collectives: 26 us -> 25 us  [exchange(): lax.all_to_all(parts, axis, 0, 0, tiled=True, axis_index_groups=groups)]
    ppermute x1, starting transfers between devices: 6.29 us -> 7.2 us  [body(): received = lax.ppermute(sent, ('rows', 'cov'), second_pairs)]
where the time goes in v12:
time: 85.1 us; the launch traced here: 83.9 us
  starting transfers between devices  38 us (45%)
  blocking collectives  25 us (29%)
  waiting for transfers between devices  13.8 us (16%)
  Pallas kernels  6.33 us (7%)
    all_to_all x2, blocking collectives, exchange(): lax.all_to_all(parts, axis, 0, 0, tiled=True, axis_index_groups=groups)  25 us
    ppermute x4, starting transfers between devices, swap(): return lax.ppermute(shard, axis, pairs + [(j, i) for i, j in pairs])  13.1 us
    ppermute x1, starting transfers between devices, body(): received = lax.ppermute(sent, ('rows', 'cov'), first_pairs)  9.46 us
    all_to_all x1, starting transfers between devices, exchange(): lax.all_to_all(parts, axis, 0, 0, tiled=True, axis_index_groups=groups)  8.23 us
    ppermute x1, starting transfers between devices, body(): received = lax.ppermute(sent, ('rows', 'cov'), second_pairs)  7.2 us
    ppermute x1, waiting for transfers between devices, body(): received = lax.ppermute(sent, ('rows', 'cov'), first_pairs)  6.87 us
    ppermute x1, waiting for transfers between devices, body(): received = lax.ppermute(sent, ('rows', 'cov'), second_pairs)  4.62 us
    ppermute x4, waiting for transfers between devices, swap(): return lax.ppermute(shard, axis, pairs + [(j, i) for i, j in pairs])  2.33 us
  transfers between devices with their start and end apart: 7, of which 3 were waited for; matrix products, arithmetic and copies ran while one was open for 0% of the time, Pallas kernels for 2%

profile of v12, /device:TPU:24, one launch (start us, length us, event | category | flops | bytes accessed | tf_op | source)
XLA Modules:
  0.0 83.9 jit_solution(2686858539538353124)
XLA Ops:
  0.6 4.3 %collective-permute-start.1 = (f32[16,256]{1,0:T(8,128)}, f32[16,256]{1,0:T(8,128)S(1)}, u32[]{:S(2)}, u32[]{:S(2)}) collective-permute-start(f32[16,256]{1,0:T(8,128)} %slopes_hbm.1), channel_id=1, source_target_pairs={{16,32},{48,64},{80,96},{112,128},{144,160},{176,192},{208,224},{2... | collective-permute-start | bytes 49160 | tf_op jit(solution)/shard_map/ppermute | solution.py:20
  4.9 1.9 %collective-permute-start = (f32[16,256]{1,0:T(8,128)}, f32[16,256]{1,0:T(8,128)S(1)}, u32[]{:S(2)}, u32[]{:S(2)}) collective-permute-start(f32[16,256]{1,0:T(8,128)} %slopes_hbm.1), channel_id=1, source_target_pairs={{0,16},{32,48},{64,80},{96,112},{128,144},{160,176},{192,208},{224... | collective-permute-start | bytes 49160 | tf_op jit(solution)/shard_map/ppermute | solution.py:20
  6.9 1.7 %select.1 = (bf16[768,512]{1,0:T(8,128)(2,1)S(1)}, f32[128,128]{1,0:T(8,128)S(1)}, f32[128,128]{1,0:T(8,128)S(1)}, f32[1,16]{1,0:T(1,128)S(1)}, f32[4,40,128]{2,...) custom-call(s32[1,512]{1,0:T(1,128)} %bitcast.4, ...), custom_call_target="tpu_custom_call" | custom-call | flops 10000000 | bytes 5000000 | tf_op jit(solution)/shard_map/select/pallas_call | solution.py:284
  8.6 0.0 collective-permute-done.1.odd_ref
  8.6 0.0 collective-permute-done.even_ref
  8.6 1.2 %predict.1 = f32[4,168,128]{2,1,0:T(8,128)S(1)} custom-call(f32[16,256]{1,0:T(8,128)S(1)} %collective-permute-done.even_ref, f32[16,256]{1,0:T(8,128)S(1)} %collective-permute-done.1.odd_ref, f32[16,512]{1,0:T(8,128)S(1)} %get-tuple-element.24.own_coef_ref, bf16[768,512]{1,0:T(8,128)(2,1)S(1)} %get-tuple-element.25.hot_ref, ...), custom_call_target="tpu_custom_call" | custom-call | tf_op jit(solution)/shard_map/predict/pallas_call | solution.py:324
  9.8 14.5 %all_to_all.15.parts_ref = f32[4,168,128]{2,1,0:T(8,128)S(1)} all-to-all(f32[4,168,128]{2,1,0:T(8,128)S(1)} %predict.1), channel_id=1, replica_groups={{0,1,2,3},{4,5,6,7},{8,9,10,11},{12,13,14,15},{18,19,20,21},{22,23,24,2..., dimensions={0} | all-to-all | bytes 688128 | tf_op jit(solution)/shard_map/all_to_all | solution.py:49
  24.3 0.4 gather.1
  24.7 9.5 %collective-permute-start.2 = (f32[192,128]{1,0:T(8,128)S(1)}, f32[192,128]{1,0:T(8,128)S(1)}, u32[]{:S(2)}, u32[]{:S(2)}) collective-permute-start(f32[192,128]{1,0:T(8,128)S(1)} %get-tuple-element.29), channel_id=1, source_target_pairs={{0,4},{4,0},{1,5},{5,1},{2,6},{6,2},{3,7},{7,3},{8,12},{12,8},{9,1... | collective-permute-start | bytes 294920 | tf_op jit(solution)/shard_map/ppermute | solution.py:344
  34.1 6.9 %collective-permute-done.2.received_ref = f32[192,128]{1,0:T(8,128)S(1)} collective-permute-done((f32[192,128]{1,0:T(8,128)S(1)}, f32[192,128]{1,0:T(8,128)S(1)}, u32[]{:S(2)}, u32[]{:S(2)}) %collective-permute-start.2) | collective-permute-done | bytes 98336 | tf_op jit(solution)/shard_map/ppermute | solution.py:344
  41.0 7.2 %collective-permute-start.3 = (f32[160,128]{1,0:T(8,128)S(1)}, f32[160,128]{1,0:T(8,128)S(1)}, u32[]{:S(2)}, u32[]{:S(2)}) collective-permute-start(f32[160,128]{1,0:T(8,128)S(1)} %get-tuple-element.31), channel_id=1, source_target_pairs={{0,12},{12,0},{1,13},{13,1},{2,14},{14,2},{3,15},{15,3},{8,4},{4,8... | collective-permute-start | bytes 245768 | tf_op jit(solution)/shard_map/ppermute | solution.py:353
  48.2 4.6 %collective-permute-done.3.received_ref = f32[160,128]{1,0:T(8,128)S(1)} collective-permute-done((f32[160,128]{1,0:T(8,128)S(1)}, f32[160,128]{1,0:T(8,128)S(1)}, u32[]{:S(2)}, u32[]{:S(2)}) %collective-permute-start.3) | collective-permute-done | bytes 81952 | tf_op jit(solution)/shard_map/ppermute | solution.py:353
  52.9 10.5 %all_to_all.16.back_ref = f32[4,128,128]{2,1,0:T(8,128)S(1)} all-to-all(f32[4,128,128]{2,1,0:T(8,128)S(1)} %get-tuple-element.34), channel_id=1, replica_groups={{0,1,2,3},{4,5,6,7},{8,9,10,11},{12,13,14,15},{18,19,20,21},{22,23,24,2..., dimensions={0} | all-to-all | bytes 524288 | tf_op jit(solution)/shard_map/all_to_all | solution.py:49
  63.4 2.0 %gradient.1 = (f32[32,2,128]{2,1,0:T(2,128)}, f32[512,128]{1,0:T(8,128)S(1)}) custom-call(bf16[16,512,128]{2,1,0:T(8,128)(2,1)S(1)} %get-tuple-element.23.design_ref, f32[4,128,128]{2,1,0:T(8,128)S(1)} %all_to_all.16.back_ref), custom_call_target="tpu_custom_call" | custom-call | tf_op jit(solution)/shard_map/gradient/pallas_call | solution.py:364
  65.5 8.2 %all-to-all-start.2 = ((f32[32,2,128]{2,1,0:T(2,128)}), f32[32,2,128]{2,1,0:T(2,128)S(1)}, u32[]{:S(2)}, u32[]{:S(2)}) async-start(f32[32,2,128]{2,1,0:T(2,128)} %get-tuple-element.35), calls=%async_computation.2 | async-start | bytes 65536 | tf_op jit(solution)/shard_map/all_to_all | solution.py:49
  73.7 0.3 group.1
  74.1 2.1 %collective-permute-start.4 = (f32[16,256]{1,0:T(8,128)S(1)}, f32[16,256]{1,0:T(8,128)S(1)}, u32[]{:S(2)}, u32[]{:S(2)}) collective-permute-start(f32[16,256]{1,0:T(8,128)S(1)} %get-tuple-element.40), channel_id=1, source_target_pairs={{0,16},{32,48},{64,80},{96,112},{128,144},{160,176},{192,208},{224... | collective-permute-start | bytes 49160 | tf_op jit(solution)/shard_map/ppermute | solution.py:20
  76.1 4.8 %collective-permute-start.5 = (f32[16,256]{1,0:T(8,128)S(1)}, f32[16,256]{1,0:T(8,128)S(1)}, u32[]{:S(2)}, u32[]{:S(2)}) collective-permute-start(f32[16,256]{1,0:T(8,128)S(1)} %get-tuple-element.41), channel_id=1, source_target_pairs={{16,32},{48,64},{80,96},{112,128},{144,160},{176,192},{208,224},{2... | collective-permute-start | bytes 49160 | tf_op jit(solution)/shard_map/ppermute | solution.py:20
  81.0 0.0 collective-permute-done.4.even_ref
  81.0 2.3 %collective-permute-done.5.odd_ref = f32[16,256]{1,0:T(8,128)S(1)} collective-permute-done((f32[16,256]{1,0:T(8,128)S(1)}, f32[16,256]{1,0:T(8,128)S(1)}, u32[]{:S(2)}, u32[]{:S(2)}) %collective-permute-start.5) | collective-permute-done | bytes 16416 | tf_op jit(solution)/shard_map/ppermute | solution.py:20
  83.3 0.0 all-to-all-done.2.fixed_all_ref
  83.3 0.6 finish.1
  (2 shorter events, 0.0 us)
Async XLA Ops:
  0.6 8.0 %collective-permute-start.1 = (f32[16,256]{1,0:T(8,128)}, f32[16,256]{1,0:T(8,128)S(1)}, u32[]{:S(2)}, u32[]{:S(2)}) collective-permute-start(f32[16,256]{1,0:T(8,128)} %slopes_hbm.1), channel_id=1, source_target_pairs={{16,32},{48,64},{80,96},{112,128},{144,160},{176,192},{208,224},{2... | collective-permute-start | bytes 49160 | tf_op jit(solution)/shard_map/ppermute | solution.py:20
  4.9 3.7 %collective-permute-start = (f32[16,256]{1,0:T(8,128)}, f32[16,256]{1,0:T(8,128)S(1)}, u32[]{:S(2)}, u32[]{:S(2)}) collective-permute-start(f32[16,256]{1,0:T(8,128)} %slopes_hbm.1), channel_id=1, source_target_pairs={{0,16},{32,48},{64,80},{96,112},{128,144},{160,176},{192,208},{224... | collective-permute-start | bytes 49160 | tf_op jit(solution)/shard_map/ppermute | solution.py:20
  24.7 16.3 %collective-permute-start.2 = (f32[192,128]{1,0:T(8,128)S(1)}, f32[192,128]{1,0:T(8,128)S(1)}, u32[]{:S(2)}, u32[]{:S(2)}) collective-permute-start(f32[192,128]{1,0:T(8,128)S(1)} %get-tuple-element.29), channel_id=1, source_target_pairs={{0,4},{4,0},{1,5},{5,1},{2,6},{6,2},{3,7},{7,3},{8,12},{12,8},{9,1... | collective-permute-start | bytes 294920 | tf_op jit(solution)/shard_map/ppermute | solution.py:344
  41.0 11.8 %collective-permute-start.3 = (f32[160,128]{1,0:T(8,128)S(1)}, f32[160,128]{1,0:T(8,128)S(1)}, u32[]{:S(2)}, u32[]{:S(2)}) collective-permute-start(f32[160,128]{1,0:T(8,128)S(1)} %get-tuple-element.31), channel_id=1, source_target_pairs={{0,12},{12,0},{1,13},{13,1},{2,14},{14,2},{3,15},{15,3},{8,4},{4,8... | collective-permute-start | bytes 245768 | tf_op jit(solution)/shard_map/ppermute | solution.py:353
  65.5 17.8 %all-to-all-start.2 = ((f32[32,2,128]{2,1,0:T(2,128)}), f32[32,2,128]{2,1,0:T(2,128)S(1)}, u32[]{:S(2)}, u32[]{:S(2)}) async-start(f32[32,2,128]{2,1,0:T(2,128)} %get-tuple-element.35), calls=%async_computation.2 | async-start | bytes 65536 | tf_op jit(solution)/shard_map/all_to_all | solution.py:49
  74.1 6.9 %collective-permute-start.4 = (f32[16,256]{1,0:T(8,128)S(1)}, f32[16,256]{1,0:T(8,128)S(1)}, u32[]{:S(2)}, u32[]{:S(2)}) collective-permute-start(f32[16,256]{1,0:T(8,128)S(1)} %get-tuple-element.40), channel_id=1, source_target_pairs={{0,16},{32,48},{64,80},{96,112},{128,144},{160,176},{192,208},{224... | collective-permute-start | bytes 49160 | tf_op jit(solution)/shard_map/ppermute | solution.py:20
  76.1 7.2 %collective-permute-start.5 = (f32[16,256]{1,0:T(8,128)S(1)}, f32[16,256]{1,0:T(8,128)S(1)}, u32[]{:S(2)}, u32[]{:S(2)}) collective-permute-start(f32[16,256]{1,0:T(8,128)S(1)} %get-tuple-element.41), channel_id=1, source_target_pairs={{16,32},{48,64},{80,96},{112,128},{144,160},{176,192},{208,224},{2... | collective-permute-start | bytes 49160 | tf_op jit(solution)/shard_map/ppermute | solution.py:20

commit v13 on v12

--- a/solution.py
+++ b/solution.py
@@ -260,10 +260,13 @@
     own_ref[...] = sums[:, groups : 2 * groups] - jnp.concatenate(halves, axis=1)
 
 
-def finish_kernel(fixed_all_ref, fixed_ref, own_ref, even_ref, odd_ref, fixed_out, slope_out):
+def slope_kernel(own_ref, even_ref, odd_ref, out_ref):
+    out_ref[...] = own_ref[...] + even_ref[...] + odd_ref[...]
+
+
+def finish_kernel(fixed_all_ref, fixed_ref, out_ref):
     size = fixed_ref.shape[1]
-    fixed_out[...] = jnp.sum(fixed_all_ref[...], axis=0)[:1, :size] - fixed_ref[...]
-    slope_out[...] = own_ref[...] + even_ref[...] + odd_ref[...]
+    out_ref[...] = jnp.sum(fixed_all_ref[...], axis=0)[:1, :size] - fixed_ref[...]
 
 
 def shape(*dims, dtype=f32):
@@ -383,14 +386,23 @@
     given_even = swap(to_even, "rows", 0)
     given_odd = swap(to_odd, "rows", 1)
 
-    fixed_grad, slope_grad = pl.pallas_call(
+    slope_grad = pl.pallas_call(
+        slope_kernel,
+        out_shape=shape(size, group_count),
+        in_specs=[VMEM] * 3,
+        out_specs=VMEM,
+        compiler_params=ROOM,
+        cost_estimate=cost(10_000, 100_000),
+        name="slope",
+    )(own, given_even, given_odd)
+    fixed_grad = pl.pallas_call(
         finish_kernel,
-        out_shape=(shape(1, size), shape(size, group_count)),
-        in_specs=[VMEM] * 5,
-        out_specs=(VMEM, VMEM),
+        out_shape=shape(1, size),
+        in_specs=[VMEM] * 2,
+        out_specs=VMEM,
         compiler_params=ROOM,
         name="finish",
-    )(fixed_all, fixed_row, own, given_even, given_odd)
+    )(fixed_all, fixed_row)
     return (fixed_grad.reshape(size), slope_grad)
 
 

time: 85.1 us -> 85.6 us (level)
  transfers between devices with their start and end apart: 7 -> 7, of which waited for: 3 -> 3; matrix products, arithmetic and copies ran while one was open for 0% -> 0% of each run, Pallas kernels for 2% -> 3%
where the time goes in v13:
time: 85.6 us; the launch traced here: 84.5 us
  starting transfers between devices  38 us (44%)
  blocking collectives  25 us (29%)
  waiting for transfers between devices  13.8 us (16%)
  Pallas kernels  6.87 us (8%)
    all_to_all x2, blocking collectives, exchange(): lax.all_to_all(parts, axis, 0, 0, tiled=True, axis_index_groups=groups)  25 us
    ppermute x4, starting transfers between devices, swap(): return lax.ppermute(shard, axis, pairs + [(j, i) for i, j in pairs])  13.1 us
    ppermute x1, starting transfers between devices, body(): received = lax.ppermute(sent, ('rows', 'cov'), first_pairs)  9.46 us
    all_to_all x1, starting transfers between devices, exchange(): lax.all_to_all(parts, axis, 0, 0, tiled=True, axis_index_groups=groups)  8.23 us
    ppermute x1, starting transfers between devices, body(): received = lax.ppermute(sent, ('rows', 'cov'), second_pairs)  7.2 us
    ppermute x1, waiting for transfers between devices, body(): received = lax.ppermute(sent, ('rows', 'cov'), first_pairs)  6.87 us
    ppermute x1, waiting for transfers between devices, body(): received = lax.ppermute(sent, ('rows', 'cov'), second_pairs)  4.62 us
    ppermute x4, waiting for transfers between devices, swap(): return lax.ppermute(shard, axis, pairs + [(j, i) for i, j in pairs])  2.33 us
  transfers between devices with their start and end apart: 7, of which 3 were waited for; matrix products, arithmetic and copies ran while one was open for 0% of the time, Pallas kernels for 3%

profile of v13, /device:TPU:24, one launch (start us, length us, event | category | flops | bytes accessed | tf_op | source)
XLA Modules:
  0.0 84.5 jit_solution(7534884862557825992)
XLA Ops:
  0.6 4.3 %collective-permute-start.1 = (f32[16,256]{1,0:T(8,128)}, f32[16,256]{1,0:T(8,128)S(1)}, u32[]{:S(2)}, u32[]{:S(2)}) collective-permute-start(f32[16,256]{1,0:T(8,128)} %slopes_hbm.1), channel_id=1, source_target_pairs={{16,32},{48,64},{80,96},{112,128},{144,160},{176,192},{208,224},{2... | collective-permute-start | bytes 49160 | tf_op jit(solution)/shard_map/ppermute | solution.py:20
  4.9 1.9 %collective-permute-start = (f32[16,256]{1,0:T(8,128)}, f32[16,256]{1,0:T(8,128)S(1)}, u32[]{:S(2)}, u32[]{:S(2)}) collective-permute-start(f32[16,256]{1,0:T(8,128)} %slopes_hbm.1), channel_id=1, source_target_pairs={{0,16},{32,48},{64,80},{96,112},{128,144},{160,176},{192,208},{224... | collective-permute-start | bytes 49160 | tf_op jit(solution)/shard_map/ppermute | solution.py:20
  6.9 1.7 %select.1 = (bf16[768,512]{1,0:T(8,128)(2,1)S(1)}, f32[128,128]{1,0:T(8,128)S(1)}, f32[128,128]{1,0:T(8,128)S(1)}, f32[1,16]{1,0:T(1,128)S(1)}, f32[4,40,128]{2,...) custom-call(s32[1,512]{1,0:T(1,128)} %bitcast.4, ...), custom_call_target="tpu_custom_call" | custom-call | flops 10000000 | bytes 5000000 | tf_op jit(solution)/shard_map/select/pallas_call | solution.py:287
  8.6 0.0 collective-permute-done.1.odd_ref
  8.6 0.0 collective-permute-done.even_ref
  8.6 1.2 %predict.1 = f32[4,168,128]{2,1,0:T(8,128)S(1)} custom-call(f32[16,256]{1,0:T(8,128)S(1)} %collective-permute-done.even_ref, f32[16,256]{1,0:T(8,128)S(1)} %collective-permute-done.1.odd_ref, f32[16,512]{1,0:T(8,128)S(1)} %get-tuple-element.22.own_coef_ref, bf16[768,512]{1,0:T(8,128)(2,1)S(1)} %get-tuple-element.23.hot_ref, ...), custom_call_target="tpu_custom_call" | custom-call | tf_op jit(solution)/shard_map/predict/pallas_call | solution.py:327
  9.8 14.5 %all_to_all.15.parts_ref = f32[4,168,128]{2,1,0:T(8,128)S(1)} all-to-all(f32[4,168,128]{2,1,0:T(8,128)S(1)} %predict.1), channel_id=1, replica_groups={{0,1,2,3},{4,5,6,7},{8,9,10,11},{12,13,14,15},{18,19,20,21},{22,23,24,2..., dimensions={0} | all-to-all | bytes 688128 | tf_op jit(solution)/shard_map/all_to_all | solution.py:49
  24.3 0.4 gather.1
  24.7 9.5 %collective-permute-start.2 = (f32[192,128]{1,0:T(8,128)S(1)}, f32[192,128]{1,0:T(8,128)S(1)}, u32[]{:S(2)}, u32[]{:S(2)}) collective-permute-start(f32[192,128]{1,0:T(8,128)S(1)} %get-tuple-element.27), channel_id=1, source_target_pairs={{0,4},{4,0},{1,5},{5,1},{2,6},{6,2},{3,7},{7,3},{8,12},{12,8},{9,1... | collective-permute-start | bytes 294920 | tf_op jit(solution)/shard_map/ppermute | solution.py:347
  34.1 6.9 %collective-permute-done.2.received_ref = f32[192,128]{1,0:T(8,128)S(1)} collective-permute-done((f32[192,128]{1,0:T(8,128)S(1)}, f32[192,128]{1,0:T(8,128)S(1)}, u32[]{:S(2)}, u32[]{:S(2)}) %collective-permute-start.2) | collective-permute-done | bytes 98336 | tf_op jit(solution)/shard_map/ppermute | solution.py:347
  41.0 7.2 %collective-permute-start.3 = (f32[160,128]{1,0:T(8,128)S(1)}, f32[160,128]{1,0:T(8,128)S(1)}, u32[]{:S(2)}, u32[]{:S(2)}) collective-permute-start(f32[160,128]{1,0:T(8,128)S(1)} %get-tuple-element.29), channel_id=1, source_target_pairs={{0,12},{12,0},{1,13},{13,1},{2,14},{14,2},{3,15},{15,3},{8,4},{4,8... | collective-permute-start | bytes 245768 | tf_op jit(solution)/shard_map/ppermute | solution.py:356
  48.2 4.6 %collective-permute-done.3.received_ref = f32[160,128]{1,0:T(8,128)S(1)} collective-permute-done((f32[160,128]{1,0:T(8,128)S(1)}, f32[160,128]{1,0:T(8,128)S(1)}, u32[]{:S(2)}, u32[]{:S(2)}) %collective-permute-start.3) | collective-permute-done | bytes 81952 | tf_op jit(solution)/shard_map/ppermute | solution.py:356
  52.9 10.5 %all_to_all.16.back_ref = f32[4,128,128]{2,1,0:T(8,128)S(1)} all-to-all(f32[4,128,128]{2,1,0:T(8,128)S(1)} %get-tuple-element.32), channel_id=1, replica_groups={{0,1,2,3},{4,5,6,7},{8,9,10,11},{12,13,14,15},{18,19,20,21},{22,23,24,2..., dimensions={0} | all-to-all | bytes 524288 | tf_op jit(solution)/shard_map/all_to_all | solution.py:49
  63.4 2.0 %gradient.1 = (f32[32,2,128]{2,1,0:T(2,128)}, f32[512,128]{1,0:T(8,128)S(1)}) custom-call(bf16[16,512,128]{2,1,0:T(8,128)(2,1)S(1)} %get-tuple-element.21.design_ref, f32[4,128,128]{2,1,0:T(8,128)S(1)} %all_to_all.16.back_ref), custom_call_target="tpu_custom_call" | custom-call | tf_op jit(solution)/shard_map/gradient/pallas_call | solution.py:367
  65.5 8.2 %all-to-all-start.2 = ((f32[32,2,128]{2,1,0:T(2,128)}), f32[32,2,128]{2,1,0:T(2,128)S(1)}, u32[]{:S(2)}, u32[]{:S(2)}) async-start(f32[32,2,128]{2,1,0:T(2,128)} %get-tuple-element.33), calls=%async_computation.2 | async-start | bytes 65536 | tf_op jit(solution)/shard_map/all_to_all | solution.py:49
  73.7 0.3 group.1
  74.1 2.1 %collective-permute-start.4 = (f32[16,256]{1,0:T(8,128)S(1)}, f32[16,256]{1,0:T(8,128)S(1)}, u32[]{:S(2)}, u32[]{:S(2)}) collective-permute-start(f32[16,256]{1,0:T(8,128)S(1)} %get-tuple-element.38), channel_id=1, source_target_pairs={{0,16},{32,48},{64,80},{96,112},{128,144},{160,176},{192,208},{224... | collective-permute-start | bytes 49160 | tf_op jit(solution)/shard_map/ppermute | solution.py:20
  76.1 4.8 %collective-permute-start.5 = (f32[16,256]{1,0:T(8,128)S(1)}, f32[16,256]{1,0:T(8,128)S(1)}, u32[]{:S(2)}, u32[]{:S(2)}) collective-permute-start(f32[16,256]{1,0:T(8,128)S(1)} %get-tuple-element.39), channel_id=1, source_target_pairs={{16,32},{48,64},{80,96},{112,128},{144,160},{176,192},{208,224},{2... | collective-permute-start | bytes 49160 | tf_op jit(solution)/shard_map/ppermute | solution.py:20
  81.0 0.0 collective-permute-done.4.even_ref
  81.0 2.3 %collective-permute-done.5.odd_ref = f32[16,256]{1,0:T(8,128)S(1)} collective-permute-done((f32[16,256]{1,0:T(8,128)S(1)}, f32[16,256]{1,0:T(8,128)S(1)}, u32[]{:S(2)}, u32[]{:S(2)}) %collective-permute-start.5) | collective-permute-done | bytes 16416 | tf_op jit(solution)/shard_map/ppermute | solution.py:20
  83.3 0.6 slope.1
  83.9 0.0 all-to-all-done.2.fixed_all_ref
  83.9 0.5 finish.1
  (2 shorter events, 0.0 us)
Async XLA Ops:
  0.6 8.0 %collective-permute-start.1 = (f32[16,256]{1,0:T(8,128)}, f32[16,256]{1,0:T(8,128)S(1)}, u32[]{:S(2)}, u32[]{:S(2)}) collective-permute-start(f32[16,256]{1,0:T(8,128)} %slopes_hbm.1), channel_id=1, source_target_pairs={{16,32},{48,64},{80,96},{112,128},{144,160},{176,192},{208,224},{2... | collective-permute-start | bytes 49160 | tf_op jit(solution)/shard_map/ppermute | solution.py:20
  4.9 3.7 %collective-permute-start = (f32[16,256]{1,0:T(8,128)}, f32[16,256]{1,0:T(8,128)S(1)}, u32[]{:S(2)}, u32[]{:S(2)}) collective-permute-start(f32[16,256]{1,0:T(8,128)} %slopes_hbm.1), channel_id=1, source_target_pairs={{0,16},{32,48},{64,80},{96,112},{128,144},{160,176},{192,208},{224... | collective-permute-start | bytes 49160 | tf_op jit(solution)/shard_map/ppermute | solution.py:20
  24.7 16.3 %collective-permute-start.2 = (f32[192,128]{1,0:T(8,128)S(1)}, f32[192,128]{1,0:T(8,128)S(1)}, u32[]{:S(2)}, u32[]{:S(2)}) collective-permute-start(f32[192,128]{1,0:T(8,128)S(1)} %get-tuple-element.27), channel_id=1, source_target_pairs={{0,4},{4,0},{1,5},{5,1},{2,6},{6,2},{3,7},{7,3},{8,12},{12,8},{9,1... | collective-permute-start | bytes 294920 | tf_op jit(solution)/shard_map/ppermute | solution.py:347
  41.0 11.8 %collective-permute-start.3 = (f32[160,128]{1,0:T(8,128)S(1)}, f32[160,128]{1,0:T(8,128)S(1)}, u32[]{:S(2)}, u32[]{:S(2)}) collective-permute-start(f32[160,128]{1,0:T(8,128)S(1)} %get-tuple-element.29), channel_id=1, source_target_pairs={{0,12},{12,0},{1,13},{13,1},{2,14},{14,2},{3,15},{15,3},{8,4},{4,8... | collective-permute-start | bytes 245768 | tf_op jit(solution)/shard_map/ppermute | solution.py:356
  65.5 18.4 %all-to-all-start.2 = ((f32[32,2,128]{2,1,0:T(2,128)}), f32[32,2,128]{2,1,0:T(2,128)S(1)}, u32[]{:S(2)}, u32[]{:S(2)}) async-start(f32[32,2,128]{2,1,0:T(2,128)} %get-tuple-element.33), calls=%async_computation.2 | async-start | bytes 65536 | tf_op jit(solution)/shard_map/all_to_all | solution.py:49
  74.1 6.9 %collective-permute-start.4 = (f32[16,256]{1,0:T(8,128)S(1)}, f32[16,256]{1,0:T(8,128)S(1)}, u32[]{:S(2)}, u32[]{:S(2)}) collective-permute-start(f32[16,256]{1,0:T(8,128)S(1)} %get-tuple-element.38), channel_id=1, source_target_pairs={{0,16},{32,48},{64,80},{96,112},{128,144},{160,176},{192,208},{224... | collective-permute-start | bytes 49160 | tf_op jit(solution)/shard_map/ppermute | solution.py:20
  76.1 7.2 %collective-permute-start.5 = (f32[16,256]{1,0:T(8,128)S(1)}, f32[16,256]{1,0:T(8,128)S(1)}, u32[]{:S(2)}, u32[]{:S(2)}) collective-permute-start(f32[16,256]{1,0:T(8,128)S(1)} %get-tuple-element.39), channel_id=1, source_target_pairs={{16,32},{48,64},{80,96},{112,128},{144,160},{176,192},{208,224},{2... | collective-permute-start | bytes 49160 | tf_op jit(solution)/shard_map/ppermute | solution.py:20

commit v14 on v12

--- a/solution.py
+++ b/solution.py
@@ -98,7 +98,7 @@
         )
         for i in range(4)
     ]
-    for copy in copies:
+    for copy in copies[6:] + copies[:6]:
         copy.start()
     for copy in copies[:2]:
         copy.wait()

time: 85.1 us -> 85.4 us (level)
  transfers between devices with their start and end apart: 7 -> 7, of which waited for: 3 -> 3; matrix products, arithmetic and copies ran while one was open for 0% -> 0% of each run, Pallas kernels for 2% -> 3%
where the time goes in v14:
time: 85.4 us; the launch traced here: 84.2 us
  starting transfers between devices  38 us (44%)
  blocking collectives  25 us (29%)
  waiting for transfers between devices  13.8 us (16%)
  Pallas kernels  6.65 us (8%)
    all_to_all x2, blocking collectives, exchange(): lax.all_to_all(parts, axis, 0, 0, tiled=True, axis_index_groups=groups)  25 us
    ppermute x4, starting transfers between devices, swap(): return lax.ppermute(shard, axis, pairs + [(j, i) for i, j in pairs])  13.1 us
    ppermute x1, starting transfers between devices, body(): received = lax.ppermute(sent, ('rows', 'cov'), first_pairs)  9.47 us
    all_to_all x1, starting transfers between devices, exchange(): lax.all_to_all(parts, axis, 0, 0, tiled=True, axis_index_groups=groups)  8.22 us
    ppermute x1, starting transfers between devices, body(): received = lax.ppermute(sent, ('rows', 'cov'), second_pairs)  7.19 us
    ppermute x1, waiting for transfers between devices, body(): received = lax.ppermute(sent, ('rows', 'cov'), first_pairs)  6.88 us
    ppermute x1, waiting for transfers between devices, body(): received = lax.ppermute(sent, ('rows', 'cov'), second_pairs)  4.63 us
    ppermute x4, waiting for transfers between devices, swap(): return lax.ppermute(shard, axis, pairs + [(j, i) for i, j in pairs])  2.33 us
  transfers between devices with their start and end apart: 7, of which 3 were waited for; matrix products, arithmetic and copies ran while one was open for 0% of the time, Pallas kernels for 3%

profile of v14, /device:TPU:24, one launch (start us, length us, event | category | flops | bytes accessed | tf_op | source)
XLA Modules:
  0.0 84.2 jit_solution(2578279328874835748)
XLA Ops:
  0.6 4.3 %collective-permute-start.1 = (f32[16,256]{1,0:T(8,128)}, f32[16,256]{1,0:T(8,128)S(1)}, u32[]{:S(2)}, u32[]{:S(2)}) collective-permute-start(f32[16,256]{1,0:T(8,128)} %slopes_hbm.1), channel_id=1, source_target_pairs={{16,32},{48,64},{80,96},{112,128},{144,160},{176,192},{208,224},{2... | collective-permute-start | bytes 49160 | tf_op jit(solution)/shard_map/ppermute | solution.py:20
  4.9 1.9 %collective-permute-start = (f32[16,256]{1,0:T(8,128)}, f32[16,256]{1,0:T(8,128)S(1)}, u32[]{:S(2)}, u32[]{:S(2)}) collective-permute-start(f32[16,256]{1,0:T(8,128)} %slopes_hbm.1), channel_id=1, source_target_pairs={{0,16},{32,48},{64,80},{96,112},{128,144},{160,176},{192,208},{224... | collective-permute-start | bytes 49160 | tf_op jit(solution)/shard_map/ppermute | solution.py:20
  6.9 2.1 %select.1 = (bf16[768,512]{1,0:T(8,128)(2,1)S(1)}, f32[128,128]{1,0:T(8,128)S(1)}, f32[128,128]{1,0:T(8,128)S(1)}, f32[1,16]{1,0:T(1,128)S(1)}, f32[4,40,128]{2,...) custom-call(s32[1,512]{1,0:T(1,128)} %bitcast.4, ...), custom_call_target="tpu_custom_call" | custom-call | flops 10000000 | bytes 5000000 | tf_op jit(solution)/shard_map/select/pallas_call | solution.py:284
  8.9 0.0 collective-permute-done.1.odd_ref
  8.9 0.0 collective-permute-done.even_ref
  8.9 1.2 %predict.1 = f32[4,168,128]{2,1,0:T(8,128)S(1)} custom-call(f32[16,256]{1,0:T(8,128)S(1)} %collective-permute-done.even_ref, f32[16,256]{1,0:T(8,128)S(1)} %collective-permute-done.1.odd_ref, f32[16,512]{1,0:T(8,128)S(1)} %get-tuple-element.24.own_coef_ref, bf16[768,512]{1,0:T(8,128)(2,1)S(1)} %get-tuple-element.25.hot_ref, ...), custom_call_target="tpu_custom_call" | custom-call | tf_op jit(solution)/shard_map/predict/pallas_call | solution.py:324
  10.1 14.5 %all_to_all.15.parts_ref = f32[4,168,128]{2,1,0:T(8,128)S(1)} all-to-all(f32[4,168,128]{2,1,0:T(8,128)S(1)} %predict.1), channel_id=1, replica_groups={{0,1,2,3},{4,5,6,7},{8,9,10,11},{12,13,14,15},{18,19,20,21},{22,23,24,2..., dimensions={0} | all-to-all | bytes 688128 | tf_op jit(solution)/shard_map/all_to_all | solution.py:49
  24.6 0.4 gather.1
  25.0 9.5 %collective-permute-start.2 = (f32[192,128]{1,0:T(8,128)S(1)}, f32[192,128]{1,0:T(8,128)S(1)}, u32[]{:S(2)}, u32[]{:S(2)}) collective-permute-start(f32[192,128]{1,0:T(8,128)S(1)} %get-tuple-element.29), channel_id=1, source_target_pairs={{0,4},{4,0},{1,5},{5,1},{2,6},{6,2},{3,7},{7,3},{8,12},{12,8},{9,1... | collective-permute-start | bytes 294920 | tf_op jit(solution)/shard_map/ppermute | solution.py:344
  34.5 6.9 %collective-permute-done.2.received_ref = f32[192,128]{1,0:T(8,128)S(1)} collective-permute-done((f32[192,128]{1,0:T(8,128)S(1)}, f32[192,128]{1,0:T(8,128)S(1)}, u32[]{:S(2)}, u32[]{:S(2)}) %collective-permute-start.2) | collective-permute-done | bytes 98336 | tf_op jit(solution)/shard_map/ppermute | solution.py:344
  41.4 7.2 %collective-permute-start.3 = (f32[160,128]{1,0:T(8,128)S(1)}, f32[160,128]{1,0:T(8,128)S(1)}, u32[]{:S(2)}, u32[]{:S(2)}) collective-permute-start(f32[160,128]{1,0:T(8,128)S(1)} %get-tuple-element.31), channel_id=1, source_target_pairs={{0,12},{12,0},{1,13},{13,1},{2,14},{14,2},{3,15},{15,3},{8,4},{4,8... | collective-permute-start | bytes 245768 | tf_op jit(solution)/shard_map/ppermute | solution.py:353
  48.6 4.6 %collective-permute-done.3.received_ref = f32[160,128]{1,0:T(8,128)S(1)} collective-permute-done((f32[160,128]{1,0:T(8,128)S(1)}, f32[160,128]{1,0:T(8,128)S(1)}, u32[]{:S(2)}, u32[]{:S(2)}) %collective-permute-start.3) | collective-permute-done | bytes 81952 | tf_op jit(solution)/shard_map/ppermute | solution.py:353
  53.2 10.5 %all_to_all.16.back_ref = f32[4,128,128]{2,1,0:T(8,128)S(1)} all-to-all(f32[4,128,128]{2,1,0:T(8,128)S(1)} %get-tuple-element.34), channel_id=1, replica_groups={{0,1,2,3},{4,5,6,7},{8,9,10,11},{12,13,14,15},{18,19,20,21},{22,23,24,2..., dimensions={0} | all-to-all | bytes 524288 | tf_op jit(solution)/shard_map/all_to_all | solution.py:49
  63.8 2.0 %gradient.1 = (f32[32,2,128]{2,1,0:T(2,128)}, f32[512,128]{1,0:T(8,128)S(1)}) custom-call(bf16[16,512,128]{2,1,0:T(8,128)(2,1)S(1)} %get-tuple-element.23.design_ref, f32[4,128,128]{2,1,0:T(8,128)S(1)} %all_to_all.16.back_ref), custom_call_target="tpu_custom_call" | custom-call | tf_op jit(solution)/shard_map/gradient/pallas_call | solution.py:364
  65.8 8.2 %all-to-all-start.2 = ((f32[32,2,128]{2,1,0:T(2,128)}), f32[32,2,128]{2,1,0:T(2,128)S(1)}, u32[]{:S(2)}, u32[]{:S(2)}) async-start(f32[32,2,128]{2,1,0:T(2,128)} %get-tuple-element.35), calls=%async_computation.2 | async-start | bytes 65536 | tf_op jit(solution)/shard_map/all_to_all | solution.py:49
  74.0 0.3 group.1
  74.4 2.1 %collective-permute-start.4 = (f32[16,256]{1,0:T(8,128)S(1)}, f32[16,256]{1,0:T(8,128)S(1)}, u32[]{:S(2)}, u32[]{:S(2)}) collective-permute-start(f32[16,256]{1,0:T(8,128)S(1)} %get-tuple-element.40), channel_id=1, source_target_pairs={{0,16},{32,48},{64,80},{96,112},{128,144},{160,176},{192,208},{224... | collective-permute-start | bytes 49160 | tf_op jit(solution)/shard_map/ppermute | solution.py:20
  76.5 4.8 %collective-permute-start.5 = (f32[16,256]{1,0:T(8,128)S(1)}, f32[16,256]{1,0:T(8,128)S(1)}, u32[]{:S(2)}, u32[]{:S(2)}) collective-permute-start(f32[16,256]{1,0:T(8,128)S(1)} %get-tuple-element.41), channel_id=1, source_target_pairs={{16,32},{48,64},{80,96},{112,128},{144,160},{176,192},{208,224},{2... | collective-permute-start | bytes 49160 | tf_op jit(solution)/shard_map/ppermute | solution.py:20
  81.3 0.0 collective-permute-done.4.even_ref
  81.3 2.3 %collective-permute-done.5.odd_ref = f32[16,256]{1,0:T(8,128)S(1)} collective-permute-done((f32[16,256]{1,0:T(8,128)S(1)}, f32[16,256]{1,0:T(8,128)S(1)}, u32[]{:S(2)}, u32[]{:S(2)}) %collective-permute-start.5) | collective-permute-done | bytes 16416 | tf_op jit(solution)/shard_map/ppermute | solution.py:20
  83.6 0.0 all-to-all-done.2.fixed_all_ref
  83.6 0.6 finish.1
  (2 shorter events, 0.0 us)
Async XLA Ops:
  0.6 8.3 %collective-permute-start.1 = (f32[16,256]{1,0:T(8,128)}, f32[16,256]{1,0:T(8,128)S(1)}, u32[]{:S(2)}, u32[]{:S(2)}) collective-permute-start(f32[16,256]{1,0:T(8,128)} %slopes_hbm.1), channel_id=1, source_target_pairs={{16,32},{48,64},{80,96},{112,128},{144,160},{176,192},{208,224},{2... | collective-permute-start | bytes 49160 | tf_op jit(solution)/shard_map/ppermute | solution.py:20
  4.9 4.0 %collective-permute-start = (f32[16,256]{1,0:T(8,128)}, f32[16,256]{1,0:T(8,128)S(1)}, u32[]{:S(2)}, u32[]{:S(2)}) collective-permute-start(f32[16,256]{1,0:T(8,128)} %slopes_hbm.1), channel_id=1, source_target_pairs={{0,16},{32,48},{64,80},{96,112},{128,144},{160,176},{192,208},{224... | collective-permute-start | bytes 49160 | tf_op jit(solution)/shard_map/ppermute | solution.py:20
  25.0 16.4 %collective-permute-start.2 = (f32[192,128]{1,0:T(8,128)S(1)}, f32[192,128]{1,0:T(8,128)S(1)}, u32[]{:S(2)}, u32[]{:S(2)}) collective-permute-start(f32[192,128]{1,0:T(8,128)S(1)} %get-tuple-element.29), channel_id=1, source_target_pairs={{0,4},{4,0},{1,5},{5,1},{2,6},{6,2},{3,7},{7,3},{8,12},{12,8},{9,1... | collective-permute-start | bytes 294920 | tf_op jit(solution)/shard_map/ppermute | solution.py:344
  41.4 11.8 %collective-permute-start.3 = (f32[160,128]{1,0:T(8,128)S(1)}, f32[160,128]{1,0:T(8,128)S(1)}, u32[]{:S(2)}, u32[]{:S(2)}) collective-permute-start(f32[160,128]{1,0:T(8,128)S(1)} %get-tuple-element.31), channel_id=1, source_target_pairs={{0,12},{12,0},{1,13},{13,1},{2,14},{14,2},{3,15},{15,3},{8,4},{4,8... | collective-permute-start | bytes 245768 | tf_op jit(solution)/shard_map/ppermute | solution.py:353
  65.8 17.8 %all-to-all-start.2 = ((f32[32,2,128]{2,1,0:T(2,128)}), f32[32,2,128]{2,1,0:T(2,128)S(1)}, u32[]{:S(2)}, u32[]{:S(2)}) async-start(f32[32,2,128]{2,1,0:T(2,128)} %get-tuple-element.35), calls=%async_computation.2 | async-start | bytes 65536 | tf_op jit(solution)/shard_map/all_to_all | solution.py:49
  74.4 6.9 %collective-permute-start.4 = (f32[16,256]{1,0:T(8,128)S(1)}, f32[16,256]{1,0:T(8,128)S(1)}, u32[]{:S(2)}, u32[]{:S(2)}) collective-permute-start(f32[16,256]{1,0:T(8,128)S(1)} %get-tuple-element.40), channel_id=1, source_target_pairs={{0,16},{32,48},{64,80},{96,112},{128,144},{160,176},{192,208},{224... | collective-permute-start | bytes 49160 | tf_op jit(solution)/shard_map/ppermute | solution.py:20
  76.5 7.2 %collective-permute-start.5 = (f32[16,256]{1,0:T(8,128)S(1)}, f32[16,256]{1,0:T(8,128)S(1)}, u32[]{:S(2)}, u32[]{:S(2)}) collective-permute-start(f32[16,256]{1,0:T(8,128)S(1)} %get-tuple-element.41), channel_id=1, source_target_pairs={{16,32},{48,64},{80,96},{112,128},{144,160},{176,192},{208,224},{2... | collective-permute-start | bytes 49160 | tf_op jit(solution)/shard_map/ppermute | solution.py:20
